TPU v7x, 32 devices: a whole 2x2x4 slice. The times are simulated.
32 devices in a mesh: gx: 4 (over y, x), gy: 4 (over z), gz: 2 (over core).
Axes of the slice: x: 2, y: 2, z: 4, core: 2. Of those that a mesh axis runs over, the one named last changes fastest.
Arguments:
- adjoint: float32 [1024, 5, 512], P(('gx', 'gy', 'gz')), may hold values from -6 to 6
- saved: bfloat16 [3, 1024, 5, 512], P(None, ('gx', 'gy', 'gz')), as said below
- inv_jac: float32 [1024], P(('gx', 'gy', 'gz')), may hold values from 0.5 to 2
- stiffness: bfloat16 [3, 512, 512], replicated, may hold values from -0.25 to 0.25
- send_face: int32 [32, 128], P(('gx', 'gy', 'gz')), may hold values from -1 to 191, as said below
- mortar_table: int32 [32, 5, 64], P(('gx', 'gy', 'gz')), may hold values from 0 to 127, as said below
- conf_faces: int32 [32, 2, 16], P(('gx', 'gy', 'gz')), may hold values from 0 to 190, as said below
Outputs:
- adjoint_out: float32 [1024, 5, 512], P(('gx', 'gy', 'gz'))
Inputs may be any that keep to these rules, and one draw needn't show every extreme that they name: `saved`: density is 1.0 to 1.4 at every node, each momentum component within 0.6 in magnitude, total energy 2 to 3. `send_face`: row d lists, owner-major, for each of the 8 owners of d's group and each of 16 slots, the local face id (6 times element plus face) sent there, or -1 for an empty slot. Live ids of a device are distinct and differ from its conforming faces. The filled slots toward one owner are its first ones, an even number of them. `mortar_table`: row d holds for each of 64 owned mortars: left received slot, right received slot (slot = source position times 16 plus slot), child position of the left side (0 whole face, 1 to 4 quadrant), normal axis (0 to 2), 1 if live else 0. The left and right slots of all mortars name each received slot once; a mortar is live exactly when both its slots are filled, and then its child is drawn from 0 to 4; dead mortars have child 0. In every group some owner receives all 16 slots filled from every source. `conf_faces`: row d holds 16 local face ids of d's lower side and 16 of its upper side along gz, all distinct; face j of the upper side meets face j of the next device's lower side, cyclically along gz.
All inputs are finite; a program needn't handle non-finite values.
Results may differ from a plain program's by a relative error of at most 0.0014.
Values may be sent and summed in bfloat16 or wider, within the bound.
No kernel may reach another device: no remote copies, remote signals or barrier semaphores. Data moves between devices by JAX's collectives and lax.ppermute only.
A program may use at most 64 MiB of HBM per device.

v0:
```python
import functools

import jax
import jax.numpy as jnp
import numpy as np
from jax import lax
from jax.experimental import pallas as pl
from jax.experimental.pallas import tpu as pltpu
from jax.sharding import PartitionSpec as P

ORDER = 7
LINE = ORDER + 1
FACE = LINE * LINE
ELEM = FACE * LINE
PAIRS = 3
TILE = 2 * FACE
WIDTH = PAIRS * TILE

gamma_gas = 1.4
penalty = 1.5
viscosity = 0.5
step_size = 0.2
section_weights = (0.25, 0.25, 0.5)
GM1 = gamma_gas - 1.0
REST = (1.0, 0.0, 0.0, 0.0, 2.5)
F32 = jnp.float32
BF16 = jnp.bfloat16


def lagrange_matrix(points, abscissa):
    out = np.ones((LINE, LINE))
    for target in range(LINE):
        for other in range(LINE):
            if other != target:
                out[:, target] *= (points - abscissa[other]) / (abscissa[target] - abscissa[other])
    return out


def split_low(matrix):
    high = matrix.astype(np.float32).astype(BF16)
    low = (matrix - high.astype(np.float64)).astype(np.float32).astype(BF16)
    return high, low


def projection_tables():
    abscissa = -np.cos(np.pi * np.arange(LINE) / ORDER)
    halves = [lagrange_matrix((abscissa + 2.0 * h - 1.0) * 0.5, abscissa) for h in range(2)]
    children = [np.kron(halves[c // 2], halves[c % 2]) for c in range(4)]
    eye2 = np.eye(2)
    forward = np.concatenate([np.kron(eye2, m.T) for m in children], axis=1)
    backward = np.concatenate([np.kron(eye2, m) for m in children], axis=1)
    fh, fl = split_low(forward)
    bh, bl = split_low(backward)
    return np.concatenate([fh, fl], axis=0), np.concatenate([bh, bh, bl], axis=0)


def restriction_table():
    column = np.arange(6 * FACE)
    face, local = column // FACE, column % FACE
    first, second = local // LINE, local % LINE
    axis, fixed = face // 2, face % 2 * (LINE - 1)
    x = np.where(axis == 0, fixed, first)
    y = np.where(axis == 0, first, np.where(axis == 1, fixed, second))
    z = np.where(axis == 2, fixed, second)
    node = x * FACE + y * LINE + z
    return (np.arange(ELEM)[:, None] == node[None, :]).astype(np.float32).astype(BF16)


def dot(a, b, ca=1, cb=0):
    return lax.dot_general(a, b, (((ca,), (cb,)), ((), ())), preferred_element_type=F32)


def low_lanes(rows):
    return lax.broadcasted_iota(jnp.int32, (rows, TILE), 1) < FACE


def swap(x):
    return pltpu.roll(x, FACE, 1)


def exchange(a, b, low):
    return jnp.where(low, a, swap(b)), jnp.where(low, swap(a), b)


def tiles(x):
    return [x[:, j * TILE : (j + 1) * TILE] for j in range(PAIRS)]


def flux_pull(u, w, picks):
    inv = 1.0 / u[0]
    vel = [u[i] * inv for i in (1, 2, 3)]
    kin = 0.5 * (vel[0] * vel[0] + vel[1] * vel[1] + vel[2] * vel[2])
    enth = gamma_gas * (u[4] * inv) - GM1 * kin
    q = w[1] * vel[0] + w[2] * vel[1] + w[3] * vel[2]
    if picks is None:
        vn, wn = vel[2], w[3]
    else:
        vn = jnp.where(picks[0], vel[0], jnp.where(picks[1], vel[1], vel[2]))
        wn = jnp.where(picks[0], w[1], jnp.where(picks[1], w[2], w[3]))
    r = vn * w[4]
    a = w[0] + q + enth * w[4]
    g = [GM1 * kin * wn - vn * q + (GM1 * kin - enth) * r]
    t = GM1 * (wn + r)
    for i in range(3):
        gi = w[1 + i] * vn - vel[i] * t
        if picks is None:
            gi = gi + a if i == 2 else gi
        else:
            gi = gi + jnp.where(picks[i], a, 0.0)
        g.append(gi)
    g.append(GM1 * wn + gamma_gas * r)
    return g


def face_rows_of(ids_row, elements):
    shape = (6 * elements, ids_row.shape[1])
    row = lax.broadcasted_iota(jnp.int32, shape, 0)
    face = row // elements
    ident = 6 * (row - face * elements) + face
    return jnp.where(ident == ids_row, 1.0, 0.0).astype(BF16)


def trace_faces(field_low, table, elements):
    traced = dot(field_low, table)
    low = low_lanes(elements)
    zero = jnp.zeros((elements, TILE), F32)
    rows = [[None] * PAIRS for _ in range(6)]

    def piece(v, k):
        if v >= 5:
            return zero
        return traced[v * elements : (v + 1) * elements, k * TILE : (k + 1) * TILE]

    for j in range(PAIRS):
        for k in range(3):
            rows[2 * k][j], rows[2 * k + 1][j] = exchange(piece(2 * j, k), piece(2 * j + 1, k), low)
    return jnp.concatenate([jnp.concatenate(r, axis=1) for r in rows], axis=0).astype(BF16)


def lift_faces(face_grad, table, elements):
    low = low_lanes(elements)
    rows = [[None] * 3 for _ in range(6)]

    def piece(f, j):
        return face_grad[f * elements : (f + 1) * elements, j * TILE : (j + 1) * TILE]

    for j in range(PAIRS):
        for k in range(3):
            rows[2 * j][k], rows[2 * j + 1][k] = exchange(piece(2 * k, j), piece(2 * k + 1, j), low)
    arranged = jnp.concatenate([jnp.concatenate(r, axis=1) for r in rows[:5]], axis=0).astype(BF16)
    return dot(arranged, table, 1, 1)


def column_of(row):
    n = row.shape[1]
    same = lax.broadcasted_iota(jnp.int32, (n, n), 0) == lax.broadcasted_iota(jnp.int32, (n, n), 1)
    return jnp.sum(jnp.where(same, jnp.broadcast_to(row, (n, n)), jnp.zeros((), row.dtype)), axis=1, keepdims=True)


def gather_outputs(faces, send_ref, conf_ref, elements):
    out = dot(face_rows_of(send_ref[...], elements), faces, 0, 0).astype(BF16)
    conf = conf_ref[0]
    lower = dot(face_rows_of(conf[0:1], elements), faces, 0, 0).astype(BF16)
    upper = dot(face_rows_of(conf[1:2], elements), faces, 0, 0).astype(BF16)
    return out, lower, upper


def start_kernel(lam_ref, saved_ref, send_ref, conf_ref, table_ref, out_ref, conf_lam_ref, conf_state_ref):
    elements = lam_ref.shape[1]
    sections = saved_ref.shape[0]
    table = table_ref[...]
    owners, rows = out_ref.shape[0], out_ref.shape[1]
    cap = rows // (sections + 1)

    def put(k, value):
        out_ref[:, k * cap : (k + 1) * cap, :] = value.reshape(owners, cap, WIDTH)

    lam_low = lam_ref[...].astype(BF16).reshape(5 * elements, ELEM)
    out, lower, upper = gather_outputs(trace_faces(lam_low, table, elements), send_ref, conf_ref, elements)
    put(0, out)
    conf_lam_ref[0] = lower
    conf_lam_ref[1] = upper
    for s in range(sections):
        state = saved_ref[s].reshape(5 * elements, ELEM)
        out, lower, upper = gather_outputs(trace_faces(state, table, elements), send_ref, conf_ref, elements)
        put(1 + s, out)
        conf_state_ref[s, 0] = lower
        conf_state_ref[s, 1] = upper


def volume_kernel(section, lam_ref, saved_ref, stiff_ref, jac_ref, own_ref, near_ref, state_ref, base_ref, grad_ref, slope_ref, smooth_ref):
    elements = lam_ref.shape[1]
    coef = step_size * section_weights[section]
    lam_low = lam_ref[...].astype(BF16).reshape(5 * elements, ELEM)
    smooth = None
    for d in range(3):
        slopes = dot(lam_low, stiff_ref[d])
        slope_ref[d] = slopes
        part = dot(slopes.astype(BF16), stiff_ref[d], 1, 1)
        smooth = part if smooth is None else smooth + part
    smooth_ref[...] = smooth
    jac = column_of(jac_ref[...]) * coef
    step = 16
    for r in range(0, elements, step):
        scale = jnp.broadcast_to(jac[r : r + step], (step, 128))
        for c in range(0, ELEM, 128):
            u = [saved_ref[section, v, r : r + step, c : c + 128].astype(F32) for v in range(5)]
            inv = 1.0 / u[0]
            vel = [u[i] * inv for i in (1, 2, 3)]
            kin = 0.5 * (vel[0] * vel[0] + vel[1] * vel[1] + vel[2] * vel[2])
            enth = gamma_gas * (u[4] * inv) - GM1 * kin
            trace = run = first = None
            g = [None, None, None, None]
            for d in range(3):
                w = [slope_ref[d, v * elements + r : v * elements + r + step, c : c + 128] for v in range(5)]
                q = w[1] * vel[0] + w[2] * vel[1] + w[3] * vel[2]
                term = vel[d] * q
                first = term if first is None else first + term
                trace = w[1 + d] if trace is None else trace + w[1 + d]
                part = vel[d] * w[4]
                run = part if run is None else run + part
                for i in range(3):
                    gi = w[1 + i] * vel[d]
                    if i == d:
                        gi = gi + (w[0] + q + enth * w[4])
                    g[1 + i] = gi if g[1 + i] is None else g[1 + i] + gi
            t = GM1 * (trace + run)
            pulled = [GM1 * kin * trace - first + (GM1 * kin - enth) * run]
            pulled += [g[1 + i] - vel[i] * t for i in range(3)]
            pulled.append(GM1 * trace + gamma_gas * run)
            for v in range(5):
                rows = slice(v * elements + r, v * elements + r + step)
                vol = pulled[v] - viscosity * smooth_ref[rows, c : c + 128]
                base_ref[v, r : r + step, c : c + 128] = lam_ref[v, r : r + step, c : c + 128] + scale * vol

    faces = own_ref.shape[1]
    low = low_lanes(faces)
    sign = jnp.where(low, -1.0, 1.0)

    def by_variable(ref, index=(), order=(0, 1)):
        lower, upper = (tiles(ref[index + (side,)].astype(F32)) for side in order)
        out = []
        for j in range(PAIRS):
            out += exchange(lower[j], upper[j], low)
        return out[:5]

    own, near, u = by_variable(own_ref), by_variable(near_ref, (), (1, 0)), by_variable(state_ref, (section,))
    w = [sign * (near[v] - own[v]) for v in range(5)]
    g = flux_pull(u, w, None)
    pull = [0.5 * g[v] + (0.5 * penalty) * sign * w[v] for v in range(5)]
    pull.append(jnp.zeros_like(pull[0]))
    for j in range(PAIRS):
        lower, upper = exchange(pull[2 * j], pull[2 * j + 1], low)
        grad_ref[0, :, j * TILE : (j + 1) * TILE] = lower.astype(BF16)
        grad_ref[1, :, j * TILE : (j + 1) * TILE] = upper.astype(BF16)


def mortar_kernel(section, lam_ref, first_ref, map_ref, forward_ref, backward_ref, out_ref):
    owners, cap = out_ref.shape[0], out_ref.shape[1]
    slots = owners * cap
    lam = lam_ref[:, 0:cap, :].reshape(slots, WIDTH)
    state = first_ref[:, (1 + section) * cap : (2 + section) * cap, :].reshape(slots, WIDTH)
    rows = map_ref[0]
    mortars = rows.shape[1]
    slot = lax.broadcasted_iota(jnp.int32, (slots, mortars), 0)
    pick_left = jnp.where(slot == rows[0:1], 1.0, 0.0).astype(BF16)
    pick_right = jnp.where(slot == rows[1:2], 1.0, 0.0).astype(BF16)
    column = [jnp.broadcast_to(column_of(rows[k : k + 1].astype(F32)), (mortars, TILE)) for k in (2, 3, 4)]
    child = [column[0] == float(c) for c in range(5)]
    picks = [column[1] == float(n) for n in range(3)]
    live = column[2]
    alive = live == 1.0
    low = low_lanes(mortars)

    left = tiles(dot(pick_left, lam, 0, 0)) + tiles(dot(pick_left, state, 0, 0))
    right = tiles(dot(pick_right, lam, 0, 0)) + tiles(dot(pick_right, state, 0, 0))

    def choose(raw, spread, j):
        out = raw
        for c in range(4):
            out = jnp.where(child[c + 1], spread[j * mortars : (j + 1) * mortars, c * TILE : (c + 1) * TILE], out)
        return out

    stacked = jnp.concatenate(left, axis=0).astype(BF16)
    spread = dot(jnp.concatenate([stacked, stacked], axis=1), forward_ref[...])
    left = [choose(left[j], spread, j) for j in range(2 * PAIRS)]

    w, u = [], []
    for j in range(PAIRS):
        jump = (right[j] - left[j]) * live
        turned = swap(jump)
        w += [jnp.where(low, jump, turned), jnp.where(low, turned, jump)]
        u += exchange(left[PAIRS + j], right[PAIRS + j], low)
    u = [jnp.where(alive, u[v], REST[v]) for v in range(5)]
    g = flux_pull(u, w[:5], picks)
    side = jnp.where(low, 0.5 * penalty, -0.5 * penalty)
    pull = [0.5 * g[v] + side * w[v] for v in range(5)]
    pull.append(jnp.zeros_like(pull[0]))
    back_left, back_right = [], []
    for j in range(PAIRS):
        a, b = exchange(pull[2 * j], pull[2 * j + 1], low)
        back_left.append(a)
        back_right.append(b)
    stacked = jnp.concatenate(back_left, axis=0)
    high = stacked.astype(BF16)
    rest = (stacked - high.astype(F32)).astype(BF16)
    spread = dot(jnp.concatenate([high, rest, high], axis=1), backward_ref[...])
    back_left = [choose(back_left[j], spread, j) for j in range(PAIRS)]
    grads = dot(pick_left, jnp.concatenate(back_left, axis=1).astype(BF16))
    grads = grads + dot(pick_right, jnp.concatenate(back_right, axis=1).astype(BF16))
    out_ref[...] = grads.astype(BF16).reshape(owners, cap, WIDTH)


def update_of(section, base_ref, back_ref, grad_ref, jac_ref, send_ref, conf_ref, table_ref):
    elements = base_ref.shape[1]
    coef = step_size * section_weights[section]
    slots = send_ref.shape[1]
    conf = conf_ref[0]
    face_grad = dot(face_rows_of(send_ref[...], elements), back_ref[...].reshape(slots, WIDTH))
    face_grad = face_grad + dot(face_rows_of(conf[0:1], elements), grad_ref[0])
    face_grad = face_grad + dot(face_rows_of(conf[1:2], elements), grad_ref[1])
    lifted = lift_faces(face_grad, table_ref[...], elements)
    jac = column_of(jac_ref[...]) * coef
    return [base_ref[v] + jac * lifted[v * elements : (v + 1) * elements] for v in range(5)]


def update_kernel(section, base_ref, back_ref, grad_ref, jac_ref, send_ref, conf_ref, table_ref, lam_ref, out_ref, conf_lam_ref):
    elements = base_ref.shape[1]
    lam = update_of(section, base_ref, back_ref, grad_ref, jac_ref, send_ref, conf_ref, table_ref)
    for v in range(5):
        lam_ref[v] = lam[v]
    lam_low = jnp.concatenate([x.astype(BF16) for x in lam], axis=0)
    out, lower, upper = gather_outputs(trace_faces(lam_low, table_ref[...], elements), send_ref, conf_ref, elements)
    out_ref[...] = out.reshape(out_ref.shape)
    conf_lam_ref[0] = lower
    conf_lam_ref[1] = upper


def final_kernel(section, base_ref, back_ref, grad_ref, jac_ref, send_ref, conf_ref, table_ref, lam_ref):
    lam = update_of(section, base_ref, back_ref, grad_ref, jac_ref, send_ref, conf_ref, table_ref)
    for v in range(5):
        lam_ref[v] = lam[v]


def call(kernel, outs, *args, scratch=()):
    single = not isinstance(outs, (list, tuple))
    shapes = outs if single else [jax.ShapeDtypeStruct(s, t) for s, t in outs]
    return pl.pallas_call(
        kernel,
        out_shape=shapes,
        in_specs=[pl.BlockSpec(memory_space=pltpu.VMEM)] * len(args),
        out_specs=jax.tree.map(lambda _: pl.BlockSpec(memory_space=pltpu.VMEM), shapes),
        scratch_shapes=list(scratch),
    )(*args)


def trade(x):
    return lax.all_to_all(x, ("gy", "gz"), split_axis=0, concat_axis=0, tiled=True)


def neighbours(payload):
    peers = lax.axis_size("gz")
    up = [(i, (i + 1) % peers) for i in range(peers)]
    down = [(j, i) for i, j in up]
    if peers == 2:
        return lax.ppermute(payload, "gz", up)
    below = lax.ppermute(payload[1], "gz", up)
    above = lax.ppermute(payload[0], "gz", down)
    return jnp.stack([above, below], axis=0)


def per_device(adjoint, saved, inv_jac, stiffness, send_face, mortar_table, conf_faces):
    elements = adjoint.shape[0]
    sections = saved.shape[0]
    owners = lax.axis_size("gy") * lax.axis_size("gz")
    cap = send_face.shape[1] // owners
    faces = conf_faces.shape[2]
    table = jnp.asarray(restriction_table())
    forward, backward = (jnp.asarray(t) for t in projection_tables())
    jac = inv_jac.reshape(1, elements)
    S = jax.ShapeDtypeStruct
    lam = jnp.transpose(adjoint, (1, 0, 2))
    states = jnp.transpose(saved, (0, 2, 1, 3))
    rows = S((5, elements, ELEM), F32)
    slots = S((owners, cap, WIDTH), BF16)
    pair = S((2, faces, WIDTH), BF16)

    outgoing, conf_lam, conf_state = call(
        start_kernel,
        [((owners, (sections + 1) * cap, WIDTH), BF16), ((2, faces, WIDTH), BF16), ((sections, 2, faces, WIDTH), BF16)],
        lam, states, send_face, conf_faces, table,
    )
    first = incoming = trade(outgoing)
    for section in (2, 1, 0):
        near = neighbours(conf_lam)
        base, grad = call(
            functools.partial(volume_kernel, section),
            [(rows.shape, F32), (pair.shape, BF16)],
            lam, states, stiffness, jac, conf_lam, near, conf_state,
            scratch=(pltpu.VMEM((3, 5 * elements, ELEM), F32), pltpu.VMEM((5 * elements, ELEM), F32)),
        )
        out = call(functools.partial(mortar_kernel, section), slots, incoming, first, mortar_table, forward, backward)
        back = trade(out)
        shared = (base, back, grad, jac, send_face, conf_faces, table)
        if section:
            lam, outgoing, conf_lam = call(
                functools.partial(update_kernel, section),
                [(rows.shape, F32), (slots.shape, BF16), (pair.shape, BF16)],
                *shared,
            )
            incoming = trade(outgoing)
        else:
            lam = call(functools.partial(final_kernel, section), rows, *shared)
    return jnp.transpose(lam, (1, 0, 2))


def solution(mesh):
    return jax.shard_map(
        per_device,
        mesh=mesh,
        in_specs=(
            P(("gx", "gy", "gz"), None, None),
            P(None, ("gx", "gy", "gz"), None, None),
            P(("gx", "gy", "gz")),
            P(),
            P(("gx", "gy", "gz"), None),
            P(("gx", "gy", "gz"), None, None),
            P(("gx", "gy", "gz"), None, None),
        ),
        out_specs=P(("gx", "gy", "gz"), None, None),
        check_vma=False,
    )
```

profile of v0, /device:TPU:0, one launch (start us, length us, event | category | flops | bytes accessed | tf_op | source)
XLA Modules:
  0.0 92.4 jit_solution(12216957593839379045)
XLA Ops:
  0.0 0.0 copy-start.10
  0.0 3.8 %shard_map.100 = (bf16[8,64,384]{2,1,0:T(8,128)(2,1)}, bf16[2,16,384]{2,1,0:T(8,128)(2,1)}, bf16[3,2,16,384]{3,2,1,0:T(8,128)(2,1)}) custom-call(f32[5,32,512]{2,1,0:T(8,128)} %bitcast.8, bf16[3,5,32,512]{3,2,1,0:T(8,128)(2,1)} %bitcast.4, s32[1,128]{1,0:T(1,128)} %send_ref.7, s32[1,2,16]{2,1,0:T(2,128)} %conf_ref.7, bf16[512,384]{1,0:T(8,128)(2,1)} %constant.6.clone.table_ref), custom_call_target="tpu_custom_call" | custom-call | tf_op jit(solution)/shard_map/pallas_call | solution.py:348
  3.8 0.0 copy-start.4
  3.8 6.5 %all-to-all-start = ((bf16[8,64,384]{2,1,0:T(8,128)(2,1)}), bf16[8,64,384]{2,1,0:T(8,128)(2,1)S(1)}, u32[]{:S(2)}, u32[]{:S(2)}) async-start(bf16[8,64,384]{2,1,0:T(8,128)(2,1)} %get-tuple-element.23), calls=%async_computation | async-start | bytes 786432 | tf_op jit(solution)/shard_map/all_to_all | solution.py:358
  10.3 0.0 copy-done.10
  10.3 0.6 copy.11.map_ref
  10.9 11.9 %all-to-all-done.lam_ref.first_ref = bf16[8,64,384]{2,1,0:T(8,128)(2,1)S(1)} async-done(((bf16[8,64,384]{2,1,0:T(8,128)(2,1)}), bf16[8,64,384]{2,1,0:T(8,128)(2,1)S(1)}, u32[]{:S(2)}, u32[]{:S(2)}) %all-to-all-start) | async-done | bytes 393248 | tf_op jit(solution)/shard_map/all_to_all | solution.py:358
  22.8 0.0 copy-start
  22.8 0.7 copy-done
  23.6 2.9 %shard_map.102 = bf16[8,16,384]{2,1,0:T(8,128)(2,1)} custom-call(bf16[8,64,384]{2,1,0:T(8,128)(2,1)} %copy-done, bf16[8,64,384]{2,1,0:T(8,128)(2,1)} %copy-done, s32[1,5,64]{2,1,0:T(8,128)} %copy.11.map_ref, bf16[256,512]{1,0:T(8,128)(2,1)} %constant.7.clone.forward_ref, bf16[384,512]{1,0:T(8,128)(2,1)} %constant.8.clone.backward_ref), custom_call_target="tpu_custom_call" | custom-call | tf_op jit(solution)/shard_map/pallas_call | solution.py:348
  26.5 3.4 %all-to-all-start.1 = ((bf16[8,16,384]{2,1,0:T(8,128)(2,1)}), bf16[8,16,384]{2,1,0:T(8,128)(2,1)S(1)}, u32[]{:S(2)}, u32[]{:S(2)}) async-start(bf16[8,16,384]{2,1,0:T(8,128)(2,1)} %shard_map.102), calls=%async_computation.1 | async-start | bytes 196608 | tf_op jit(solution)/shard_map/all_to_all | solution.py:358
  29.8 0.0 copy-done.4
  29.8 0.4 collective-permute-start
  30.2 0.9 collective-permute-done.near_ref
  31.1 0.0 copy-start.9
  31.1 0.6 copy-done.9
  31.7 3.5 %shard_map.101 = (f32[5,32,512]{2,1,0:T(8,128)}, bf16[2,16,384]{2,1,0:T(8,128)(2,1)}) custom-call(f32[5,32,512]{2,1,0:T(8,128)} %bitcast.9, bf16[3,5,32,512]{3,2,1,0:T(8,128)(2,1)} %bitcast.5, bf16[3,512,512]{2,1,0:T(8,128)(2,1)} %stiff_ref.5, f32[1,32]{1,0:T(1,128)} %bitcast.10, bf16[2,16,384]{2,1,0:T(8,128)(2,1)} %get-tuple-element.20.own_ref, ...), custom_call_target="tpu_custom_call" | custom-call | tf_op jit(solution)/shard_map/pallas_call | solution.py:348
  35.3 0.8 all-to-all-done.1.back_ref
  36.1 0.0 copy-start.2
  36.1 0.6 copy-done.2
  36.7 2.9 %shard_map.103 = (f32[5,32,512]{2,1,0:T(8,128)}, bf16[8,16,384]{2,1,0:T(8,128)(2,1)}, bf16[2,16,384]{2,1,0:T(8,128)(2,1)}) custom-call(f32[5,32,512]{2,1,0:T(8,128)} %get-tuple-element.22.base_ref, bf16[8,16,384]{2,1,0:T(8,128)(2,1)} %copy-done.2, bf16[2,16,384]{2,1,0:T(8,128)(2,1)} %get-tuple-element.24.grad_ref, f32[1,32]{1,0:T(1,128)} %bitcast.11, ...), custom_call_target="tpu_custom_call" | custom-call | tf_op jit(solution)/shard_map/pallas_call | solution.py:348
  39.6 0.0 copy-start.6
  39.6 10.6 %all_to_all.30.lam_ref = bf16[8,16,384]{2,1,0:T(8,128)(2,1)} all-to-all(bf16[8,16,384]{2,1,0:T(8,128)(2,1)} %get-tuple-element.28), channel_id=1, replica_groups=mesh['gx'=4,'gy'=4,'gz'=2] {'gy','gz'}, dimensions={0} | all-to-all | bytes 196608 | tf_op jit(solution)/shard_map/all_to_all | solution.py:358
  50.3 2.8 %shard_map.105 = bf16[8,16,384]{2,1,0:T(8,128)(2,1)} custom-call(bf16[8,16,384]{2,1,0:T(8,128)(2,1)} %all_to_all.30.lam_ref, bf16[8,64,384]{2,1,0:T(8,128)(2,1)} %copy-done, s32[1,5,64]{2,1,0:T(8,128)} %copy.11.map_ref, bf16[256,512]{1,0:T(8,128)(2,1)} %constant.7.clone.forward_ref, bf16[384,512]{1,0:T(8,128)(2,1)} %constant.8.clone.backward_ref), custom_call_target="tpu_custom_call" | custom-call | tf_op jit(solution)/shard_map/pallas_call | solution.py:348
  53.1 3.4 %all-to-all-start.3 = ((bf16[8,16,384]{2,1,0:T(8,128)(2,1)}), bf16[8,16,384]{2,1,0:T(8,128)(2,1)S(1)}, u32[]{:S(2)}, u32[]{:S(2)}) async-start(bf16[8,16,384]{2,1,0:T(8,128)(2,1)} %shard_map.105), calls=%async_computation.3 | async-start | bytes 196608 | tf_op jit(solution)/shard_map/all_to_all | solution.py:358
  56.4 0.0 copy-done.6
  56.4 0.4 collective-permute-start.1
  56.8 0.9 collective-permute-done.1.near_ref
  57.7 0.0 copy-start.8
  57.7 0.6 copy-done.8
  58.3 3.5 %shard_map.104 = (f32[5,32,512]{2,1,0:T(8,128)}, bf16[2,16,384]{2,1,0:T(8,128)(2,1)}) custom-call(f32[5,32,512]{2,1,0:T(8,128)} %get-tuple-element.25.lam_ref, bf16[3,5,32,512]{3,2,1,0:T(8,128)(2,1)} %bitcast.6, bf16[3,512,512]{2,1,0:T(8,128)(2,1)} %stiff_ref.5, f32[1,32]{1,0:T(1,128)} %bitcast.12, bf16[2,16,384]{2,1,0:T(8,128)(2,1)} %get-tuple-element.26.own_ref, ...), custom_call_target="tpu_custom_call" | custom-call | tf_op jit(solution)/shard_map/pallas_call | solution.py:348
  61.9 0.8 all-to-all-done.3.back_ref
  62.7 0.0 copy-start.1
  62.7 0.6 copy-done.1
  63.3 2.9 %shard_map.106 = (f32[5,32,512]{2,1,0:T(8,128)}, bf16[8,16,384]{2,1,0:T(8,128)(2,1)}, bf16[2,16,384]{2,1,0:T(8,128)(2,1)}) custom-call(f32[5,32,512]{2,1,0:T(8,128)} %get-tuple-element.27.base_ref, bf16[8,16,384]{2,1,0:T(8,128)(2,1)} %copy-done.1, bf16[2,16,384]{2,1,0:T(8,128)(2,1)} %get-tuple-element.29.grad_ref, f32[1,32]{1,0:T(1,128)} %bitcast.13, ...), custom_call_target="tpu_custom_call" | custom-call | tf_op jit(solution)/shard_map/pallas_call | solution.py:348
  66.2 0.0 copy-start.5
  66.2 10.6 %all_to_all.31.lam_ref = bf16[8,16,384]{2,1,0:T(8,128)(2,1)} all-to-all(bf16[8,16,384]{2,1,0:T(8,128)(2,1)} %get-tuple-element.33), channel_id=1, replica_groups=mesh['gx'=4,'gy'=4,'gz'=2] {'gy','gz'}, dimensions={0} | all-to-all | bytes 196608 | tf_op jit(solution)/shard_map/all_to_all | solution.py:358
  76.9 2.8 %shard_map.108 = bf16[8,16,384]{2,1,0:T(8,128)(2,1)} custom-call(bf16[8,16,384]{2,1,0:T(8,128)(2,1)} %all_to_all.31.lam_ref, bf16[8,64,384]{2,1,0:T(8,128)(2,1)} %copy-done, s32[1,5,64]{2,1,0:T(8,128)} %copy.11.map_ref, bf16[256,512]{1,0:T(8,128)(2,1)} %constant.7.clone.forward_ref, bf16[384,512]{1,0:T(8,128)(2,1)} %constant.8.clone.backward_ref), custom_call_target="tpu_custom_call" | custom-call | tf_op jit(solution)/shard_map/pallas_call | solution.py:348
  79.7 3.4 %all-to-all-start.5 = ((bf16[8,16,384]{2,1,0:T(8,128)(2,1)}), bf16[8,16,384]{2,1,0:T(8,128)(2,1)S(1)}, u32[]{:S(2)}, u32[]{:S(2)}) async-start(bf16[8,16,384]{2,1,0:T(8,128)(2,1)} %shard_map.108), calls=%async_computation.5 | async-start | bytes 196608 | tf_op jit(solution)/shard_map/all_to_all | solution.py:358
  83.0 0.0 copy-done.5
  83.0 0.4 collective-permute-start.2
  83.4 0.9 collective-permute-done.2.near_ref
  84.3 0.0 copy-start.7
  84.3 0.6 copy-done.7
  84.9 3.5 %shard_map.107 = (f32[5,32,512]{2,1,0:T(8,128)}, bf16[2,16,384]{2,1,0:T(8,128)(2,1)}) custom-call(f32[5,32,512]{2,1,0:T(8,128)} %get-tuple-element.30.lam_ref, bf16[3,5,32,512]{3,2,1,0:T(8,128)(2,1)} %bitcast.7, bf16[3,512,512]{2,1,0:T(8,128)(2,1)} %stiff_ref.5, f32[1,32]{1,0:T(1,128)} %bitcast.14, bf16[2,16,384]{2,1,0:T(8,128)(2,1)} %get-tuple-element.31.own_ref, ...), custom_call_target="tpu_custom_call" | custom-call | tf_op jit(solution)/shard_map/pallas_call | solution.py:348
  88.5 0.8 all-to-all-done.5.back_ref
  89.3 0.0 copy-start.3
  89.3 0.6 copy-done.3
  89.9 2.5 %shard_map.109 = f32[5,32,512]{2,1,0:T(8,128)} custom-call(f32[5,32,512]{2,1,0:T(8,128)} %get-tuple-element.32.base_ref, bf16[8,16,384]{2,1,0:T(8,128)(2,1)} %copy-done.3, bf16[2,16,384]{2,1,0:T(8,128)(2,1)} %get-tuple-element.34.grad_ref, f32[1,32]{1,0:T(1,128)} %bitcast.15, s32[1,128]{1,0:T(1,128)} %send_ref.7, s32[1,2,16]{2,1,0:T(2,128)} %conf_ref.7, ...), custom_call_target="tpu_custom_call" | custom-call | tf_op jit(solution)/shard_map/pallas_call | solution.py:348
Async XLA Ops:
  0.0 10.3 %copy-start.10 = (s32[1,5,64]{2,0,1:T(1,128)S(1)}, s32[1,5,64]{2,0,1:T(1,128)}, u32[]{:S(2)}) copy-start(s32[1,5,64]{2,0,1:T(1,128)} %param.15) | copy-start | bytes 3844
  3.8 26.0 %copy-start.4 = (bf16[2,16,384]{2,1,0:T(8,128)(2,1)S(1)}, bf16[2,16,384]{2,1,0:T(8,128)(2,1)}, u32[]{:S(2)}) copy-start(bf16[2,16,384]{2,1,0:T(8,128)(2,1)} %get-tuple-element.20.own_ref) | copy-start | bytes 73732
  3.8 19.0 %all-to-all-start = ((bf16[8,64,384]{2,1,0:T(8,128)(2,1)}), bf16[8,64,384]{2,1,0:T(8,128)(2,1)S(1)}, u32[]{:S(2)}, u32[]{:S(2)}) async-start(bf16[8,64,384]{2,1,0:T(8,128)(2,1)} %get-tuple-element.23), calls=%async_computation | async-start | bytes 786432 | tf_op jit(solution)/shard_map/all_to_all | solution.py:358
  22.8 0.7 copy-start
  26.5 9.6 %all-to-all-start.1 = ((bf16[8,16,384]{2,1,0:T(8,128)(2,1)}), bf16[8,16,384]{2,1,0:T(8,128)(2,1)S(1)}, u32[]{:S(2)}, u32[]{:S(2)}) async-start(bf16[8,16,384]{2,1,0:T(8,128)(2,1)} %shard_map.102), calls=%async_computation.1 | async-start | bytes 196608 | tf_op jit(solution)/shard_map/all_to_all | solution.py:358
  29.8 1.3 %collective-permute-start = (bf16[2,16,384]{2,1,0:T(8,128)(2,1)S(1)}, bf16[2,16,384]{2,1,0:T(8,128)(2,1)S(1)}, u32[]{:S(2)}, u32[]{:S(2)}) collective-permute-start(bf16[2,16,384]{2,1,0:T(8,128)(2,1)S(1)} %copy-done.4), channel_id=1, source_target_pairs={{0,1},{1,0},{2,3},{3,2},{4,5},{5,4},{6,7},{7,6},{8,9},{9,8},{10,11... | collective-permute-start | bytes 73736 | tf_op jit(solution)/shard_map/ppermute | solution.py:366
  31.1 0.6 copy-start.9
  36.1 0.6 copy-start.2
  39.6 16.8 %copy-start.6 = (bf16[2,16,384]{2,1,0:T(8,128)(2,1)S(1)}, bf16[2,16,384]{2,1,0:T(8,128)(2,1)}, u32[]{:S(2)}) copy-start(bf16[2,16,384]{2,1,0:T(8,128)(2,1)} %get-tuple-element.26.own_ref) | copy-start | bytes 73732
  53.1 9.6 %all-to-all-start.3 = ((bf16[8,16,384]{2,1,0:T(8,128)(2,1)}), bf16[8,16,384]{2,1,0:T(8,128)(2,1)S(1)}, u32[]{:S(2)}, u32[]{:S(2)}) async-start(bf16[8,16,384]{2,1,0:T(8,128)(2,1)} %shard_map.105), calls=%async_computation.3 | async-start | bytes 196608 | tf_op jit(solution)/shard_map/all_to_all | solution.py:358
  56.4 1.3 %collective-permute-start.1 = (bf16[2,16,384]{2,1,0:T(8,128)(2,1)S(1)}, bf16[2,16,384]{2,1,0:T(8,128)(2,1)S(1)}, u32[]{:S(2)}, u32[]{:S(2)}) collective-permute-start(bf16[2,16,384]{2,1,0:T(8,128)(2,1)S(1)} %copy-done.6), channel_id=1, source_target_pairs={{0,1},{1,0},{2,3},{3,2},{4,5},{5,4},{6,7},{7,6},{8,9},{9,8},{10,11... | collective-permute-start | bytes 73736 | tf_op jit(solution)/shard_map/ppermute | solution.py:366
  57.7 0.6 copy-start.8
  62.7 0.6 copy-start.1
  66.2 16.8 %copy-start.5 = (bf16[2,16,384]{2,1,0:T(8,128)(2,1)S(1)}, bf16[2,16,384]{2,1,0:T(8,128)(2,1)}, u32[]{:S(2)}) copy-start(bf16[2,16,384]{2,1,0:T(8,128)(2,1)} %get-tuple-element.31.own_ref) | copy-start | bytes 73732
  79.7 9.6 %all-to-all-start.5 = ((bf16[8,16,384]{2,1,0:T(8,128)(2,1)}), bf16[8,16,384]{2,1,0:T(8,128)(2,1)S(1)}, u32[]{:S(2)}, u32[]{:S(2)}) async-start(bf16[8,16,384]{2,1,0:T(8,128)(2,1)} %shard_map.108), calls=%async_computation.5 | async-start | bytes 196608 | tf_op jit(solution)/shard_map/all_to_all | solution.py:358
  83.0 1.3 %collective-permute-start.2 = (bf16[2,16,384]{2,1,0:T(8,128)(2,1)S(1)}, bf16[2,16,384]{2,1,0:T(8,128)(2,1)S(1)}, u32[]{:S(2)}, u32[]{:S(2)}) collective-permute-start(bf16[2,16,384]{2,1,0:T(8,128)(2,1)S(1)} %copy-done.5), channel_id=1, source_target_pairs={{0,1},{1,0},{2,3},{3,2},{4,5},{5,4},{6,7},{7,6},{8,9},{9,8},{10,11... | collective-permute-start | bytes 73736 | tf_op jit(solution)/shard_map/ppermute | solution.py:366
  84.3 0.6 copy-start.7
  89.3 0.6 copy-start.3
where the time goes:
time: 93.4 us; the launch traced here: 92.4 us
  Pallas kernels  31.2 us (33%)
  blocking collectives  21.3 us (23%)
  starting transfers between devices  17.7 us (19%)
  waiting for transfers between devices  17.1 us (18%)
  local copies, waits for them, and re-layouts  5.05 us (5%)
    pallas_call x10, Pallas kernels, call(): pl.pallas_call(kernel, out_shape=shapes, in_specs=[pl.BlockSpec(memory_sp...  31.2 us
    all_to_all x2, blocking collectives, trade(): lax.all_to_all(x, ('gy', 'gz'), split_axis=0, concat_axis=0, tiled=True)  21.3 us
    all_to_all x4, starting transfers between devices, trade(): lax.all_to_all(x, ('gy', 'gz'), split_axis=0, concat_axis=0, tiled=True)  16.6 us
    all_to_all x4, waiting for transfers between devices, trade(): lax.all_to_all(x, ('gy', 'gz'), split_axis=0, concat_axis=0, tiled=True)  14.3 us
    unnamed x23, local copies, waits for them, and re-layouts  5.05 us
    ppermute x3, waiting for transfers between devices, neighbours(): return lax.ppermute(payload, 'gz', up)  2.72 us
  transfers between devices with their start and end apart: 7, of which 7 were waited for; matrix products, arithmetic and copies ran while one was open for 1% of the time, Pallas kernels for 11%

commit v1 on v0

v1 whole, which is shorter than its diff:
```python
import functools

import jax
import jax.numpy as jnp
import numpy as np
from jax import lax
from jax.experimental import pallas as pl
from jax.experimental.pallas import tpu as pltpu
from jax.sharding import PartitionSpec as P

ORDER = 7
LINE = ORDER + 1
FACE = LINE * LINE
ELEM = FACE * LINE
PAIRS = 3
TILE = 2 * FACE
ROWS = 5 * FACE
EXTRA = 16

gamma_gas = 1.4
penalty = 1.5
viscosity = 0.5
step_size = 0.2
section_weights = (0.25, 0.25, 0.5)
GM1 = gamma_gas - 1.0
REST = (1.0, 0.0, 0.0, 0.0, 2.5)
F32 = jnp.float32
VMEM_GRANT = 24 << 20
BF16 = jnp.bfloat16


def lagrange_matrix(points, abscissa):
    out = np.ones((LINE, LINE))
    for target in range(LINE):
        for other in range(LINE):
            if other != target:
                out[:, target] *= (points - abscissa[other]) / (abscissa[target] - abscissa[other])
    return out


def split_low(matrix):
    high = matrix.astype(np.float32).astype(BF16)
    low = (matrix - high.astype(np.float64)).astype(np.float32).astype(BF16)
    return high, low


def projection_tables():
    abscissa = -np.cos(np.pi * np.arange(LINE) / ORDER)
    halves = [lagrange_matrix((abscissa + 2.0 * h - 1.0) * 0.5, abscissa) for h in range(2)]
    children = [np.kron(halves[c // 2], halves[c % 2]) for c in range(4)]
    fh, fl = split_low(np.concatenate(children, axis=0))
    bh, bl = split_low(np.concatenate([m.T for m in children], axis=0))
    return np.concatenate([fh, fl], axis=1), np.concatenate([bh, bh, bl], axis=1)


def restriction_table():
    column = np.arange(6 * FACE)
    face, local = column // FACE, column % FACE
    first, second = local // LINE, local % LINE
    axis, fixed = face // 2, face % 2 * (LINE - 1)
    x = np.where(axis == 0, fixed, first)
    y = np.where(axis == 0, first, np.where(axis == 1, fixed, second))
    z = np.where(axis == 2, fixed, second)
    node = x * FACE + y * LINE + z
    return (np.arange(ELEM)[:, None] == node[None, :]).astype(np.float32).astype(BF16)


def dot(a, b, ca=1, cb=0):
    return lax.dot_general(a, b, (((ca,), (cb,)), ((), ())), preferred_element_type=F32)


def low_lanes(rows):
    return lax.broadcasted_iota(jnp.int32, (rows, TILE), 1) < FACE


def swap(x):
    return pltpu.roll(x, FACE, 1)


def exchange(a, b, low):
    return jnp.where(low, a, swap(b)), jnp.where(low, swap(a), b)


def flux_pull(u, w, picks):
    inv = 1.0 / u[0]
    vel = [u[i] * inv for i in (1, 2, 3)]
    kin = 0.5 * (vel[0] * vel[0] + vel[1] * vel[1] + vel[2] * vel[2])
    enth = gamma_gas * (u[4] * inv) - GM1 * kin
    q = w[1] * vel[0] + w[2] * vel[1] + w[3] * vel[2]
    if picks is None:
        vn, wn = vel[2], w[3]
    else:
        vn = jnp.where(picks[0], vel[0], jnp.where(picks[1], vel[1], vel[2]))
        wn = jnp.where(picks[0], w[1], jnp.where(picks[1], w[2], w[3]))
    r = vn * w[4]
    a = w[0] + q + enth * w[4]
    g = [GM1 * kin * wn - vn * q + (GM1 * kin - enth) * r]
    t = GM1 * (wn + r)
    for i in range(3):
        gi = w[1 + i] * vn - vel[i] * t
        if picks is None:
            gi = gi + a if i == 2 else gi
        else:
            gi = gi + jnp.where(picks[i], a, 0.0)
        g.append(gi)
    g.append(GM1 * wn + gamma_gas * r)
    return g


def trace_faces(field_low, table, elements):
    traced = dot(field_low, table)
    low = low_lanes(elements)
    zero = jnp.zeros((elements, TILE), F32)
    rows = [[None] * PAIRS for _ in range(6)]

    def piece(v, k):
        if v >= 5:
            return zero
        return traced[v * elements : (v + 1) * elements, k * TILE : (k + 1) * TILE]

    for j in range(PAIRS):
        for k in range(3):
            rows[2 * k][j], rows[2 * k + 1][j] = exchange(piece(2 * j, k), piece(2 * j + 1, k), low)
    return jnp.concatenate([jnp.concatenate(r, axis=1) for r in rows], axis=0).astype(BF16)


def lift_slots(grads, hot, table, elements):
    padded = jnp.concatenate([g.astype(BF16) for g in grads] + [jnp.zeros(grads[0].shape, BF16)], axis=0)
    face_grad = dot(hot, padded, 1, 1)
    low = low_lanes(elements)
    rows = [[None] * 3 for _ in range(6)]

    def piece(f, j):
        return face_grad[f * elements : (f + 1) * elements, j * TILE : (j + 1) * TILE]

    for j in range(PAIRS):
        for k in range(3):
            rows[2 * j][k], rows[2 * j + 1][k] = exchange(piece(2 * k, j), piece(2 * k + 1, j), low)
    arranged = jnp.concatenate([jnp.concatenate(r, axis=1) for r in rows[:5]], axis=0).astype(BF16)
    return dot(arranged, table, 1, 1)


def column_of(row):
    n = row.shape[1]
    same = lax.broadcasted_iota(jnp.int32, (n, n), 0) == lax.broadcasted_iota(jnp.int32, (n, n), 1)
    return jnp.sum(jnp.where(same, jnp.broadcast_to(row, (n, n)), 0.0), axis=1, keepdims=True)


def slot_values(field_low, hot, table, elements):
    faces = trace_faces(field_low, table, elements)
    return dot(faces, hot, 0, 0).astype(BF16)[:ROWS]


def start_kernel(lam_ref, send_ref, conf_ref, map_ref, table_ref, out_ref, shared_ref, hot_ref, ids_ref):
    elements = lam_ref.shape[1]
    slots = send_ref.shape[1]
    faces = conf_ref.shape[2]
    ids_ref[...] = jnp.full(ids_ref.shape, -1, jnp.int32)
    ids_ref[0:1, 0:slots] = send_ref[...]
    ids_ref[0:1, slots : slots + faces] = conf_ref[0, 0:1]
    ids_ref[0:1, slots + faces : slots + 2 * faces] = conf_ref[0, 1:2]
    shape = hot_ref.shape
    row = lax.broadcasted_iota(jnp.int32, shape, 0)
    face = row // elements
    ident = 6 * (row - face * elements) + face
    hot = jnp.where(ident == ids_ref[0:1], 1.0, 0.0).astype(BF16)
    hot_ref[...] = hot
    lam_low = lam_ref[...].astype(BF16).reshape(5 * elements, ELEM)
    values = slot_values(lam_low, hot, table_ref[...], elements)
    out_ref[0:ROWS] = values[:, :slots]
    shared_ref[...] = values[:, slots:]
    rows = map_ref[0]
    mortars = rows.shape[1]
    slot = lax.broadcasted_iota(jnp.int32, (slots, mortars), 0)
    field = lax.broadcasted_iota(jnp.int32, (EXTRA, mortars), 0)
    known = jnp.where(field == 1, rows[2:3], jnp.where(field == 2, rows[3:4], jnp.where(field == 3, rows[4:5], 0)))
    info = None
    for mine, other, left in ((0, 1, 1), (1, 0, 0)):
        hits = jnp.where(slot == rows[mine : mine + 1], 1.0, 0.0).astype(BF16)
        fields = jnp.where(field == 0, rows[other : other + 1], jnp.where(field == 4, left, known))
        part = dot(fields.astype(F32).astype(BF16), hits, 1, 1)
        info = part if info is None else info + part
    out_ref[ROWS:] = info.astype(BF16)


def state_kernel(saved_ref, hot_ref, table_ref, out_ref):
    elements = saved_ref.shape[2]
    for s in range(saved_ref.shape[0]):
        out_ref[s] = slot_values(saved_ref[s].reshape(5 * elements, ELEM), hot_ref[...], table_ref[...], elements)


def volume_kernel(section, faces, lam_ref, saved_ref, stiff_ref, jac_ref, own_ref, near_ref, state_ref, hot_ref, table_ref, base_ref, slope_ref, smooth_ref):
    elements = lam_ref.shape[1]
    coef = step_size * section_weights[section]
    lam_low = lam_ref[...].astype(BF16).reshape(5 * elements, ELEM)

    slots = state_ref.shape[2] - own_ref.shape[1]
    width = own_ref.shape[1]
    lane = lax.broadcasted_iota(jnp.int32, (FACE, width), 1)
    used = lane < 2 * faces
    lower = lane < faces
    sign = jnp.where(lower, -1.0, 1.0)
    w, u = [], []
    for v in range(5):
        rows = slice(v * FACE, (v + 1) * FACE)
        near = near_ref[rows].astype(F32)
        near = jnp.where(lower, pltpu.roll(near, width - faces, 1), pltpu.roll(near, faces, 1))
        w.append(jnp.where(used, sign * (near - own_ref[rows].astype(F32)), 0.0))
        u.append(jnp.where(used, state_ref[section, rows, slots:].astype(F32), REST[v]))
    g = flux_pull(u, w, None)
    grads = [0.5 * g[v] + (0.5 * penalty) * sign * w[v] for v in range(5)]
    total = viscosity * -1.0
    smooth = lift_slots(grads, hot_ref[:, slots:], table_ref[...], elements)
    for d in range(3):
        slopes = dot(lam_low, stiff_ref[d])
        slope_ref[d] = slopes
        smooth = smooth + total * dot(slopes.astype(BF16), stiff_ref[d], 1, 1)
    smooth_ref[...] = smooth
    jac = column_of(jac_ref[...]) * coef
    step = 16
    for r in range(0, elements, step):
        scale = jnp.broadcast_to(jac[r : r + step], (step, 128))
        for c in range(0, ELEM, 128):
            u = [saved_ref[section, v, r : r + step, c : c + 128].astype(F32) for v in range(5)]
            inv = 1.0 / u[0]
            vel = [u[i] * inv for i in (1, 2, 3)]
            kin = 0.5 * (vel[0] * vel[0] + vel[1] * vel[1] + vel[2] * vel[2])
            enth = gamma_gas * (u[4] * inv) - GM1 * kin
            trace = run = first = None
            g = [None, None, None, None]
            for d in range(3):
                w = [slope_ref[d, v * elements + r : v * elements + r + step, c : c + 128] for v in range(5)]
                q = w[1] * vel[0] + w[2] * vel[1] + w[3] * vel[2]
                term = vel[d] * q
                first = term if first is None else first + term
                trace = w[1 + d] if trace is None else trace + w[1 + d]
                part = vel[d] * w[4]
                run = part if run is None else run + part
                for i in range(3):
                    gi = w[1 + i] * vel[d]
                    if i == d:
                        gi = gi + (w[0] + q + enth * w[4])
                    g[1 + i] = gi if g[1 + i] is None else g[1 + i] + gi
            t = GM1 * (trace + run)
            pulled = [GM1 * kin * trace - first + (GM1 * kin - enth) * run]
            pulled += [g[1 + i] - vel[i] * t for i in range(3)]
            pulled.append(GM1 * trace + gamma_gas * run)
            for v in range(5):
                rows = slice(v * elements + r, v * elements + r + step)
                vol = pulled[v] + smooth_ref[rows, c : c + 128]
                base_ref[v, r : r + step, c : c + 128] = lam_ref[v, r : r + step, c : c + 128] + scale * vol

def spread_children(matrix, stacked):
    return dot(matrix, jnp.concatenate(stacked, axis=0))


def choose(raw, spread, child, keep=None):
    out = []
    for v, value in enumerate(raw):
        width = value.shape[1]
        picked = value
        for c in range(4):
            hit = child[c] if keep is None else child[c] & keep
            picked = jnp.where(hit, spread[c * FACE : (c + 1) * FACE, v * width : (v + 1) * width], picked)
        out.append(picked)
    return out


def read_table(pieces, me_ref, cap, relative):
    slots = pieces[0].shape[1]
    me = me_ref[0]
    lane = lax.broadcasted_iota(jnp.int32, (EXTRA, slots), 1)
    owner_of = lane // cap
    info = jnp.zeros((EXTRA, slots), F32)
    for p, piece in enumerate(pieces):
        owner = me ^ p if relative else p
        shift = lax.rem((owner - me) * cap + slots, slots)
        moved = pltpu.roll(piece[ROWS:].astype(F32), shift, 1)
        info = jnp.where(owner_of == owner, moved, info)
    info = info.astype(jnp.int32)
    source = info[0:1] // cap
    rank = info[0:1] - source * cap
    if relative:
        source = source ^ me
    code = source * slots + owner_of[0:1] * cap + rank
    field = lax.broadcasted_iota(jnp.int32, (EXTRA, slots), 0)
    return jnp.where(field == 0, code, info)


def mortar_update(section, relative, first, last, count, *refs):
    refs = list(refs)
    pieces = [r[...] for r in refs[:count]]
    own_ref = refs[count]
    base_ref, state_ref, hot_ref, table_ref, jac_ref, forward_ref, backward_ref, me_ref, info_ref = refs[count + 1 : count + 10]
    outs = refs[count + 10 :]
    elements = base_ref.shape[1]
    if len(pieces) == 1 and pieces[0].ndim == 3:
        pieces = [pieces[0][p] for p in range(pieces[0].shape[0])]
    slots = pieces[0].shape[1]
    cap = slots // len(pieces)
    if first:
        info = read_table(pieces, me_ref, cap, relative)
        outs[0][...] = info
        outs = outs[1:]
    else:
        info = info_ref[...]
    code, child, axis, live, left = (jnp.broadcast_to(info[k : k + 1], (FACE, slots)) for k in range(5))
    row = lax.broadcasted_iota(jnp.int32, (slots, slots), 0)
    partner = None
    for p in range(0, len(pieces), 2):
        both = jnp.concatenate([pieces[p][:ROWS], pieces[p + 1][:ROWS]], axis=1)
        hits = [jnp.where(row + (p + i) * slots == info[0:1], 1.0, 0.0).astype(BF16) for i in range(2)]
        part = dot(both, jnp.concatenate(hits, axis=0))
        partner = part if partner is None else partner + part
    is_left = left == 1
    alive = live == 1
    child = [child == c + 1 for c in range(4)]
    picks = [axis == n for n in range(3)]

    def variables(x):
        return [x[v * FACE : (v + 1) * FACE].astype(F32) for v in range(5)]

    own, partner, state = variables(own_ref[:ROWS]), variables(partner), variables(state_ref[section][:, :slots])
    left_lam = [jnp.where(is_left, a, b) for a, b in zip(own, partner)]
    right_lam = [jnp.where(is_left, b, a) for a, b in zip(own, partner)]
    stacked = jnp.concatenate([x.astype(BF16) for x in left_lam + state], axis=1)
    spread = spread_children(forward_ref[...], [stacked, stacked])
    left_lam = choose(left_lam, spread, child)
    u = choose(state, spread[:, 5 * slots :], child, is_left)
    w = [jnp.where(alive, b - a, 0.0) for a, b in zip(left_lam, right_lam)]
    u = [jnp.where(alive, u[v], REST[v]) for v in range(5)]
    g = flux_pull(u, w, picks)
    side = jnp.where(is_left, 0.5 * penalty, -0.5 * penalty)
    pull = [0.5 * g[v] + side * w[v] for v in range(5)]
    stacked = jnp.concatenate(pull, axis=1)
    high = stacked.astype(BF16)
    rest = (stacked - high.astype(F32)).astype(BF16)
    spread = spread_children(backward_ref[...], [high, rest, high])
    grads = choose(pull, spread, child, is_left)

    table = table_ref[...]
    lifted = lift_slots(grads, hot_ref[:, :slots], table, elements)
    jac = column_of(jac_ref[...]) * (step_size * section_weights[section])
    lam = [base_ref[v] + jac * lifted[v * elements : (v + 1) * elements] for v in range(5)]
    for v in range(5):
        outs[0][v] = lam[v]
    if not last:
        lam_low = jnp.concatenate([x.astype(BF16) for x in lam], axis=0)
        values = slot_values(lam_low, hot_ref[...], table, elements)
        outs[1][...] = values[:, :slots]
        outs[2][...] = values[:, slots:]


def call(kernel, outs, args, scratch=(), scalars=(), last=False):
    specs = [pl.BlockSpec(memory_space=pltpu.SMEM if i in scalars else pltpu.VMEM) for i in range(len(args))]
    args = [a if i in scalars else pltpu.with_memory_space_constraint(a, pltpu.VMEM) for i, a in enumerate(args)]
    shapes = [jax.ShapeDtypeStruct(o, t) if last else pltpu.VMEM(o, t) for o, t in outs]
    return pl.pallas_call(
        kernel,
        out_shape=shapes,
        in_specs=specs,
        out_specs=[pl.BlockSpec(memory_space=pltpu.VMEM)] * len(outs),
        scratch_shapes=list(scratch),
        compiler_params=pltpu.CompilerParams(vmem_limit_bytes=VMEM_GRANT),
    )(*args)


def power_of_two(n):
    return n & (n - 1) == 0


def gather_group(x):
    ny, nz = lax.axis_size("gy"), lax.axis_size("gz")
    if nz != 2 or not power_of_two(ny) or ny > 8:
        return [lax.all_gather(x, ("gy", "gz"), axis=0, tiled=False)], False
    pieces = []
    for k in range(ny):
        here = x if k == 0 else lax.ppermute(x, "gy", [(i, i ^ k) for i in range(ny)])
        pieces += [here, lax.ppermute(here, "gz", [(0, 1), (1, 0)])]
    return pieces, True


def neighbours(payload, faces):
    peers = lax.axis_size("gz")
    up = [(i, (i + 1) % peers) for i in range(peers)]
    down = [(j, i) for i, j in up]
    if peers == 2:
        return lax.ppermute(payload, "gz", up)
    below = lax.ppermute(payload, "gz", up)
    above = lax.ppermute(payload, "gz", down)
    lane = lax.broadcasted_iota(jnp.int32, payload.shape, 1)
    return jnp.where(lane < faces, above, below)


def per_device(adjoint, saved, inv_jac, stiffness, send_face, mortar_table, conf_faces):
    elements = adjoint.shape[0]
    sections = saved.shape[0]
    slots = send_face.shape[1]
    faces = conf_faces.shape[2]
    shared = -(-2 * faces // 128) * 128
    table = jnp.asarray(restriction_table())
    forward, backward = (jnp.asarray(t) for t in projection_tables())
    jac = inv_jac.reshape(1, elements)
    lam = jnp.transpose(adjoint, (1, 0, 2))
    states = jnp.transpose(saved, (0, 2, 1, 3))
    me = lax.axis_index(("gy", "gz")).astype(jnp.int32).reshape(1)
    rows = ((5, elements, ELEM), F32)
    sent = ((ROWS, slots), BF16)
    conforming = ((ROWS, shared), BF16)
    info_shape = ((EXTRA, slots), jnp.int32)

    outgoing, own_shared, hot = call(
        start_kernel,
        [((ROWS + EXTRA, slots), BF16), conforming, ((6 * elements, slots + shared), BF16)],
        [lam, send_face, conf_faces, mortar_table, table],
        scratch=(pltpu.VMEM((8, slots + shared), jnp.int32),),
    )
    (values,) = call(state_kernel, [((sections, ROWS, slots + shared), BF16)], [states, hot, table])
    info = jnp.zeros(info_shape[0], jnp.int32)
    for section in (2, 1, 0):
        pieces, relative = gather_group(outgoing)
        near = neighbours(own_shared, faces)
        (base,) = call(
            functools.partial(volume_kernel, section, faces),
            [rows],
            [lam, states, stiffness, jac, own_shared, near, values, hot, table],
            scratch=(pltpu.VMEM((3, 5 * elements, ELEM), F32), pltpu.VMEM((5 * elements, ELEM), F32)),
        )
        first, last = section == sections - 1, section == 0
        outs = ([info_shape] if first else []) + [rows] + ([] if last else [sent, conforming])
        args = pieces + [outgoing, base, values, hot, table, jac, forward, backward, me, info]
        out = call(
            functools.partial(mortar_update, section, relative, first, last, len(pieces)),
            outs, args, scalars=(len(args) - 2,), last=last,
        )
        if first:
            info, out = out[0], out[1:]
        lam = out[0]
        if not last:
            outgoing, own_shared = out[1:]
    return jnp.transpose(lam, (1, 0, 2))


def solution(mesh):
    return jax.shard_map(
        per_device,
        mesh=mesh,
        in_specs=(
            P(("gx", "gy", "gz"), None, None),
            P(None, ("gx", "gy", "gz"), None, None),
            P(("gx", "gy", "gz")),
            P(),
            P(("gx", "gy", "gz"), None),
            P(("gx", "gy", "gz"), None, None),
            P(("gx", "gy", "gz"), None, None),
        ),
        out_specs=P(("gx", "gy", "gz"), None, None),
        check_vma=False,
    )
```

time: 93.4 us -> 55.3 us (0.59)
  blocking collectives: 21.3 us -> 0 us
  Pallas kernels: 31.2 us -> 13.1 us
  local copies, waits for them, and re-layouts: 5.05 us -> 7.46 us
    all_to_all x2 -> x0, blocking collectives: 21.3 us -> none  [trade(): lax.all_to_all(x, ('gy', 'gz'), split_axis=0, concat_axis=0, tiled=True)]
    pallas_call x10 -> x8, Pallas kernels: 31.2 us -> 13.1 us  [call(): pl.pallas_call(kernel, out_shape=shapes, in_specs=specs, out_specs=[pl.Bl...]
    ppermute x0 -> x21, waiting for transfers between devices: none -> 16.9 us  [the longest x9 16.9 us: gather_group(): lax.ppermute(x, 'gy', [(i, i ^ k) for i in range(ny)])]
    all_to_all x4 -> x0, starting transfers between devices: 16.6 us -> none  [trade(): lax.all_to_all(x, ('gy', 'gz'), split_axis=0, concat_axis=0, tiled=True)]
    ppermute x0 -> x21, starting transfers between devices: none -> 16.2 us  [the longest x9 14.7 us: gather_group(): lax.ppermute(x, 'gy', [(i, i ^ k) for i in range(ny)])]
    all_to_all x4 -> x0, waiting for transfers between devices: 14.3 us -> none  [trade(): lax.all_to_all(x, ('gy', 'gz'), split_axis=0, concat_axis=0, tiled=True)]
    ppermute x3, waiting for transfers between devices: 2.72 us -> 0.01 us  [neighbours(): return lax.ppermute(payload, 'gz', up)]
    unnamed x23 -> x29, local copies, waits for them, and re-layouts: 5.05 us -> 7.45 us
  transfers between devices with their start and end apart: 7 -> 24, of which waited for: 7 -> 6; matrix products, arithmetic and copies ran while one was open for 1% -> 0% of each run, Pallas kernels for 11% -> 10%
where the time goes in v1:
time: 55.3 us; the launch traced here: 54.9 us
  starting transfers between devices  17.3 us (31%)
  waiting for transfers between devices  16.9 us (31%)
  Pallas kernels  13.1 us (24%)
  local copies, waits for them, and re-layouts  7.46 us (13%)
    ppermute x9, waiting for transfers between devices, gather_group(): lax.ppermute(x, 'gy', [(i, i ^ k) for i in range(ny)])  16.9 us
    ppermute x9, starting transfers between devices, gather_group(): lax.ppermute(x, 'gy', [(i, i ^ k) for i in range(ny)])  14.7 us
    pallas_call x8, Pallas kernels, call(): pl.pallas_call(kernel, out_shape=shapes, in_specs=specs, out_specs=[pl.Bl...  13.1 us
    unnamed x29, local copies, waits for them, and re-layouts  7.45 us
    ppermute x12, starting transfers between devices, gather_group(): pieces += [here, lax.ppermute(here, 'gz', [(0, 1), (1, 0)])]  1.55 us
  transfers between devices with their start and end apart: 24, of which 6 were waited for; matrix products, arithmetic and copies ran while one was open for 0% of the time, Pallas kernels for 10%

profile of v1, /device:TPU:0, one launch (start us, length us, event | category | flops | bytes accessed | tf_op | source)
XLA Modules:
  0.0 54.9 jit_solution(7622177165786900857)
XLA Ops:
  0.0 0.7 %copy.11.map_ref = s32[1,5,64]{2,1,0:T(8,128)S(1)} copy(s32[1,5,64]{2,0,1:T(1,128)} %param.15) | data formatting | bytes 2560 | tf_op args[5]
  0.7 1.0 %copy-done = bf16[512,384]{1,0:T(8,128)(2,1)S(1)} copy-done((bf16[512,384]{1,0:T(8,128)(2,1)S(1)}, bf16[512,384]{1,0:T(8,128)(2,1)}, u32[]{:S(2)}) %copy-start) | copy-done | bytes 393240
  1.7 1.0 %copy-done.7 = f32[32,5,512]{2,0,1:T(8,128)S(1)} copy-done((f32[32,5,512]{2,0,1:T(8,128)S(1)}, f32[32,5,512]{2,0,1:T(8,128)}, u32[]{:S(2)}) %copy-start.7) | copy-done | bytes 327704
  2.7 0.7 %copy-done.12 = s32[1,2,16]{2,1,0:T(2,128)S(1)} copy-done((s32[1,2,16]{2,1,0:T(2,128)S(1)}, s32[1,2,16]{2,1,0:T(2,128)}, u32[]{:S(2)}) %copy-start.12) | copy-done | bytes 152
  3.4 0.7 %copy-done.13 = s32[1,128]{1,0:T(1,128)S(1)} copy-done((s32[1,128]{1,0:T(1,128)S(1)}, s32[1,128]{1,0:T(1,128)}, u32[]{:S(2)}) %copy-start.13) | copy-done | bytes 536
  4.0 0.6 %shard_map.100 = (bf16[336,128]{1,0:T(8,128)(2,1)S(1)}, bf16[320,128]{1,0:T(8,128)(2,1)S(1)}, bf16[192,256]{1,0:T(8,128)(2,1)S(1)}) custom-call(f32[5,32,512]{2,1,0:T(8,128)S(1)} %bitcast.9, s32[1,128]{1,0:T(1,128)S(1)} %copy-done.13, s32[1,2,16]{2,1,0:T(2,128)S(1)} %copy-done.12, s32[1,5,64]{2,1,0:T(8,128)S(1)} %copy.11.map_ref, bf16[512,384]{1,0:T(8,128)(2,1)S(1)} %copy-done), custom_call_target="tpu_custom_call" | custom-call | tf_op jit(solution)/shard_map/pallas_call | solution.py:358
  4.6 5.1 %collective-permute-start.5 = (bf16[336,128]{1,0:T(8,128)(2,1)S(1)}, bf16[336,128]{1,0:T(8,128)(2,1)S(1)}, u32[]{:S(2)}, u32[]{:S(2)}) collective-permute-start(bf16[336,128]{1,0:T(8,128)(2,1)S(1)} %get-tuple-element.15.refs_0_.refs_8_), channel_id=1, source_target_pairs={{0,6},{2,4},{4,2},{6,0},{1,7},{3,5},{5,3},{7,1},{8,14},{10,12},{12... | collective-permute-start | bytes 258056 | tf_op jit(solution)/shard_map/ppermute | solution.py:378
  9.8 0.0 collective-permute-start.3
  9.8 0.6 %collective-permute-start.1 = (bf16[336,128]{1,0:T(8,128)(2,1)S(1)}, bf16[336,128]{1,0:T(8,128)(2,1)S(1)}, u32[]{:S(2)}, u32[]{:S(2)}) collective-permute-start(bf16[336,128]{1,0:T(8,128)(2,1)S(1)} %get-tuple-element.15.refs_0_.refs_8_), channel_id=1, source_target_pairs={{0,2},{2,0},{4,6},{6,4},{1,3},{3,1},{5,7},{7,5},{8,10},{10,8},{12,... | collective-permute-start | bytes 258056 | tf_op jit(solution)/shard_map/ppermute | solution.py:378
  10.4 0.0 collective-permute-start
  10.4 2.5 %collective-permute-done.5.refs_6_ = bf16[336,128]{1,0:T(8,128)(2,1)S(1)} collective-permute-done((bf16[336,128]{1,0:T(8,128)(2,1)S(1)}, bf16[336,128]{1,0:T(8,128)(2,1)S(1)}, u32[]{:S(2)}, u32[]{:S(2)}) %collective-permute-start.5) | collective-permute-done | bytes 86048 | tf_op jit(solution)/shard_map/ppermute | solution.py:378
  12.9 0.0 collective-permute-start.6
  12.9 4.0 %collective-permute-done.3.refs_4_ = bf16[336,128]{1,0:T(8,128)(2,1)S(1)} collective-permute-done((bf16[336,128]{1,0:T(8,128)(2,1)S(1)}, bf16[336,128]{1,0:T(8,128)(2,1)S(1)}, u32[]{:S(2)}, u32[]{:S(2)}) %collective-permute-start.3) | collective-permute-done | bytes 86048 | tf_op jit(solution)/shard_map/ppermute | solution.py:378
  17.0 0.0 collective-permute-start.4
  17.0 0.0 collective-permute-done.1.refs_2_
  17.0 0.5 collective-permute-start.2
  17.5 0.0 collective-permute-start.7
  17.5 1.0 %copy-done.1 = bf16[512,384]{1,0:T(8,128)(2,1)S(1)} copy-done((bf16[512,384]{1,0:T(8,128)(2,1)S(1)}, bf16[512,384]{1,0:T(8,128)(2,1)}, u32[]{:S(2)}) %copy-start.1) | copy-done | bytes 393240
  18.5 1.0 %copy-done.5 = bf16[3,32,5,512]{3,1,2,0:T(8,128)(2,1)S(1)} copy-done((bf16[3,32,5,512]{3,1,2,0:T(8,128)(2,1)S(1)}, bf16[3,32,5,512]{3,1,2,0:T(8,128)(2,1)}, u32[]{:S(2)}) %copy-start.5) | copy-done | bytes 491544
  19.5 1.4 %shard_map.101.state_ref.refs_10_ = bf16[3,320,256]{2,1,0:T(8,128)(2,1)S(1)} custom-call(bf16[3,5,32,512]{3,2,1,0:T(8,128)(2,1)S(1)} %bitcast.5, bf16[192,256]{1,0:T(8,128)(2,1)S(1)} %get-tuple-element.17.hot_ref.refs_11_, bf16[512,384]{1,0:T(8,128)(2,1)S(1)} %copy-done.1), custom_call_target="tpu_custom_call" | custom-call | tf_op jit(solution)/shard_map/pallas_call | solution.py:358
  20.9 0.0 collective-permute-done.7.near_ref
  20.9 0.0 copy-start.3
  20.9 1.4 %copy-done.3 = bf16[3,512,512]{2,1,0:T(8,128)(2,1)S(1)} copy-done((bf16[3,512,512]{2,1,0:T(8,128)(2,1)S(1)}, bf16[3,512,512]{2,1,0:T(8,128)(2,1)}, u32[]{:S(2)}) %copy-start.3) | copy-done | bytes 1572888
  22.3 1.4 %shard_map.102.refs_9_ = f32[5,32,512]{2,1,0:T(8,128)S(1)} custom-call(f32[5,32,512]{2,1,0:T(8,128)S(1)} %bitcast.10, bf16[3,5,32,512]{3,2,1,0:T(8,128)(2,1)S(1)} %bitcast.6, bf16[3,512,512]{2,1,0:T(8,128)(2,1)S(1)} %copy-done.3, f32[1,32]{1,0:T(1,128)S(1)} %bitcast.11, bf16[320,128]{1,0:T(8,128)(2,1)S(1)} %get-tuple-element.16.own_ref, ...), custom_call_target="tpu_custom_call" | custom-call | tf_op jit(solution)/shard_map/pallas_call | solution.py:358
  23.7 0.0 copy-start.4
  23.7 0.0 collective-permute-done.refs_1_
  23.8 0.0 collective-permute-done.6.refs_7_
  23.8 0.0 collective-permute-done.4.refs_5_
  23.8 0.0 collective-permute-done.2.refs_3_
  23.8 2.3 %shard_map.103 = (s32[16,128]{1,0:T(8,128)S(1)}, f32[5,32,512]{2,1,0:T(8,128)S(1)}, bf16[320,128]{1,0:T(8,128)(2,1)S(1)}, bf16[320,128]{1,0:T(8,128)(2,1)S(1)}) custom-call(bf16[336,128]{1,0:T(8,128)(2,1)S(1)} %get-tuple-element.15.refs_0_.refs_8_, bf16[336,128]{1,0:T(8,128)(2,1)S(1)} %collective-permute-done.refs_1_, ...), custom_call_target="tpu_custom_call" | custom-call | tf_op jit(solution)/shard_map/pallas_call | solution.py:358
  26.1 2.7 %collective-permute-start.13 = (bf16[320,128]{1,0:T(8,128)(2,1)S(1)}, bf16[320,128]{1,0:T(8,128)(2,1)S(1)}, u32[]{:S(2)}, u32[]{:S(2)}) collective-permute-start(bf16[320,128]{1,0:T(8,128)(2,1)S(1)} %get-tuple-element.18.refs_0_.refs_8_), channel_id=1, source_target_pairs={{0,6},{2,4},{4,2},{6,0},{1,7},{3,5},{5,3},{7,1},{8,14},{10,12},{12... | collective-permute-start | bytes 245768 | tf_op jit(solution)/shard_map/ppermute | solution.py:378
  28.8 0.0 collective-permute-start.11
  28.8 1.7 %collective-permute-start.9 = (bf16[320,128]{1,0:T(8,128)(2,1)S(1)}, bf16[320,128]{1,0:T(8,128)(2,1)S(1)}, u32[]{:S(2)}, u32[]{:S(2)}) collective-permute-start(bf16[320,128]{1,0:T(8,128)(2,1)S(1)} %get-tuple-element.18.refs_0_.refs_8_), channel_id=1, source_target_pairs={{0,2},{2,0},{4,6},{6,4},{1,3},{3,1},{5,7},{7,5},{8,10},{10,8},{12,... | collective-permute-start | bytes 245768 | tf_op jit(solution)/shard_map/ppermute | solution.py:378
  30.6 0.0 collective-permute-start.8
  30.6 0.5 collective-permute-start.15
  31.1 2.3 %collective-permute-done.13.refs_6_ = bf16[320,128]{1,0:T(8,128)(2,1)S(1)} collective-permute-done((bf16[320,128]{1,0:T(8,128)(2,1)S(1)}, bf16[320,128]{1,0:T(8,128)(2,1)S(1)}, u32[]{:S(2)}, u32[]{:S(2)}) %collective-permute-start.13) | collective-permute-done | bytes 81952 | tf_op jit(solution)/shard_map/ppermute | solution.py:378
  33.4 0.0 collective-permute-start.14
  33.4 3.0 %collective-permute-done.11.refs_4_ = bf16[320,128]{1,0:T(8,128)(2,1)S(1)} collective-permute-done((bf16[320,128]{1,0:T(8,128)(2,1)S(1)}, bf16[320,128]{1,0:T(8,128)(2,1)S(1)}, u32[]{:S(2)}, u32[]{:S(2)}) %collective-permute-start.11) | collective-permute-done | bytes 81952 | tf_op jit(solution)/shard_map/ppermute | solution.py:378
  36.3 0.0 collective-permute-start.12
  36.4 0.0 collective-permute-done.9.refs_2_
  36.4 0.5 collective-permute-start.10
  36.9 0.0 collective-permute-done.15.near_ref
  36.9 1.4 %shard_map.104.refs_9_ = f32[5,32,512]{2,1,0:T(8,128)S(1)} custom-call(f32[5,32,512]{2,1,0:T(8,128)S(1)} %get-tuple-element.19.lam_ref, bf16[3,5,32,512]{3,2,1,0:T(8,128)(2,1)S(1)} %bitcast.7, bf16[3,512,512]{2,1,0:T(8,128)(2,1)S(1)} %copy-done.4, f32[1,32]{1,0:T(1,128)S(1)} %bitcast.13, bf16[320,128]{1,0:T(8,128)(2,1)S(1)} %get-tuple-element.20.own_ref, ...), custom_call_target="tpu_custom_call" | custom-call | tf_op jit(solution)/shard_map/pallas_call | solution.py:358
  38.3 0.0 collective-permute-done.8.refs_1_
  38.3 0.0 collective-permute-done.14.refs_7_
  38.3 0.0 collective-permute-done.12.refs_5_
  38.4 0.0 collective-permute-done.10.refs_3_
  38.4 2.2 %shard_map.105 = (f32[5,32,512]{2,1,0:T(8,128)S(1)}, bf16[320,128]{1,0:T(8,128)(2,1)S(1)}, bf16[320,128]{1,0:T(8,128)(2,1)S(1)}) custom-call(bf16[320,128]{1,0:T(8,128)(2,1)S(1)} %get-tuple-element.18.refs_0_.refs_8_, bf16[320,128]{1,0:T(8,128)(2,1)S(1)} %collective-permute-done.8.refs_1_, bf16[320,128]{1,0:T(8,128)(2,1)S(1)} %collective-permute-done.9.refs_2_, ...), custom_call_target="tpu_custom_call" | custom-call | tf_op jit(solution)/shard_map/pallas_call | solution.py:358
  40.5 2.7 %collective-permute-start.21 = (bf16[320,128]{1,0:T(8,128)(2,1)S(1)}, bf16[320,128]{1,0:T(8,128)(2,1)S(1)}, u32[]{:S(2)}, u32[]{:S(2)}) collective-permute-start(bf16[320,128]{1,0:T(8,128)(2,1)S(1)} %get-tuple-element.22.refs_0_.refs_8_), channel_id=1, source_target_pairs={{0,6},{2,4},{4,2},{6,0},{1,7},{3,5},{5,3},{7,1},{8,14},{10,12},{12... | collective-permute-start | bytes 245768 | tf_op jit(solution)/shard_map/ppermute | solution.py:378
  43.3 0.0 collective-permute-start.19
  43.3 1.7 %collective-permute-start.17 = (bf16[320,128]{1,0:T(8,128)(2,1)S(1)}, bf16[320,128]{1,0:T(8,128)(2,1)S(1)}, u32[]{:S(2)}, u32[]{:S(2)}) collective-permute-start(bf16[320,128]{1,0:T(8,128)(2,1)S(1)} %get-tuple-element.22.refs_0_.refs_8_), channel_id=1, source_target_pairs={{0,2},{2,0},{4,6},{6,4},{1,3},{3,1},{5,7},{7,5},{8,10},{10,8},{12,... | collective-permute-start | bytes 245768 | tf_op jit(solution)/shard_map/ppermute | solution.py:378
  45.0 0.0 collective-permute-start.16
  45.0 0.5 collective-permute-start.23
  45.5 2.3 %collective-permute-done.21.refs_6_ = bf16[320,128]{1,0:T(8,128)(2,1)S(1)} collective-permute-done((bf16[320,128]{1,0:T(8,128)(2,1)S(1)}, bf16[320,128]{1,0:T(8,128)(2,1)S(1)}, u32[]{:S(2)}, u32[]{:S(2)}) %collective-permute-start.21) | collective-permute-done | bytes 81952 | tf_op jit(solution)/shard_map/ppermute | solution.py:378
  47.8 0.0 collective-permute-start.22
  47.8 2.8 %collective-permute-done.19.refs_4_ = bf16[320,128]{1,0:T(8,128)(2,1)S(1)} collective-permute-done((bf16[320,128]{1,0:T(8,128)(2,1)S(1)}, bf16[320,128]{1,0:T(8,128)(2,1)S(1)}, u32[]{:S(2)}, u32[]{:S(2)}) %collective-permute-start.19) | collective-permute-done | bytes 81952 | tf_op jit(solution)/shard_map/ppermute | solution.py:378
  50.5 0.0 collective-permute-start.20
  50.5 0.0 collective-permute-done.17.refs_2_
  50.5 0.5 collective-permute-start.18
  51.1 0.0 collective-permute-done.23.near_ref
  51.1 1.4 %shard_map.106.refs_9_ = f32[5,32,512]{2,1,0:T(8,128)S(1)} custom-call(f32[5,32,512]{2,1,0:T(8,128)S(1)} %get-tuple-element.23.lam_ref, bf16[3,5,32,512]{3,2,1,0:T(8,128)(2,1)S(1)} %bitcast.8, bf16[3,512,512]{2,1,0:T(8,128)(2,1)S(1)} %copy-done.4, f32[1,32]{1,0:T(1,128)S(1)} %bitcast.15, bf16[320,128]{1,0:T(8,128)(2,1)S(1)} %get-tuple-element.24.own_ref, ...), custom_call_target="tpu_custom_call" | custom-call | tf_op jit(solution)/shard_map/pallas_call | solution.py:358
  52.5 0.0 collective-permute-done.16.refs_1_
  52.5 0.0 collective-permute-done.20.refs_5_
  52.5 2.4 %shard_map.107 = f32[5,32,512]{2,1,0:T(8,128)} custom-call(bf16[320,128]{1,0:T(8,128)(2,1)S(1)} %get-tuple-element.22.refs_0_.refs_8_, bf16[320,128]{1,0:T(8,128)(2,1)S(1)} %collective-permute-done.16.refs_1_, bf16[320,128]{1,0:T(8,128)(2,1)S(1)} %collective-permute-done.17.refs_2_, bf16[320,128]{1,0:T(8,128)(2,1)S(1)} %collective-permute-done.18.refs_3_, ...), custom_call_target="tpu_custom_call" | custom-call | tf_op jit(solution)/shard_map/pallas_call | solution.py:358
  (22 shorter events, 0.0 us)
Async XLA Ops:
  0.0 20.9 %copy-start.11 = (f32[32]{0:T(128)S(1)}, f32[32]{0:T(128)}, u32[]{:S(2)}) copy-start(f32[32]{0:T(128)} %param.12) | copy-start | bytes 388
  0.7 1.0 %copy-start = (bf16[512,384]{1,0:T(8,128)(2,1)S(1)}, bf16[512,384]{1,0:T(8,128)(2,1)}, u32[]{:S(2)}) copy-start(bf16[512,384]{1,0:T(8,128)(2,1)} %constant.18.clone.table_ref.refs_12_) | copy-start | bytes 1179652
  1.7 1.0 %copy-start.7 = (f32[32,5,512]{2,0,1:T(8,128)S(1)}, f32[32,5,512]{2,0,1:T(8,128)}, u32[]{:S(2)}) copy-start(f32[32,5,512]{2,0,1:T(8,128)} %param.10) | copy-start | bytes 983044
  2.7 0.7 %copy-start.12 = (s32[1,2,16]{2,1,0:T(2,128)S(1)}, s32[1,2,16]{2,1,0:T(2,128)}, u32[]{:S(2)}) copy-start(s32[1,2,16]{2,1,0:T(2,128)} %conf_ref.1) | copy-start | bytes 388
  3.3 0.7 %copy-start.13 = (s32[1,128]{1,0:T(1,128)S(1)}, s32[1,128]{1,0:T(1,128)}, u32[]{:S(2)}) copy-start(s32[1,128]{1,0:T(1,128)} %send_ref.1) | copy-start | bytes 1540
  4.0 16.9 %copy-start.2 = (bf16[512,384]{1,0:T(8,128)(2,1)S(1)}, bf16[512,384]{1,0:T(8,128)(2,1)}, u32[]{:S(2)}) copy-start(bf16[512,384]{1,0:T(8,128)(2,1)} %constant.18.clone.table_ref.refs_12_) | copy-start | bytes 1179652
  4.0 16.9 %copy-start.8 = (f32[32,5,512]{2,0,1:T(8,128)S(1)}, f32[32,5,512]{2,0,1:T(8,128)}, u32[]{:S(2)}) copy-start(f32[32,5,512]{2,0,1:T(8,128)} %param.10) | copy-start | bytes 983044
  4.6 8.3 %collective-permute-start.5 = (bf16[336,128]{1,0:T(8,128)(2,1)S(1)}, bf16[336,128]{1,0:T(8,128)(2,1)S(1)}, u32[]{:S(2)}, u32[]{:S(2)}) collective-permute-start(bf16[336,128]{1,0:T(8,128)(2,1)S(1)} %get-tuple-element.15.refs_0_.refs_8_), channel_id=1, source_target_pairs={{0,6},{2,4},{4,2},{6,0},{1,7},{3,5},{5,3},{7,1},{8,14},{10,12},{12... | collective-permute-start | bytes 258056 | tf_op jit(solution)/shard_map/ppermute | solution.py:378
  9.8 7.2 %collective-permute-start.3 = (bf16[336,128]{1,0:T(8,128)(2,1)S(1)}, bf16[336,128]{1,0:T(8,128)(2,1)S(1)}, u32[]{:S(2)}, u32[]{:S(2)}) collective-permute-start(bf16[336,128]{1,0:T(8,128)(2,1)S(1)} %get-tuple-element.15.refs_0_.refs_8_), channel_id=1, source_target_pairs={{0,4},{2,6},{4,0},{6,2},{1,5},{3,7},{5,1},{7,3},{8,12},{10,14},{12... | collective-permute-start | bytes 258056 | tf_op jit(solution)/shard_map/ppermute | solution.py:378
  9.8 7.2 %collective-permute-start.1 = (bf16[336,128]{1,0:T(8,128)(2,1)S(1)}, bf16[336,128]{1,0:T(8,128)(2,1)S(1)}, u32[]{:S(2)}, u32[]{:S(2)}) collective-permute-start(bf16[336,128]{1,0:T(8,128)(2,1)S(1)} %get-tuple-element.15.refs_0_.refs_8_), channel_id=1, source_target_pairs={{0,2},{2,0},{4,6},{6,4},{1,3},{3,1},{5,7},{7,5},{8,10},{10,8},{12,... | collective-permute-start | bytes 258056 | tf_op jit(solution)/shard_map/ppermute | solution.py:378
  10.4 13.4 %collective-permute-start = (bf16[336,128]{1,0:T(8,128)(2,1)S(1)}, bf16[336,128]{1,0:T(8,128)(2,1)S(1)}, u32[]{:S(2)}, u32[]{:S(2)}) collective-permute-start(bf16[336,128]{1,0:T(8,128)(2,1)S(1)} %get-tuple-element.15.refs_0_.refs_8_), channel_id=1, source_target_pairs={{0,1},{1,0},{2,3},{3,2},{4,5},{5,4},{6,7},{7,6},{8,9},{9,8},{10,11... | collective-permute-start | bytes 258056 | tf_op jit(solution)/shard_map/ppermute | solution.py:379
  12.9 10.8 %collective-permute-start.6 = (bf16[336,128]{1,0:T(8,128)(2,1)S(1)}, bf16[336,128]{1,0:T(8,128)(2,1)S(1)}, u32[]{:S(2)}, u32[]{:S(2)}) collective-permute-start(bf16[336,128]{1,0:T(8,128)(2,1)S(1)} %collective-permute-done.5.refs_6_), channel_id=1, source_target_pairs={{0,1},{1,0},{2,3},{3,2},{4,5},{5,4},{6,7},{7,6},{8,9},{9,8},{10,11... | collective-permute-start | bytes 258056 | tf_op jit(solution)/shard_map/ppermute | solution.py:379
  17.0 6.8 %collective-permute-start.4 = (bf16[336,128]{1,0:T(8,128)(2,1)S(1)}, bf16[336,128]{1,0:T(8,128)(2,1)S(1)}, u32[]{:S(2)}, u32[]{:S(2)}) collective-permute-start(bf16[336,128]{1,0:T(8,128)(2,1)S(1)} %collective-permute-done.3.refs_4_), channel_id=1, source_target_pairs={{0,1},{1,0},{2,3},{3,2},{4,5},{5,4},{6,7},{7,6},{8,9},{9,8},{10,11... | collective-permute-start | bytes 258056 | tf_op jit(solution)/shard_map/ppermute | solution.py:379
  17.0 6.8 %collective-permute-start.2 = (bf16[336,128]{1,0:T(8,128)(2,1)S(1)}, bf16[336,128]{1,0:T(8,128)(2,1)S(1)}, u32[]{:S(2)}, u32[]{:S(2)}) collective-permute-start(bf16[336,128]{1,0:T(8,128)(2,1)S(1)} %collective-permute-done.1.refs_2_), channel_id=1, source_target_pairs={{0,1},{1,0},{2,3},{3,2},{4,5},{5,4},{6,7},{7,6},{8,9},{9,8},{10,11... | collective-permute-start | bytes 258056 | tf_op jit(solution)/shard_map/ppermute | solution.py:379
  17.5 3.4 %collective-permute-start.7 = (bf16[320,128]{1,0:T(8,128)(2,1)S(1)}, bf16[320,128]{1,0:T(8,128)(2,1)S(1)}, u32[]{:S(2)}, u32[]{:S(2)}) collective-permute-start(bf16[320,128]{1,0:T(8,128)(2,1)S(1)} %get-tuple-element.16.own_ref), channel_id=1, source_target_pairs={{0,1},{1,0},{2,3},{3,2},{4,5},{5,4},{6,7},{7,6},{8,9},{9,8},{10,11... | collective-permute-start | bytes 245768 | tf_op jit(solution)/shard_map/ppermute | solution.py:388
  17.5 1.0 %copy-start.1 = (bf16[512,384]{1,0:T(8,128)(2,1)S(1)}, bf16[512,384]{1,0:T(8,128)(2,1)}, u32[]{:S(2)}) copy-start(bf16[512,384]{1,0:T(8,128)(2,1)} %constant.18.clone.table_ref.refs_12_) | copy-start | bytes 1179652
  18.5 1.0 %copy-start.5 = (bf16[3,32,5,512]{3,1,2,0:T(8,128)(2,1)S(1)}, bf16[3,32,5,512]{3,1,2,0:T(8,128)(2,1)}, u32[]{:S(2)}) copy-start(bf16[3,32,5,512]{3,1,2,0:T(8,128)(2,1)} %param.11) | copy-start | bytes 1474564
  19.5 1.4 %copy-start.6 = (bf16[3,32,5,512]{3,1,2,0:T(8,128)(2,1)S(1)}, bf16[3,32,5,512]{3,1,2,0:T(8,128)(2,1)}, u32[]{:S(2)}) copy-start(bf16[3,32,5,512]{3,1,2,0:T(8,128)(2,1)} %param.11) | copy-start | bytes 1474564
  20.9 1.4 %copy-start.3 = (bf16[3,512,512]{2,1,0:T(8,128)(2,1)S(1)}, bf16[3,512,512]{2,1,0:T(8,128)(2,1)}, u32[]{:S(2)}) copy-start(bf16[3,512,512]{2,1,0:T(8,128)(2,1)} %stiff_ref.5) | copy-start | bytes 4718596
  22.3 1.5 %copy-start.9 = (bf16[256,192]{1,0:T(8,128)(2,1)S(1)}, bf16[256,192]{1,0:T(8,128)(2,1)}, u32[]{:S(2)}) copy-start(bf16[256,192]{1,0:T(8,128)(2,1)} %constant.20.clone.refs_15_) | copy-start | bytes 294916
  22.3 1.5 %copy-start.10 = (bf16[256,128]{1,0:T(8,128)(2,1)S(1)}, bf16[256,128]{1,0:T(8,128)(2,1)}, u32[]{:S(2)}) copy-start(bf16[256,128]{1,0:T(8,128)(2,1)} %constant.19.clone.refs_14_) | copy-start | bytes 196612
  23.7 13.1 %copy-start.4 = (bf16[3,512,512]{2,1,0:T(8,128)(2,1)S(1)}, bf16[3,512,512]{2,1,0:T(8,128)(2,1)}, u32[]{:S(2)}) copy-start(bf16[3,512,512]{2,1,0:T(8,128)(2,1)} %stiff_ref.5) | copy-start | bytes 4718596
  26.1 7.3 %collective-permute-start.13 = (bf16[320,128]{1,0:T(8,128)(2,1)S(1)}, bf16[320,128]{1,0:T(8,128)(2,1)S(1)}, u32[]{:S(2)}, u32[]{:S(2)}) collective-permute-start(bf16[320,128]{1,0:T(8,128)(2,1)S(1)} %get-tuple-element.18.refs_0_.refs_8_), channel_id=1, source_target_pairs={{0,6},{2,4},{4,2},{6,0},{1,7},{3,5},{5,3},{7,1},{8,14},{10,12},{12... | collective-permute-start | bytes 245768 | tf_op jit(solution)/shard_map/ppermute | solution.py:378
  28.8 7.5 %collective-permute-start.11 = (bf16[320,128]{1,0:T(8,128)(2,1)S(1)}, bf16[320,128]{1,0:T(8,128)(2,1)S(1)}, u32[]{:S(2)}, u32[]{:S(2)}) collective-permute-start(bf16[320,128]{1,0:T(8,128)(2,1)S(1)} %get-tuple-element.18.refs_0_.refs_8_), channel_id=1, source_target_pairs={{0,4},{2,6},{4,0},{6,2},{1,5},{3,7},{5,1},{7,3},{8,12},{10,14},{12... | collective-permute-start | bytes 245768 | tf_op jit(solution)/shard_map/ppermute | solution.py:378
  28.8 7.6 %collective-permute-start.9 = (bf16[320,128]{1,0:T(8,128)(2,1)S(1)}, bf16[320,128]{1,0:T(8,128)(2,1)S(1)}, u32[]{:S(2)}, u32[]{:S(2)}) collective-permute-start(bf16[320,128]{1,0:T(8,128)(2,1)S(1)} %get-tuple-element.18.refs_0_.refs_8_), channel_id=1, source_target_pairs={{0,2},{2,0},{4,6},{6,4},{1,3},{3,1},{5,7},{7,5},{8,10},{10,8},{12,... | collective-permute-start | bytes 245768 | tf_op jit(solution)/shard_map/ppermute | solution.py:378
  30.6 7.8 %collective-permute-start.8 = (bf16[320,128]{1,0:T(8,128)(2,1)S(1)}, bf16[320,128]{1,0:T(8,128)(2,1)S(1)}, u32[]{:S(2)}, u32[]{:S(2)}) collective-permute-start(bf16[320,128]{1,0:T(8,128)(2,1)S(1)} %get-tuple-element.18.refs_0_.refs_8_), channel_id=1, source_target_pairs={{0,1},{1,0},{2,3},{3,2},{4,5},{5,4},{6,7},{7,6},{8,9},{9,8},{10,11... | collective-permute-start | bytes 245768 | tf_op jit(solution)/shard_map/ppermute | solution.py:379
  30.6 6.3 %collective-permute-start.15 = (bf16[320,128]{1,0:T(8,128)(2,1)S(1)}, bf16[320,128]{1,0:T(8,128)(2,1)S(1)}, u32[]{:S(2)}, u32[]{:S(2)}) collective-permute-start(bf16[320,128]{1,0:T(8,128)(2,1)S(1)} %get-tuple-element.20.own_ref), channel_id=1, source_target_pairs={{0,1},{1,0},{2,3},{3,2},{4,5},{5,4},{6,7},{7,6},{8,9},{9,8},{10,11... | collective-permute-start | bytes 245768 | tf_op jit(solution)/shard_map/ppermute | solution.py:388
  33.4 5.0 %collective-permute-start.14 = (bf16[320,128]{1,0:T(8,128)(2,1)S(1)}, bf16[320,128]{1,0:T(8,128)(2,1)S(1)}, u32[]{:S(2)}, u32[]{:S(2)}) collective-permute-start(bf16[320,128]{1,0:T(8,128)(2,1)S(1)} %collective-permute-done.13.refs_6_), channel_id=1, source_target_pairs={{0,1},{1,0},{2,3},{3,2},{4,5},{5,4},{6,7},{7,6},{8,9},{9,8},{10,11... | collective-permute-start | bytes 245768 | tf_op jit(solution)/shard_map/ppermute | solution.py:379
  36.3 2.0 %collective-permute-start.12 = (bf16[320,128]{1,0:T(8,128)(2,1)S(1)}, bf16[320,128]{1,0:T(8,128)(2,1)S(1)}, u32[]{:S(2)}, u32[]{:S(2)}) collective-permute-start(bf16[320,128]{1,0:T(8,128)(2,1)S(1)} %collective-permute-done.11.refs_4_), channel_id=1, source_target_pairs={{0,1},{1,0},{2,3},{3,2},{4,5},{5,4},{6,7},{7,6},{8,9},{9,8},{10,11... | collective-permute-start | bytes 245768 | tf_op jit(solution)/shard_map/ppermute | solution.py:379
  36.4 2.0 %collective-permute-start.10 = (bf16[320,128]{1,0:T(8,128)(2,1)S(1)}, bf16[320,128]{1,0:T(8,128)(2,1)S(1)}, u32[]{:S(2)}, u32[]{:S(2)}) collective-permute-start(bf16[320,128]{1,0:T(8,128)(2,1)S(1)} %collective-permute-done.9.refs_2_), channel_id=1, source_target_pairs={{0,1},{1,0},{2,3},{3,2},{4,5},{5,4},{6,7},{7,6},{8,9},{9,8},{10,11... | collective-permute-start | bytes 245768 | tf_op jit(solution)/shard_map/ppermute | solution.py:379
  40.5 7.2 %collective-permute-start.21 = (bf16[320,128]{1,0:T(8,128)(2,1)S(1)}, bf16[320,128]{1,0:T(8,128)(2,1)S(1)}, u32[]{:S(2)}, u32[]{:S(2)}) collective-permute-start(bf16[320,128]{1,0:T(8,128)(2,1)S(1)} %get-tuple-element.22.refs_0_.refs_8_), channel_id=1, source_target_pairs={{0,6},{2,4},{4,2},{6,0},{1,7},{3,5},{5,3},{7,1},{8,14},{10,12},{12... | collective-permute-start | bytes 245768 | tf_op jit(solution)/shard_map/ppermute | solution.py:378
  43.3 7.3 %collective-permute-start.19 = (bf16[320,128]{1,0:T(8,128)(2,1)S(1)}, bf16[320,128]{1,0:T(8,128)(2,1)S(1)}, u32[]{:S(2)}, u32[]{:S(2)}) collective-permute-start(bf16[320,128]{1,0:T(8,128)(2,1)S(1)} %get-tuple-element.22.refs_0_.refs_8_), channel_id=1, source_target_pairs={{0,4},{2,6},{4,0},{6,2},{1,5},{3,7},{5,1},{7,3},{8,12},{10,14},{12... | collective-permute-start | bytes 245768 | tf_op jit(solution)/shard_map/ppermute | solution.py:378
  43.3 7.3 %collective-permute-start.17 = (bf16[320,128]{1,0:T(8,128)(2,1)S(1)}, bf16[320,128]{1,0:T(8,128)(2,1)S(1)}, u32[]{:S(2)}, u32[]{:S(2)}) collective-permute-start(bf16[320,128]{1,0:T(8,128)(2,1)S(1)} %get-tuple-element.22.refs_0_.refs_8_), channel_id=1, source_target_pairs={{0,2},{2,0},{4,6},{6,4},{1,3},{3,1},{5,7},{7,5},{8,10},{10,8},{12,... | collective-permute-start | bytes 245768 | tf_op jit(solution)/shard_map/ppermute | solution.py:378
  45.0 7.5 %collective-permute-start.16 = (bf16[320,128]{1,0:T(8,128)(2,1)S(1)}, bf16[320,128]{1,0:T(8,128)(2,1)S(1)}, u32[]{:S(2)}, u32[]{:S(2)}) collective-permute-start(bf16[320,128]{1,0:T(8,128)(2,1)S(1)} %get-tuple-element.22.refs_0_.refs_8_), channel_id=1, source_target_pairs={{0,1},{1,0},{2,3},{3,2},{4,5},{5,4},{6,7},{7,6},{8,9},{9,8},{10,11... | collective-permute-start | bytes 245768 | tf_op jit(solution)/shard_map/ppermute | solution.py:379
  45.0 6.1 %collective-permute-start.23 = (bf16[320,128]{1,0:T(8,128)(2,1)S(1)}, bf16[320,128]{1,0:T(8,128)(2,1)S(1)}, u32[]{:S(2)}, u32[]{:S(2)}) collective-permute-start(bf16[320,128]{1,0:T(8,128)(2,1)S(1)} %get-tuple-element.24.own_ref), channel_id=1, source_target_pairs={{0,1},{1,0},{2,3},{3,2},{4,5},{5,4},{6,7},{7,6},{8,9},{9,8},{10,11... | collective-permute-start | bytes 245768 | tf_op jit(solution)/shard_map/ppermute | solution.py:388
  47.8 4.7 %collective-permute-start.22 = (bf16[320,128]{1,0:T(8,128)(2,1)S(1)}, bf16[320,128]{1,0:T(8,128)(2,1)S(1)}, u32[]{:S(2)}, u32[]{:S(2)}) collective-permute-start(bf16[320,128]{1,0:T(8,128)(2,1)S(1)} %collective-permute-done.21.refs_6_), channel_id=1, source_target_pairs={{0,1},{1,0},{2,3},{3,2},{4,5},{5,4},{6,7},{7,6},{8,9},{9,8},{10,11... | collective-permute-start | bytes 245768 | tf_op jit(solution)/shard_map/ppermute | solution.py:379
  50.5 2.0 %collective-permute-start.20 = (bf16[320,128]{1,0:T(8,128)(2,1)S(1)}, bf16[320,128]{1,0:T(8,128)(2,1)S(1)}, u32[]{:S(2)}, u32[]{:S(2)}) collective-permute-start(bf16[320,128]{1,0:T(8,128)(2,1)S(1)} %collective-permute-done.19.refs_4_), channel_id=1, source_target_pairs={{0,1},{1,0},{2,3},{3,2},{4,5},{5,4},{6,7},{7,6},{8,9},{9,8},{10,11... | collective-permute-start | bytes 245768 | tf_op jit(solution)/shard_map/ppermute | solution.py:379
  50.5 2.0 %collective-permute-start.18 = (bf16[320,128]{1,0:T(8,128)(2,1)S(1)}, bf16[320,128]{1,0:T(8,128)(2,1)S(1)}, u32[]{:S(2)}, u32[]{:S(2)}) collective-permute-start(bf16[320,128]{1,0:T(8,128)(2,1)S(1)} %collective-permute-done.17.refs_2_), channel_id=1, source_target_pairs={{0,1},{1,0},{2,3},{3,2},{4,5},{5,4},{6,7},{7,6},{8,9},{9,8},{10,11... | collective-permute-start | bytes 245768 | tf_op jit(solution)/shard_map/ppermute | solution.py:379

commit v2 on v1

--- a/solution.py
+++ b/solution.py
@@ -151,11 +151,22 @@
     return dot(faces, hot, 0, 0).astype(BF16)[:ROWS]
 
 
-def start_kernel(lam_ref, send_ref, conf_ref, map_ref, table_ref, out_ref, shared_ref, hot_ref, ids_ref):
+def fetch(pairs, sems):
+    copies = [pltpu.make_async_copy(a, b, sems.at[i]) for i, (a, b) in enumerate(pairs)]
+    for copy in copies:
+        copy.start()
+    return copies
+
+
+def start_kernel(lam_hbm, send_hbm, conf_hbm, map_hbm, table_hbm, out_ref, shared_ref, hot_ref, lam_ref, table_ref, send_ref, conf_ref, map_ref, ids_ref, sems):
+    pairs = ((send_hbm, send_ref), (conf_hbm, conf_ref), (map_hbm, map_ref), (lam_hbm, lam_ref), (table_hbm, table_ref))
+    copies = fetch(pairs, sems)
     elements = lam_ref.shape[1]
     slots = send_ref.shape[1]
     faces = conf_ref.shape[2]
     ids_ref[...] = jnp.full(ids_ref.shape, -1, jnp.int32)
+    for copy in copies[:3]:
+        copy.wait()
     ids_ref[0:1, 0:slots] = send_ref[...]
     ids_ref[0:1, slots : slots + faces] = conf_ref[0, 0:1]
     ids_ref[0:1, slots + faces : slots + 2 * faces] = conf_ref[0, 1:2]
@@ -165,28 +176,35 @@
     ident = 6 * (row - face * elements) + face
     hot = jnp.where(ident == ids_ref[0:1], 1.0, 0.0).astype(BF16)
     hot_ref[...] = hot
+    rows = [map_ref[k] for k in range(5)]
+    mortars = rows[0].shape[1]
+    slot = lax.broadcasted_iota(jnp.int32, (slots, mortars), 0)
+    field = lax.broadcasted_iota(jnp.int32, (EXTRA, mortars), 0)
+    known = jnp.where(field == 1, rows[2], jnp.where(field == 2, rows[3], jnp.where(field == 3, rows[4], 0)))
+    info = None
+    for mine, other, left in ((0, 1, 1), (1, 0, 0)):
+        hits = jnp.where(slot == rows[mine], 1.0, 0.0).astype(BF16)
+        fields = jnp.where(field == 0, rows[other], jnp.where(field == 4, left, known))
+        part = dot(fields.astype(F32).astype(BF16), hits, 1, 1)
+        info = part if info is None else info + part
+    out_ref[ROWS:] = info.astype(BF16)
+    for copy in copies[3:]:
+        copy.wait()
     lam_low = lam_ref[...].astype(BF16).reshape(5 * elements, ELEM)
     values = slot_values(lam_low, hot, table_ref[...], elements)
     out_ref[0:ROWS] = values[:, :slots]
     shared_ref[...] = values[:, slots:]
-    rows = map_ref[0]
-    mortars = rows.shape[1]
-    slot = lax.broadcasted_iota(jnp.int32, (slots, mortars), 0)
-    field = lax.broadcasted_iota(jnp.int32, (EXTRA, mortars), 0)
-    known = jnp.where(field == 1, rows[2:3], jnp.where(field == 2, rows[3:4], jnp.where(field == 3, rows[4:5], 0)))
-    info = None
-    for mine, other, left in ((0, 1, 1), (1, 0, 0)):
-        hits = jnp.where(slot == rows[mine : mine + 1], 1.0, 0.0).astype(BF16)
-        fields = jnp.where(field == 0, rows[other : other + 1], jnp.where(field == 4, left, known))
-        part = dot(fields.astype(F32).astype(BF16), hits, 1, 1)
-        info = part if info is None else info + part
-    out_ref[ROWS:] = info.astype(BF16)
-
-
-def state_kernel(saved_ref, hot_ref, table_ref, out_ref):
+
+
+def state_kernel(saved_hbm, stiff_hbm, forward_hbm, backward_hbm, hot_ref, table_ref, out_ref, saved_ref, stiff_ref, forward_ref, backward_ref, sems):
+    pairs = ((saved_hbm, saved_ref), (stiff_hbm, stiff_ref), (forward_hbm, forward_ref), (backward_hbm, backward_ref))
+    copies = fetch(pairs, sems)
+    copies[0].wait()
     elements = saved_ref.shape[2]
     for s in range(saved_ref.shape[0]):
         out_ref[s] = slot_values(saved_ref[s].reshape(5 * elements, ELEM), hot_ref[...], table_ref[...], elements)
+    for copy in copies[1:]:
+        copy.wait()
 
 
 def volume_kernel(section, faces, lam_ref, saved_ref, stiff_ref, jac_ref, own_ref, near_ref, state_ref, hot_ref, table_ref, base_ref, slope_ref, smooth_ref):
@@ -291,8 +309,8 @@
     refs = list(refs)
     pieces = [r[...] for r in refs[:count]]
     own_ref = refs[count]
-    base_ref, state_ref, hot_ref, table_ref, jac_ref, forward_ref, backward_ref, me_ref, info_ref = refs[count + 1 : count + 10]
-    outs = refs[count + 10 :]
+    base_ref, state_ref, hot_ref, table_ref, jac_ref, forward_ref, backward_ref, me_ref = refs[count + 1 : count + 9]
+    outs = refs[count + 9 :]
     elements = base_ref.shape[1]
     if len(pieces) == 1 and pieces[0].ndim == 3:
         pieces = [pieces[0][p] for p in range(pieces[0].shape[0])]
@@ -303,7 +321,8 @@
         outs[0][...] = info
         outs = outs[1:]
     else:
-        info = info_ref[...]
+        info = outs[0][...]
+        outs = outs[1:]
     code, child, axis, live, left = (jnp.broadcast_to(info[k : k + 1], (FACE, slots)) for k in range(5))
     row = lax.broadcasted_iota(jnp.int32, (slots, slots), 0)
     partner = None
@@ -351,14 +370,16 @@
         outs[2][...] = values[:, slots:]
 
 
-def call(kernel, outs, args, scratch=(), scalars=(), last=False):
-    specs = [pl.BlockSpec(memory_space=pltpu.SMEM if i in scalars else pltpu.VMEM) for i in range(len(args))]
-    args = [a if i in scalars else pltpu.with_memory_space_constraint(a, pltpu.VMEM) for i, a in enumerate(args)]
+def call(kernel, outs, args, scratch=(), scalars=(), far=0, last=False):
+    def space(i):
+        return pl.ANY if i < far else pltpu.SMEM if i in scalars else pltpu.VMEM
+
+    args = [pltpu.with_memory_space_constraint(a, pltpu.VMEM) if space(i) is pltpu.VMEM else a for i, a in enumerate(args)]
     shapes = [jax.ShapeDtypeStruct(o, t) if last else pltpu.VMEM(o, t) for o, t in outs]
     return pl.pallas_call(
         kernel,
         out_shape=shapes,
-        in_specs=specs,
+        in_specs=[pl.BlockSpec(memory_space=space(i)) for i in range(len(args))],
         out_specs=[pl.BlockSpec(memory_space=pltpu.VMEM)] * len(outs),
         scratch_shapes=list(scratch),
         compiler_params=pltpu.CompilerParams(vmem_limit_bytes=VMEM_GRANT),
@@ -409,14 +430,29 @@
     conforming = ((ROWS, shared), BF16)
     info_shape = ((EXTRA, slots), jnp.int32)
 
-    outgoing, own_shared, hot = call(
+    mortars = jnp.transpose(mortar_table, (1, 0, 2))
+    held = lambda x: (x.shape, x.dtype)
+    outgoing, own_shared, hot, lam, table = call(
         start_kernel,
-        [((ROWS + EXTRA, slots), BF16), conforming, ((6 * elements, slots + shared), BF16)],
-        [lam, send_face, conf_faces, mortar_table, table],
-        scratch=(pltpu.VMEM((8, slots + shared), jnp.int32),),
+        [((ROWS + EXTRA, slots), BF16), conforming, ((6 * elements, slots + shared), BF16), held(lam), held(table)],
+        [lam, send_face, conf_faces, mortars, table],
+        scratch=(
+            pltpu.VMEM(send_face.shape, jnp.int32),
+            pltpu.VMEM(conf_faces.shape, jnp.int32),
+            pltpu.VMEM(mortars.shape, jnp.int32),
+            pltpu.VMEM((8, slots + shared), jnp.int32),
+            pltpu.SemaphoreType.DMA((5,)),
+        ),
+        far=5,
     )
-    (values,) = call(state_kernel, [((sections, ROWS, slots + shared), BF16)], [states, hot, table])
-    info = jnp.zeros(info_shape[0], jnp.int32)
+    values, states, stiffness, forward, backward = call(
+        state_kernel,
+        [((sections, ROWS, slots + shared), BF16), held(states), held(stiffness), held(forward), held(backward)],
+        [states, stiffness, forward, backward, hot, table],
+        scratch=(pltpu.SemaphoreType.DMA((4,)),),
+        far=4,
+    )
+    info = None
     for section in (2, 1, 0):
         pieces, relative = gather_group(outgoing)
         near = neighbours(own_shared, faces)
@@ -428,10 +464,10 @@
         )
         first, last = section == sections - 1, section == 0
         outs = ([info_shape] if first else []) + [rows] + ([] if last else [sent, conforming])
-        args = pieces + [outgoing, base, values, hot, table, jac, forward, backward, me, info]
+        args = pieces + [outgoing, base, values, hot, table, jac, forward, backward, me] + ([] if first else [info])
         out = call(
             functools.partial(mortar_update, section, relative, first, last, len(pieces)),
-            outs, args, scalars=(len(args) - 2,), last=last,
+            outs, args, scalars=(len(pieces) + 8,), last=last,
         )
         if first:
             info, out = out[0], out[1:]

time: 55.3 us -> 57.1 us (1.033)
  Pallas kernels: 13.1 us -> 14.2 us
  local copies, waits for them, and re-layouts: 7.46 us -> 8.17 us
    pallas_call x8, Pallas kernels: 13.1 us -> 14.2 us  [call(): pl.pallas_call(kernel, out_shape=shapes, in_specs=[pl.BlockSpec(memory_sp...]
    unnamed x29 -> x20, local copies, waits for them, and re-layouts: 7.45 us -> 8.17 us
  transfers between devices with their start and end apart: 24 -> 24, of which waited for: 6 -> 6; matrix products, arithmetic and copies ran while one was open for 0% -> 0% of each run, Pallas kernels for 10% -> 11%
where the time goes in v2:
time: 57.1 us; the launch traced here: 56.8 us
  starting transfers between devices  17.3 us (30%)
  waiting for transfers between devices  16.9 us (30%)
  Pallas kernels  14.2 us (25%)
  local copies, waits for them, and re-layouts  8.17 us (14%)
    ppermute x9, waiting for transfers between devices, gather_group(): lax.ppermute(x, 'gy', [(i, i ^ k) for i in range(ny)])  16.9 us
    ppermute x9, starting transfers between devices, gather_group(): lax.ppermute(x, 'gy', [(i, i ^ k) for i in range(ny)])  14.7 us
    pallas_call x8, Pallas kernels, call(): pl.pallas_call(kernel, out_shape=shapes, in_specs=[pl.BlockSpec(memory_sp...  14.2 us
    unnamed x20, local copies, waits for them, and re-layouts  8.17 us
    ppermute x12, starting transfers between devices, gather_group(): pieces += [here, lax.ppermute(here, 'gz', [(0, 1), (1, 0)])]  1.55 us
  transfers between devices with their start and end apart: 24, of which 6 were waited for; matrix products, arithmetic and copies ran while one was open for 0% of the time, Pallas kernels for 11%

profile of v2, /device:TPU:0, one launch (start us, length us, event | category | flops | bytes accessed | tf_op | source)
XLA Modules:
  0.0 56.8 jit_solution(15197184117290429924)
XLA Ops:
  0.0 1.0 %copy-done.2 = bf16[512,384]{1,0:T(8,128)(2,1)S(1)} copy-done((bf16[512,384]{1,0:T(8,128)(2,1)S(1)}, bf16[512,384]{1,0:T(8,128)(2,1)}, u32[]{:S(2)}) %copy-start.2) | copy-done | bytes 393240
  1.0 1.0 %copy-done.3 = f32[32,5,512]{2,0,1:T(8,128)S(1)} copy-done((f32[32,5,512]{2,0,1:T(8,128)S(1)}, f32[32,5,512]{2,0,1:T(8,128)}, u32[]{:S(2)}) %copy-start.3) | copy-done | bytes 327704
  2.0 0.7 %copy-done.7 = s32[1,5,64]{2,0,1:T(1,128)S(1)} copy-done((s32[1,5,64]{2,0,1:T(1,128)S(1)}, s32[1,5,64]{2,0,1:T(1,128)}, u32[]{:S(2)}) %copy-start.7) | copy-done | bytes 1304
  2.7 0.7 %copy-done.8 = s32[1,2,16]{2,1,0:T(2,128)S(1)} copy-done((s32[1,2,16]{2,1,0:T(2,128)S(1)}, s32[1,2,16]{2,1,0:T(2,128)}, u32[]{:S(2)}) %copy-start.8) | copy-done | bytes 152
  3.3 0.7 %copy-done.9 = s32[1,128]{1,0:T(1,128)S(1)} copy-done((s32[1,128]{1,0:T(1,128)S(1)}, s32[1,128]{1,0:T(1,128)}, u32[]{:S(2)}) %copy-start.9) | copy-done | bytes 536
  4.0 1.1 %shard_map.100 = (bf16[336,128]{1,0:T(8,128)(2,1)S(1)}, bf16[320,128]{1,0:T(8,128)(2,1)S(1)}, bf16[192,256]{1,0:T(8,128)(2,1)S(1)}, f32[5,32,512]{2,1,0:T(8,128)S(1)}, bf16[512,384]{1,0:T(8,128)(2,1)S(1)}) custom-call(f32[5,32,512]{2,1,0:T(8,128)S(1)} %bitcast.7, s32[1,128]{1,0:T(1,128)S(1)} %copy-done.9, s32[1,2,16]{2,1,0:T(2,128)S(1)} %copy-done.8, ...), custom_call_target="tpu_custom_call" | custom-call | tf_op jit(solution)/shard_map/pallas_call | solution.py:379
  5.1 0.0 copy-start.6
  5.1 5.1 %collective-permute-start.5 = (bf16[336,128]{1,0:T(8,128)(2,1)S(1)}, bf16[336,128]{1,0:T(8,128)(2,1)S(1)}, u32[]{:S(2)}, u32[]{:S(2)}) collective-permute-start(bf16[336,128]{1,0:T(8,128)(2,1)S(1)} %get-tuple-element.22.refs_0_.refs_8_), channel_id=1, source_target_pairs={{0,6},{2,4},{4,2},{6,0},{1,7},{3,5},{5,3},{7,1},{8,14},{10,12},{12... | collective-permute-start | bytes 258056 | tf_op jit(solution)/shard_map/ppermute | solution.py:399
  10.3 0.0 collective-permute-start.3
  10.3 0.6 %collective-permute-start.1 = (bf16[336,128]{1,0:T(8,128)(2,1)S(1)}, bf16[336,128]{1,0:T(8,128)(2,1)S(1)}, u32[]{:S(2)}, u32[]{:S(2)}) collective-permute-start(bf16[336,128]{1,0:T(8,128)(2,1)S(1)} %get-tuple-element.22.refs_0_.refs_8_), channel_id=1, source_target_pairs={{0,2},{2,0},{4,6},{6,4},{1,3},{3,1},{5,7},{7,5},{8,10},{10,8},{12,... | collective-permute-start | bytes 258056 | tf_op jit(solution)/shard_map/ppermute | solution.py:399
  10.9 0.0 collective-permute-start
  10.9 2.5 %collective-permute-done.5.refs_6_ = bf16[336,128]{1,0:T(8,128)(2,1)S(1)} collective-permute-done((bf16[336,128]{1,0:T(8,128)(2,1)S(1)}, bf16[336,128]{1,0:T(8,128)(2,1)S(1)}, u32[]{:S(2)}, u32[]{:S(2)}) %collective-permute-start.5) | collective-permute-done | bytes 86048 | tf_op jit(solution)/shard_map/ppermute | solution.py:399
  13.4 0.0 collective-permute-start.6
  13.4 4.0 %collective-permute-done.3.refs_4_ = bf16[336,128]{1,0:T(8,128)(2,1)S(1)} collective-permute-done((bf16[336,128]{1,0:T(8,128)(2,1)S(1)}, bf16[336,128]{1,0:T(8,128)(2,1)S(1)}, u32[]{:S(2)}, u32[]{:S(2)}) %collective-permute-start.3) | collective-permute-done | bytes 86048 | tf_op jit(solution)/shard_map/ppermute | solution.py:399
  17.5 0.0 collective-permute-start.4
  17.5 0.0 collective-permute-done.1.refs_2_
  17.5 0.5 collective-permute-start.2
  18.0 0.0 collective-permute-start.7
  18.0 1.4 %copy-done = bf16[3,512,512]{2,1,0:T(8,128)(2,1)S(1)} copy-done((bf16[3,512,512]{2,1,0:T(8,128)(2,1)S(1)}, bf16[3,512,512]{2,1,0:T(8,128)(2,1)}, u32[]{:S(2)}) %copy-start) | copy-done | bytes 1572888
  19.4 1.0 %copy-done.1 = bf16[3,32,5,512]{3,1,2,0:T(8,128)(2,1)S(1)} copy-done((bf16[3,32,5,512]{3,1,2,0:T(8,128)(2,1)S(1)}, bf16[3,32,5,512]{3,1,2,0:T(8,128)(2,1)}, u32[]{:S(2)}) %copy-start.1) | copy-done | bytes 491544
  20.4 0.9 %copy-done.4 = bf16[256,192]{1,0:T(8,128)(2,1)S(1)} copy-done((bf16[256,192]{1,0:T(8,128)(2,1)S(1)}, bf16[256,192]{1,0:T(8,128)(2,1)}, u32[]{:S(2)}) %copy-start.4) | copy-done | bytes 98328
  21.3 0.8 %copy-done.5 = bf16[256,128]{1,0:T(8,128)(2,1)S(1)} copy-done((bf16[256,128]{1,0:T(8,128)(2,1)S(1)}, bf16[256,128]{1,0:T(8,128)(2,1)}, u32[]{:S(2)}) %copy-start.5) | copy-done | bytes 65560
  22.2 2.1 %shard_map.101 = (bf16[3,320,256]{2,1,0:T(8,128)(2,1)S(1)}, bf16[3,5,32,512]{3,2,1,0:T(8,128)(2,1)S(1)}, bf16[3,512,512]{2,1,0:T(8,128)(2,1)S(1)}, bf16[256,128]{1,0:T(8,128)(2,1)S(1)}, bf16[256,192]{1,0:T(8,128)(2,1)S(1)}) custom-call(bf16[3,5,32,512]{3,2,1,0:T(8,128)(2,1)S(1)} %bitcast.6, bf16[3,512,512]{2,1,0:T(8,128)(2,1)S(1)} %copy-done, ...), custom_call_target="tpu_custom_call" | custom-call | tf_op jit(solution)/shard_map/pallas_call | solution.py:379
  24.3 0.0 collective-permute-done.7.near_ref
  24.3 1.4 %shard_map.102.refs_9_ = f32[5,32,512]{2,1,0:T(8,128)S(1)} custom-call(f32[5,32,512]{2,1,0:T(8,128)S(1)} %get-tuple-element.23.lam_ref, bf16[3,5,32,512]{3,2,1,0:T(8,128)(2,1)S(1)} %get-tuple-element.26.saved_ref, bf16[3,512,512]{2,1,0:T(8,128)(2,1)S(1)} %get-tuple-element.27.stiff_ref, f32[1,32]{1,0:T(1,128)S(1)} %bitcast.8, ...), custom_call_target="tpu_custom_call" | custom-call | tf_op jit(solution)/shard_map/pallas_call | solution.py:379
  25.7 0.0 collective-permute-done.refs_1_
  25.7 0.0 collective-permute-done.6.refs_7_
  25.7 0.0 collective-permute-done.4.refs_5_
  25.7 0.0 collective-permute-done.2.refs_3_
  25.7 2.3 %shard_map.103 = (s32[16,128]{1,0:T(8,128)S(1)}, f32[5,32,512]{2,1,0:T(8,128)S(1)}, bf16[320,128]{1,0:T(8,128)(2,1)S(1)}, bf16[320,128]{1,0:T(8,128)(2,1)S(1)}) custom-call(bf16[336,128]{1,0:T(8,128)(2,1)S(1)} %get-tuple-element.22.refs_0_.refs_8_, bf16[336,128]{1,0:T(8,128)(2,1)S(1)} %collective-permute-done.refs_1_, ...), custom_call_target="tpu_custom_call" | custom-call | tf_op jit(solution)/shard_map/pallas_call | solution.py:379
  28.0 2.7 %collective-permute-start.13 = (bf16[320,128]{1,0:T(8,128)(2,1)S(1)}, bf16[320,128]{1,0:T(8,128)(2,1)S(1)}, u32[]{:S(2)}, u32[]{:S(2)}) collective-permute-start(bf16[320,128]{1,0:T(8,128)(2,1)S(1)} %get-tuple-element.32.refs_0_.refs_8_), channel_id=1, source_target_pairs={{0,6},{2,4},{4,2},{6,0},{1,7},{3,5},{5,3},{7,1},{8,14},{10,12},{12... | collective-permute-start | bytes 245768 | tf_op jit(solution)/shard_map/ppermute | solution.py:399
  30.7 0.0 collective-permute-start.11
  30.7 1.7 %collective-permute-start.9 = (bf16[320,128]{1,0:T(8,128)(2,1)S(1)}, bf16[320,128]{1,0:T(8,128)(2,1)S(1)}, u32[]{:S(2)}, u32[]{:S(2)}) collective-permute-start(bf16[320,128]{1,0:T(8,128)(2,1)S(1)} %get-tuple-element.32.refs_0_.refs_8_), channel_id=1, source_target_pairs={{0,2},{2,0},{4,6},{6,4},{1,3},{3,1},{5,7},{7,5},{8,10},{10,8},{12,... | collective-permute-start | bytes 245768 | tf_op jit(solution)/shard_map/ppermute | solution.py:399
  32.5 0.0 collective-permute-start.8
  32.5 0.5 collective-permute-start.15
  33.0 2.3 %collective-permute-done.13.refs_6_ = bf16[320,128]{1,0:T(8,128)(2,1)S(1)} collective-permute-done((bf16[320,128]{1,0:T(8,128)(2,1)S(1)}, bf16[320,128]{1,0:T(8,128)(2,1)S(1)}, u32[]{:S(2)}, u32[]{:S(2)}) %collective-permute-start.13) | collective-permute-done | bytes 81952 | tf_op jit(solution)/shard_map/ppermute | solution.py:399
  35.3 0.0 collective-permute-start.14
  35.3 3.0 %collective-permute-done.11.refs_4_ = bf16[320,128]{1,0:T(8,128)(2,1)S(1)} collective-permute-done((bf16[320,128]{1,0:T(8,128)(2,1)S(1)}, bf16[320,128]{1,0:T(8,128)(2,1)S(1)}, u32[]{:S(2)}, u32[]{:S(2)}) %collective-permute-start.11) | collective-permute-done | bytes 81952 | tf_op jit(solution)/shard_map/ppermute | solution.py:399
  38.3 0.0 collective-permute-start.12
  38.3 0.0 collective-permute-done.9.refs_2_
  38.3 0.5 collective-permute-start.10
  38.8 0.0 collective-permute-done.15.near_ref
  38.8 1.4 %shard_map.104.refs_9_ = f32[5,32,512]{2,1,0:T(8,128)S(1)} custom-call(f32[5,32,512]{2,1,0:T(8,128)S(1)} %get-tuple-element.33.lam_ref, bf16[3,5,32,512]{3,2,1,0:T(8,128)(2,1)S(1)} %get-tuple-element.26.saved_ref, bf16[3,512,512]{2,1,0:T(8,128)(2,1)S(1)} %get-tuple-element.27.stiff_ref, f32[1,32]{1,0:T(1,128)S(1)} %bitcast.10, ...), custom_call_target="tpu_custom_call" | custom-call | tf_op jit(solution)/shard_map/pallas_call | solution.py:379
  40.2 0.0 collective-permute-done.8.refs_1_
  40.2 0.0 collective-permute-done.14.refs_7_
  40.2 0.0 collective-permute-done.12.refs_5_
  40.2 0.0 collective-permute-done.10.refs_3_
  40.2 2.2 %shard_map.105 = (f32[5,32,512]{2,1,0:T(8,128)S(1)}, bf16[320,128]{1,0:T(8,128)(2,1)S(1)}, bf16[320,128]{1,0:T(8,128)(2,1)S(1)}) custom-call(bf16[320,128]{1,0:T(8,128)(2,1)S(1)} %get-tuple-element.32.refs_0_.refs_8_, bf16[320,128]{1,0:T(8,128)(2,1)S(1)} %collective-permute-done.8.refs_1_, bf16[320,128]{1,0:T(8,128)(2,1)S(1)} %collective-permute-done.9.refs_2_, ...), custom_call_target="tpu_custom_call" | custom-call | tf_op jit(solution)/shard_map/pallas_call | solution.py:379
  42.4 2.7 %collective-permute-start.21 = (bf16[320,128]{1,0:T(8,128)(2,1)S(1)}, bf16[320,128]{1,0:T(8,128)(2,1)S(1)}, u32[]{:S(2)}, u32[]{:S(2)}) collective-permute-start(bf16[320,128]{1,0:T(8,128)(2,1)S(1)} %get-tuple-element.36.refs_0_.refs_8_), channel_id=1, source_target_pairs={{0,6},{2,4},{4,2},{6,0},{1,7},{3,5},{5,3},{7,1},{8,14},{10,12},{12... | collective-permute-start | bytes 245768 | tf_op jit(solution)/shard_map/ppermute | solution.py:399
  45.1 0.0 collective-permute-start.19
  45.1 1.7 %collective-permute-start.17 = (bf16[320,128]{1,0:T(8,128)(2,1)S(1)}, bf16[320,128]{1,0:T(8,128)(2,1)S(1)}, u32[]{:S(2)}, u32[]{:S(2)}) collective-permute-start(bf16[320,128]{1,0:T(8,128)(2,1)S(1)} %get-tuple-element.36.refs_0_.refs_8_), channel_id=1, source_target_pairs={{0,2},{2,0},{4,6},{6,4},{1,3},{3,1},{5,7},{7,5},{8,10},{10,8},{12,... | collective-permute-start | bytes 245768 | tf_op jit(solution)/shard_map/ppermute | solution.py:399
  46.9 0.0 collective-permute-start.16
  46.9 0.5 collective-permute-start.23
  47.4 2.3 %collective-permute-done.21.refs_6_ = bf16[320,128]{1,0:T(8,128)(2,1)S(1)} collective-permute-done((bf16[320,128]{1,0:T(8,128)(2,1)S(1)}, bf16[320,128]{1,0:T(8,128)(2,1)S(1)}, u32[]{:S(2)}, u32[]{:S(2)}) %collective-permute-start.21) | collective-permute-done | bytes 81952 | tf_op jit(solution)/shard_map/ppermute | solution.py:399
  49.6 2.8 %collective-permute-done.19.refs_4_ = bf16[320,128]{1,0:T(8,128)(2,1)S(1)} collective-permute-done((bf16[320,128]{1,0:T(8,128)(2,1)S(1)}, bf16[320,128]{1,0:T(8,128)(2,1)S(1)}, u32[]{:S(2)}, u32[]{:S(2)}) %collective-permute-start.19) | collective-permute-done | bytes 81952 | tf_op jit(solution)/shard_map/ppermute | solution.py:399
  52.4 0.0 collective-permute-start.20
  52.4 0.0 collective-permute-done.17.refs_2_
  52.4 0.5 collective-permute-start.18
  52.9 0.0 collective-permute-done.23.near_ref
  52.9 1.4 %shard_map.106.refs_9_ = f32[5,32,512]{2,1,0:T(8,128)S(1)} custom-call(f32[5,32,512]{2,1,0:T(8,128)S(1)} %get-tuple-element.37.lam_ref, bf16[3,5,32,512]{3,2,1,0:T(8,128)(2,1)S(1)} %get-tuple-element.26.saved_ref, bf16[3,512,512]{2,1,0:T(8,128)(2,1)S(1)} %get-tuple-element.27.stiff_ref, f32[1,32]{1,0:T(1,128)S(1)} %bitcast.12, ...), custom_call_target="tpu_custom_call" | custom-call | tf_op jit(solution)/shard_map/pallas_call | solution.py:379
  54.3 0.0 collective-permute-done.16.refs_1_
  54.3 0.0 collective-permute-done.22.refs_7_
  54.3 0.0 collective-permute-done.18.refs_3_
  54.4 2.4 %shard_map.107 = f32[5,32,512]{2,1,0:T(8,128)} custom-call(bf16[320,128]{1,0:T(8,128)(2,1)S(1)} %get-tuple-element.36.refs_0_.refs_8_, bf16[320,128]{1,0:T(8,128)(2,1)S(1)} %collective-permute-done.16.refs_1_, bf16[320,128]{1,0:T(8,128)(2,1)S(1)} %collective-permute-done.17.refs_2_, bf16[320,128]{1,0:T(8,128)(2,1)S(1)} %collective-permute-done.18.refs_3_, ...), custom_call_target="tpu_custom_call" | custom-call | tf_op jit(solution)/shard_map/pallas_call | solution.py:379
  (12 shorter events, 0.0 us)
Async XLA Ops:
  0.0 1.0 %copy-start.2 = (bf16[512,384]{1,0:T(8,128)(2,1)S(1)}, bf16[512,384]{1,0:T(8,128)(2,1)}, u32[]{:S(2)}) copy-start(bf16[512,384]{1,0:T(8,128)(2,1)} %constant.16.clone.table_hbm) | copy-start | bytes 1179652
  1.0 1.0 %copy-start.3 = (f32[32,5,512]{2,0,1:T(8,128)S(1)}, f32[32,5,512]{2,0,1:T(8,128)}, u32[]{:S(2)}) copy-start(f32[32,5,512]{2,0,1:T(8,128)} %param.10) | copy-start | bytes 983044
  2.0 0.7 %copy-start.7 = (s32[1,5,64]{2,0,1:T(1,128)S(1)}, s32[1,5,64]{2,0,1:T(1,128)}, u32[]{:S(2)}) copy-start(s32[1,5,64]{2,0,1:T(1,128)} %param.15) | copy-start | bytes 3844
  2.7 0.7 %copy-start.8 = (s32[1,2,16]{2,1,0:T(2,128)S(1)}, s32[1,2,16]{2,1,0:T(2,128)}, u32[]{:S(2)}) copy-start(s32[1,2,16]{2,1,0:T(2,128)} %conf_hbm.1) | copy-start | bytes 388
  3.3 0.7 %copy-start.9 = (s32[1,128]{1,0:T(1,128)S(1)}, s32[1,128]{1,0:T(1,128)}, u32[]{:S(2)}) copy-start(s32[1,128]{1,0:T(1,128)} %send_hbm.1) | copy-start | bytes 1540
  5.1 19.2 %copy-start.6 = (f32[32]{0:T(128)S(1)}, f32[32]{0:T(128)}, u32[]{:S(2)}) copy-start(f32[32]{0:T(128)} %param.12) | copy-start | bytes 388
  5.1 8.3 %collective-permute-start.5 = (bf16[336,128]{1,0:T(8,128)(2,1)S(1)}, bf16[336,128]{1,0:T(8,128)(2,1)S(1)}, u32[]{:S(2)}, u32[]{:S(2)}) collective-permute-start(bf16[336,128]{1,0:T(8,128)(2,1)S(1)} %get-tuple-element.22.refs_0_.refs_8_), channel_id=1, source_target_pairs={{0,6},{2,4},{4,2},{6,0},{1,7},{3,5},{5,3},{7,1},{8,14},{10,12},{12... | collective-permute-start | bytes 258056 | tf_op jit(solution)/shard_map/ppermute | solution.py:399
  10.3 7.2 %collective-permute-start.3 = (bf16[336,128]{1,0:T(8,128)(2,1)S(1)}, bf16[336,128]{1,0:T(8,128)(2,1)S(1)}, u32[]{:S(2)}, u32[]{:S(2)}) collective-permute-start(bf16[336,128]{1,0:T(8,128)(2,1)S(1)} %get-tuple-element.22.refs_0_.refs_8_), channel_id=1, source_target_pairs={{0,4},{2,6},{4,0},{6,2},{1,5},{3,7},{5,1},{7,3},{8,12},{10,14},{12... | collective-permute-start | bytes 258056 | tf_op jit(solution)/shard_map/ppermute | solution.py:399
  10.3 7.2 %collective-permute-start.1 = (bf16[336,128]{1,0:T(8,128)(2,1)S(1)}, bf16[336,128]{1,0:T(8,128)(2,1)S(1)}, u32[]{:S(2)}, u32[]{:S(2)}) collective-permute-start(bf16[336,128]{1,0:T(8,128)(2,1)S(1)} %get-tuple-element.22.refs_0_.refs_8_), channel_id=1, source_target_pairs={{0,2},{2,0},{4,6},{6,4},{1,3},{3,1},{5,7},{7,5},{8,10},{10,8},{12,... | collective-permute-start | bytes 258056 | tf_op jit(solution)/shard_map/ppermute | solution.py:399
  10.9 14.8 %collective-permute-start = (bf16[336,128]{1,0:T(8,128)(2,1)S(1)}, bf16[336,128]{1,0:T(8,128)(2,1)S(1)}, u32[]{:S(2)}, u32[]{:S(2)}) collective-permute-start(bf16[336,128]{1,0:T(8,128)(2,1)S(1)} %get-tuple-element.22.refs_0_.refs_8_), channel_id=1, source_target_pairs={{0,1},{1,0},{2,3},{3,2},{4,5},{5,4},{6,7},{7,6},{8,9},{9,8},{10,11... | collective-permute-start | bytes 258056 | tf_op jit(solution)/shard_map/ppermute | solution.py:400
  13.4 12.3 %collective-permute-start.6 = (bf16[336,128]{1,0:T(8,128)(2,1)S(1)}, bf16[336,128]{1,0:T(8,128)(2,1)S(1)}, u32[]{:S(2)}, u32[]{:S(2)}) collective-permute-start(bf16[336,128]{1,0:T(8,128)(2,1)S(1)} %collective-permute-done.5.refs_6_), channel_id=1, source_target_pairs={{0,1},{1,0},{2,3},{3,2},{4,5},{5,4},{6,7},{7,6},{8,9},{9,8},{10,11... | collective-permute-start | bytes 258056 | tf_op jit(solution)/shard_map/ppermute | solution.py:400
  17.5 8.2 %collective-permute-start.4 = (bf16[336,128]{1,0:T(8,128)(2,1)S(1)}, bf16[336,128]{1,0:T(8,128)(2,1)S(1)}, u32[]{:S(2)}, u32[]{:S(2)}) collective-permute-start(bf16[336,128]{1,0:T(8,128)(2,1)S(1)} %collective-permute-done.3.refs_4_), channel_id=1, source_target_pairs={{0,1},{1,0},{2,3},{3,2},{4,5},{5,4},{6,7},{7,6},{8,9},{9,8},{10,11... | collective-permute-start | bytes 258056 | tf_op jit(solution)/shard_map/ppermute | solution.py:400
  17.5 8.2 %collective-permute-start.2 = (bf16[336,128]{1,0:T(8,128)(2,1)S(1)}, bf16[336,128]{1,0:T(8,128)(2,1)S(1)}, u32[]{:S(2)}, u32[]{:S(2)}) collective-permute-start(bf16[336,128]{1,0:T(8,128)(2,1)S(1)} %collective-permute-done.1.refs_2_), channel_id=1, source_target_pairs={{0,1},{1,0},{2,3},{3,2},{4,5},{5,4},{6,7},{7,6},{8,9},{9,8},{10,11... | collective-permute-start | bytes 258056 | tf_op jit(solution)/shard_map/ppermute | solution.py:400
  18.0 6.3 %collective-permute-start.7 = (bf16[320,128]{1,0:T(8,128)(2,1)S(1)}, bf16[320,128]{1,0:T(8,128)(2,1)S(1)}, u32[]{:S(2)}, u32[]{:S(2)}) collective-permute-start(bf16[320,128]{1,0:T(8,128)(2,1)S(1)} %get-tuple-element.28.own_ref), channel_id=1, source_target_pairs={{0,1},{1,0},{2,3},{3,2},{4,5},{5,4},{6,7},{7,6},{8,9},{9,8},{10,11... | collective-permute-start | bytes 245768 | tf_op jit(solution)/shard_map/ppermute | solution.py:409
  18.0 1.4 %copy-start = (bf16[3,512,512]{2,1,0:T(8,128)(2,1)S(1)}, bf16[3,512,512]{2,1,0:T(8,128)(2,1)}, u32[]{:S(2)}) copy-start(bf16[3,512,512]{2,1,0:T(8,128)(2,1)} %stiff_hbm.1) | copy-start | bytes 4718596
  19.4 1.0 %copy-start.1 = (bf16[3,32,5,512]{3,1,2,0:T(8,128)(2,1)S(1)}, bf16[3,32,5,512]{3,1,2,0:T(8,128)(2,1)}, u32[]{:S(2)}) copy-start(bf16[3,32,5,512]{3,1,2,0:T(8,128)(2,1)} %param.11) | copy-start | bytes 1474564
  20.4 0.9 %copy-start.4 = (bf16[256,192]{1,0:T(8,128)(2,1)S(1)}, bf16[256,192]{1,0:T(8,128)(2,1)}, u32[]{:S(2)}) copy-start(bf16[256,192]{1,0:T(8,128)(2,1)} %constant.18.clone.backward_hbm) | copy-start | bytes 294916
  21.3 0.8 %copy-start.5 = (bf16[256,128]{1,0:T(8,128)(2,1)S(1)}, bf16[256,128]{1,0:T(8,128)(2,1)}, u32[]{:S(2)}) copy-start(bf16[256,128]{1,0:T(8,128)(2,1)} %constant.17.clone.forward_hbm) | copy-start | bytes 196612
  28.0 7.3 %collective-permute-start.13 = (bf16[320,128]{1,0:T(8,128)(2,1)S(1)}, bf16[320,128]{1,0:T(8,128)(2,1)S(1)}, u32[]{:S(2)}, u32[]{:S(2)}) collective-permute-start(bf16[320,128]{1,0:T(8,128)(2,1)S(1)} %get-tuple-element.32.refs_0_.refs_8_), channel_id=1, source_target_pairs={{0,6},{2,4},{4,2},{6,0},{1,7},{3,5},{5,3},{7,1},{8,14},{10,12},{12... | collective-permute-start | bytes 245768 | tf_op jit(solution)/shard_map/ppermute | solution.py:399
  30.7 7.5 %collective-permute-start.11 = (bf16[320,128]{1,0:T(8,128)(2,1)S(1)}, bf16[320,128]{1,0:T(8,128)(2,1)S(1)}, u32[]{:S(2)}, u32[]{:S(2)}) collective-permute-start(bf16[320,128]{1,0:T(8,128)(2,1)S(1)} %get-tuple-element.32.refs_0_.refs_8_), channel_id=1, source_target_pairs={{0,4},{2,6},{4,0},{6,2},{1,5},{3,7},{5,1},{7,3},{8,12},{10,14},{12... | collective-permute-start | bytes 245768 | tf_op jit(solution)/shard_map/ppermute | solution.py:399
  30.7 7.6 %collective-permute-start.9 = (bf16[320,128]{1,0:T(8,128)(2,1)S(1)}, bf16[320,128]{1,0:T(8,128)(2,1)S(1)}, u32[]{:S(2)}, u32[]{:S(2)}) collective-permute-start(bf16[320,128]{1,0:T(8,128)(2,1)S(1)} %get-tuple-element.32.refs_0_.refs_8_), channel_id=1, source_target_pairs={{0,2},{2,0},{4,6},{6,4},{1,3},{3,1},{5,7},{7,5},{8,10},{10,8},{12,... | collective-permute-start | bytes 245768 | tf_op jit(solution)/shard_map/ppermute | solution.py:399
  32.5 7.7 %collective-permute-start.8 = (bf16[320,128]{1,0:T(8,128)(2,1)S(1)}, bf16[320,128]{1,0:T(8,128)(2,1)S(1)}, u32[]{:S(2)}, u32[]{:S(2)}) collective-permute-start(bf16[320,128]{1,0:T(8,128)(2,1)S(1)} %get-tuple-element.32.refs_0_.refs_8_), channel_id=1, source_target_pairs={{0,1},{1,0},{2,3},{3,2},{4,5},{5,4},{6,7},{7,6},{8,9},{9,8},{10,11... | collective-permute-start | bytes 245768 | tf_op jit(solution)/shard_map/ppermute | solution.py:400
  32.5 6.3 %collective-permute-start.15 = (bf16[320,128]{1,0:T(8,128)(2,1)S(1)}, bf16[320,128]{1,0:T(8,128)(2,1)S(1)}, u32[]{:S(2)}, u32[]{:S(2)}) collective-permute-start(bf16[320,128]{1,0:T(8,128)(2,1)S(1)} %get-tuple-element.34.own_ref), channel_id=1, source_target_pairs={{0,1},{1,0},{2,3},{3,2},{4,5},{5,4},{6,7},{7,6},{8,9},{9,8},{10,11... | collective-permute-start | bytes 245768 | tf_op jit(solution)/shard_map/ppermute | solution.py:409
  35.3 4.9 %collective-permute-start.14 = (bf16[320,128]{1,0:T(8,128)(2,1)S(1)}, bf16[320,128]{1,0:T(8,128)(2,1)S(1)}, u32[]{:S(2)}, u32[]{:S(2)}) collective-permute-start(bf16[320,128]{1,0:T(8,128)(2,1)S(1)} %collective-permute-done.13.refs_6_), channel_id=1, source_target_pairs={{0,1},{1,0},{2,3},{3,2},{4,5},{5,4},{6,7},{7,6},{8,9},{9,8},{10,11... | collective-permute-start | bytes 245768 | tf_op jit(solution)/shard_map/ppermute | solution.py:400
  38.3 1.9 %collective-permute-start.12 = (bf16[320,128]{1,0:T(8,128)(2,1)S(1)}, bf16[320,128]{1,0:T(8,128)(2,1)S(1)}, u32[]{:S(2)}, u32[]{:S(2)}) collective-permute-start(bf16[320,128]{1,0:T(8,128)(2,1)S(1)} %collective-permute-done.11.refs_4_), channel_id=1, source_target_pairs={{0,1},{1,0},{2,3},{3,2},{4,5},{5,4},{6,7},{7,6},{8,9},{9,8},{10,11... | collective-permute-start | bytes 245768 | tf_op jit(solution)/shard_map/ppermute | solution.py:400
  38.3 1.9 %collective-permute-start.10 = (bf16[320,128]{1,0:T(8,128)(2,1)S(1)}, bf16[320,128]{1,0:T(8,128)(2,1)S(1)}, u32[]{:S(2)}, u32[]{:S(2)}) collective-permute-start(bf16[320,128]{1,0:T(8,128)(2,1)S(1)} %collective-permute-done.9.refs_2_), channel_id=1, source_target_pairs={{0,1},{1,0},{2,3},{3,2},{4,5},{5,4},{6,7},{7,6},{8,9},{9,8},{10,11... | collective-permute-start | bytes 245768 | tf_op jit(solution)/shard_map/ppermute | solution.py:400
  42.4 7.2 %collective-permute-start.21 = (bf16[320,128]{1,0:T(8,128)(2,1)S(1)}, bf16[320,128]{1,0:T(8,128)(2,1)S(1)}, u32[]{:S(2)}, u32[]{:S(2)}) collective-permute-start(bf16[320,128]{1,0:T(8,128)(2,1)S(1)} %get-tuple-element.36.refs_0_.refs_8_), channel_id=1, source_target_pairs={{0,6},{2,4},{4,2},{6,0},{1,7},{3,5},{5,3},{7,1},{8,14},{10,12},{12... | collective-permute-start | bytes 245768 | tf_op jit(solution)/shard_map/ppermute | solution.py:399
  45.1 7.3 %collective-permute-start.19 = (bf16[320,128]{1,0:T(8,128)(2,1)S(1)}, bf16[320,128]{1,0:T(8,128)(2,1)S(1)}, u32[]{:S(2)}, u32[]{:S(2)}) collective-permute-start(bf16[320,128]{1,0:T(8,128)(2,1)S(1)} %get-tuple-element.36.refs_0_.refs_8_), channel_id=1, source_target_pairs={{0,4},{2,6},{4,0},{6,2},{1,5},{3,7},{5,1},{7,3},{8,12},{10,14},{12... | collective-permute-start | bytes 245768 | tf_op jit(solution)/shard_map/ppermute | solution.py:399
  45.1 7.3 %collective-permute-start.17 = (bf16[320,128]{1,0:T(8,128)(2,1)S(1)}, bf16[320,128]{1,0:T(8,128)(2,1)S(1)}, u32[]{:S(2)}, u32[]{:S(2)}) collective-permute-start(bf16[320,128]{1,0:T(8,128)(2,1)S(1)} %get-tuple-element.36.refs_0_.refs_8_), channel_id=1, source_target_pairs={{0,2},{2,0},{4,6},{6,4},{1,3},{3,1},{5,7},{7,5},{8,10},{10,8},{12,... | collective-permute-start | bytes 245768 | tf_op jit(solution)/shard_map/ppermute | solution.py:399
  46.9 7.5 %collective-permute-start.16 = (bf16[320,128]{1,0:T(8,128)(2,1)S(1)}, bf16[320,128]{1,0:T(8,128)(2,1)S(1)}, u32[]{:S(2)}, u32[]{:S(2)}) collective-permute-start(bf16[320,128]{1,0:T(8,128)(2,1)S(1)} %get-tuple-element.36.refs_0_.refs_8_), channel_id=1, source_target_pairs={{0,1},{1,0},{2,3},{3,2},{4,5},{5,4},{6,7},{7,6},{8,9},{9,8},{10,11... | collective-permute-start | bytes 245768 | tf_op jit(solution)/shard_map/ppermute | solution.py:400
  46.9 6.1 %collective-permute-start.23 = (bf16[320,128]{1,0:T(8,128)(2,1)S(1)}, bf16[320,128]{1,0:T(8,128)(2,1)S(1)}, u32[]{:S(2)}, u32[]{:S(2)}) collective-permute-start(bf16[320,128]{1,0:T(8,128)(2,1)S(1)} %get-tuple-element.38.own_ref), channel_id=1, source_target_pairs={{0,1},{1,0},{2,3},{3,2},{4,5},{5,4},{6,7},{7,6},{8,9},{9,8},{10,11... | collective-permute-start | bytes 245768 | tf_op jit(solution)/shard_map/ppermute | solution.py:409
  49.6 4.7 %collective-permute-start.22 = (bf16[320,128]{1,0:T(8,128)(2,1)S(1)}, bf16[320,128]{1,0:T(8,128)(2,1)S(1)}, u32[]{:S(2)}, u32[]{:S(2)}) collective-permute-start(bf16[320,128]{1,0:T(8,128)(2,1)S(1)} %collective-permute-done.21.refs_6_), channel_id=1, source_target_pairs={{0,1},{1,0},{2,3},{3,2},{4,5},{5,4},{6,7},{7,6},{8,9},{9,8},{10,11... | collective-permute-start | bytes 245768 | tf_op jit(solution)/shard_map/ppermute | solution.py:400
  52.4 1.9 %collective-permute-start.20 = (bf16[320,128]{1,0:T(8,128)(2,1)S(1)}, bf16[320,128]{1,0:T(8,128)(2,1)S(1)}, u32[]{:S(2)}, u32[]{:S(2)}) collective-permute-start(bf16[320,128]{1,0:T(8,128)(2,1)S(1)} %collective-permute-done.19.refs_4_), channel_id=1, source_target_pairs={{0,1},{1,0},{2,3},{3,2},{4,5},{5,4},{6,7},{7,6},{8,9},{9,8},{10,11... | collective-permute-start | bytes 245768 | tf_op jit(solution)/shard_map/ppermute | solution.py:400
  52.4 1.9 %collective-permute-start.18 = (bf16[320,128]{1,0:T(8,128)(2,1)S(1)}, bf16[320,128]{1,0:T(8,128)(2,1)S(1)}, u32[]{:S(2)}, u32[]{:S(2)}) collective-permute-start(bf16[320,128]{1,0:T(8,128)(2,1)S(1)} %collective-permute-done.17.refs_2_), channel_id=1, source_target_pairs={{0,1},{1,0},{2,3},{3,2},{4,5},{5,4},{6,7},{7,6},{8,9},{9,8},{10,11... | collective-permute-start | bytes 245768 | tf_op jit(solution)/shard_map/ppermute | solution.py:400

commit v3 on v2

--- a/solution.py
+++ b/solution.py
@@ -7,6 +7,7 @@
 from jax.experimental import pallas as pl
 from jax.experimental.pallas import tpu as pltpu
 from jax.sharding import PartitionSpec as P
+
 
 ORDER = 7
 LINE = ORDER + 1
@@ -158,7 +159,7 @@
     return copies
 
 
-def start_kernel(lam_hbm, send_hbm, conf_hbm, map_hbm, table_hbm, out_ref, shared_ref, hot_ref, lam_ref, table_ref, send_ref, conf_ref, map_ref, ids_ref, sems):
+def start_kernel(lam_hbm, send_hbm, conf_hbm, map_hbm, table_hbm, me_ref, out_ref, pair_ref, hot_ref, lam_ref, table_ref, send_ref, conf_ref, map_ref, ids_ref, sems):
     pairs = ((send_hbm, send_ref), (conf_hbm, conf_ref), (map_hbm, map_ref), (lam_hbm, lam_ref), (table_hbm, table_ref))
     copies = fetch(pairs, sems)
     elements = lam_ref.shape[1]
@@ -188,12 +189,14 @@
         part = dot(fields.astype(F32).astype(BF16), hits, 1, 1)
         info = part if info is None else info + part
     out_ref[ROWS:] = info.astype(BF16)
+    pair_ref[ROWS:, :slots] = info.astype(BF16)
+    pair_ref[ROWS:, slots:] = jnp.zeros((EXTRA, pair_ref.shape[1] - slots), BF16)
     for copy in copies[3:]:
         copy.wait()
     lam_low = lam_ref[...].astype(BF16).reshape(5 * elements, ELEM)
     values = slot_values(lam_low, hot, table_ref[...], elements)
     out_ref[0:ROWS] = values[:, :slots]
-    shared_ref[...] = values[:, slots:]
+    pair_ref[0:ROWS] = values
 
 
 def state_kernel(saved_hbm, stiff_hbm, forward_hbm, backward_hbm, hot_ref, table_ref, out_ref, saved_ref, stiff_ref, forward_ref, backward_ref, sems):
@@ -207,13 +210,12 @@
         copy.wait()
 
 
-def volume_kernel(section, faces, lam_ref, saved_ref, stiff_ref, jac_ref, own_ref, near_ref, state_ref, hot_ref, table_ref, base_ref, slope_ref, smooth_ref):
+def volume_kernel(section, slots, faces, lam_ref, saved_ref, stiff_ref, jac_ref, own_ref, near_ref, state_ref, hot_ref, table_ref, base_ref, slope_ref, smooth_ref):
     elements = lam_ref.shape[1]
     coef = step_size * section_weights[section]
     lam_low = lam_ref[...].astype(BF16).reshape(5 * elements, ELEM)
 
-    slots = state_ref.shape[2] - own_ref.shape[1]
-    width = own_ref.shape[1]
+    width = own_ref.shape[1] - slots
     lane = lax.broadcasted_iota(jnp.int32, (FACE, width), 1)
     used = lane < 2 * faces
     lower = lane < faces
@@ -221,9 +223,9 @@
     w, u = [], []
     for v in range(5):
         rows = slice(v * FACE, (v + 1) * FACE)
-        near = near_ref[rows].astype(F32)
+        near = near_ref[rows, slots:].astype(F32)
         near = jnp.where(lower, pltpu.roll(near, width - faces, 1), pltpu.roll(near, faces, 1))
-        w.append(jnp.where(used, sign * (near - own_ref[rows].astype(F32)), 0.0))
+        w.append(jnp.where(used, sign * (near - own_ref[rows, slots:].astype(F32)), 0.0))
         u.append(jnp.where(used, state_ref[section, rows, slots:].astype(F32), REST[v]))
     g = flux_pull(u, w, None)
     grads = [0.5 * g[v] + (0.5 * penalty) * sign * w[v] for v in range(5)]
@@ -268,6 +270,7 @@
                 vol = pulled[v] + smooth_ref[rows, c : c + 128]
                 base_ref[v, r : r + step, c : c + 128] = lam_ref[v, r : r + step, c : c + 128] + scale * vol
 
+
 def spread_children(matrix, stacked):
     return dot(matrix, jnp.concatenate(stacked, axis=0))
 
@@ -307,14 +310,14 @@
 
 def mortar_update(section, relative, first, last, count, *refs):
     refs = list(refs)
-    pieces = [r[...] for r in refs[:count]]
+    slots = refs[count].shape[1]
+    pieces = [r[...] if len(r.shape) == 3 else r[:, :slots] for r in refs[:count]]
     own_ref = refs[count]
     base_ref, state_ref, hot_ref, table_ref, jac_ref, forward_ref, backward_ref, me_ref = refs[count + 1 : count + 9]
     outs = refs[count + 9 :]
     elements = base_ref.shape[1]
     if len(pieces) == 1 and pieces[0].ndim == 3:
         pieces = [pieces[0][p] for p in range(pieces[0].shape[0])]
-    slots = pieces[0].shape[1]
     cap = slots // len(pieces)
     if first:
         info = read_table(pieces, me_ref, cap, relative)
@@ -323,7 +326,7 @@
     else:
         info = outs[0][...]
         outs = outs[1:]
-    code, child, axis, live, left = (jnp.broadcast_to(info[k : k + 1], (FACE, slots)) for k in range(5))
+    _, child, axis, live, left = (jnp.broadcast_to(info[k : k + 1], (FACE, slots)) for k in range(5))
     row = lax.broadcasted_iota(jnp.int32, (slots, slots), 0)
     partner = None
     for p in range(0, len(pieces), 2):
@@ -367,14 +370,14 @@
         lam_low = jnp.concatenate([x.astype(BF16) for x in lam], axis=0)
         values = slot_values(lam_low, hot_ref[...], table, elements)
         outs[1][...] = values[:, :slots]
-        outs[2][...] = values[:, slots:]
+        outs[2][...] = values
 
 
 def call(kernel, outs, args, scratch=(), scalars=(), far=0, last=False):
     def space(i):
-        return pl.ANY if i < far else pltpu.SMEM if i in scalars else pltpu.VMEM
-
-    args = [pltpu.with_memory_space_constraint(a, pltpu.VMEM) if space(i) is pltpu.VMEM else a for i, a in enumerate(args)]
+        return pltpu.HBM if i < far else pltpu.SMEM if i in scalars else pltpu.VMEM
+
+    args = [a if i in scalars else pltpu.with_memory_space_constraint(a, space(i)) for i, a in enumerate(args)]
     shapes = [jax.ShapeDtypeStruct(o, t) if last else pltpu.VMEM(o, t) for o, t in outs]
     return pl.pallas_call(
         kernel,
@@ -390,27 +393,28 @@
     return n & (n - 1) == 0
 
 
-def gather_group(x):
+def paired():
     ny, nz = lax.axis_size("gy"), lax.axis_size("gz")
-    if nz != 2 or not power_of_two(ny) or ny > 8:
-        return [lax.all_gather(x, ("gy", "gz"), axis=0, tiled=False)], False
-    pieces = []
-    for k in range(ny):
-        here = x if k == 0 else lax.ppermute(x, "gy", [(i, i ^ k) for i in range(ny)])
-        pieces += [here, lax.ppermute(here, "gz", [(0, 1), (1, 0)])]
-    return pieces, True
-
-
-def neighbours(payload, faces):
+    return nz == 2 and power_of_two(ny) and ny <= 8
+
+
+def swap_pair(x):
+    return lax.ppermute(x, "gz", [(0, 1), (1, 0)])
+
+
+def send_along(x, k):
+    ny = lax.axis_size("gy")
+    return lax.ppermute(x, "gy", [(i, i ^ k) for i in range(ny)])
+
+
+def neighbours(payload, slots, faces):
     peers = lax.axis_size("gz")
     up = [(i, (i + 1) % peers) for i in range(peers)]
     down = [(j, i) for i, j in up]
-    if peers == 2:
-        return lax.ppermute(payload, "gz", up)
     below = lax.ppermute(payload, "gz", up)
     above = lax.ppermute(payload, "gz", down)
     lane = lax.broadcasted_iota(jnp.int32, payload.shape, 1)
-    return jnp.where(lane < faces, above, below)
+    return jnp.where(lane < slots + faces, above, below)
 
 
 def per_device(adjoint, saved, inv_jac, stiffness, send_face, mortar_table, conf_faces):
@@ -427,15 +431,15 @@
     me = lax.axis_index(("gy", "gz")).astype(jnp.int32).reshape(1)
     rows = ((5, elements, ELEM), F32)
     sent = ((ROWS, slots), BF16)
-    conforming = ((ROWS, shared), BF16)
+    pair = ((ROWS, slots + shared), BF16)
     info_shape = ((EXTRA, slots), jnp.int32)
 
     mortars = jnp.transpose(mortar_table, (1, 0, 2))
     held = lambda x: (x.shape, x.dtype)
-    outgoing, own_shared, hot, lam, table = call(
+    outgoing, both, hot, lam, table = call(
         start_kernel,
-        [((ROWS + EXTRA, slots), BF16), conforming, ((6 * elements, slots + shared), BF16), held(lam), held(table)],
-        [lam, send_face, conf_faces, mortars, table],
+        [((ROWS + EXTRA, slots), BF16), ((ROWS + EXTRA, slots + shared), BF16), ((6 * elements, slots + shared), BF16), held(lam), held(table)],
+        [lam, send_face, conf_faces, mortars, table, me],
         scratch=(
             pltpu.VMEM(send_face.shape, jnp.int32),
             pltpu.VMEM(conf_faces.shape, jnp.int32),
@@ -444,6 +448,7 @@
             pltpu.SemaphoreType.DMA((5,)),
         ),
         far=5,
+        scalars=(5,),
     )
     values, states, stiffness, forward, backward = call(
         state_kernel,
@@ -454,16 +459,28 @@
     )
     info = None
     for section in (2, 1, 0):
-        pieces, relative = gather_group(outgoing)
-        near = neighbours(own_shared, faces)
+        relative = paired()
+        if relative:
+            column = [None] * (lax.axis_size("gy") - 1)
+            for k in reversed(range(len(column))):
+                column[k] = send_along(outgoing, k + 1)
+            near = swap_pair(both)
+        else:
+            near = neighbours(both, slots, faces)
         (base,) = call(
-            functools.partial(volume_kernel, section, faces),
+            functools.partial(volume_kernel, section, slots, faces),
             [rows],
-            [lam, states, stiffness, jac, own_shared, near, values, hot, table],
+            [lam, states, stiffness, jac, both, near, values, hot, table],
             scratch=(pltpu.VMEM((3, 5 * elements, ELEM), F32), pltpu.VMEM((5 * elements, ELEM), F32)),
         )
+        if relative:
+            pieces = [outgoing, near]
+            for here in column:
+                pieces += [here, swap_pair(here)]
+        else:
+            pieces = [lax.all_gather(outgoing, ("gy", "gz"), axis=0, tiled=False)]
         first, last = section == sections - 1, section == 0
-        outs = ([info_shape] if first else []) + [rows] + ([] if last else [sent, conforming])
+        outs = ([info_shape] if first else []) + [rows] + ([] if last else [sent, pair])
         args = pieces + [outgoing, base, values, hot, table, jac, forward, backward, me] + ([] if first else [info])
         out = call(
             functools.partial(mortar_update, section, relative, first, last, len(pieces)),
@@ -473,7 +490,7 @@
             info, out = out[0], out[1:]
         lam = out[0]
         if not last:
-            outgoing, own_shared = out[1:]
+            outgoing, both = out[1:]
     return jnp.transpose(lam, (1, 0, 2))
 
 

time: 57.1 us -> 50.1 us (0.88)
  local copies, waits for them, and re-layouts: 8.17 us -> 0.01 us
  waiting for transfers between devices: 16.9 us -> 18.1 us
  Pallas kernels: 14.2 us -> 15.4 us
  starting transfers between devices: 17.3 us -> 16.3 us
    unnamed x20 -> x2, local copies, waits for them, and re-layouts: 8.17 us -> 0.01 us
    pallas_call x8, Pallas kernels: 14.2 us -> 15.4 us  [call(): pl.pallas_call(kernel, out_shape=shapes, in_specs=[pl.BlockSpec(memory_sp...]
    ppermute x24 -> x21, waiting for transfers between devices: 16.9 us -> 18.1 us  [the longest x9 18 us: send_along(): return lax.ppermute(x, 'gy', [(i, i ^ k) for i in range(ny)])]
    ppermute x24 -> x21, starting transfers between devices: 17.3 us -> 16.3 us  [the longest x9 14.2 us: send_along(): return lax.ppermute(x, 'gy', [(i, i ^ k) for i in range(ny)])]
  transfers between devices with their start and end apart: 24 -> 21, of which waited for: 6 -> 7; matrix products, arithmetic and copies ran while one was open for 0% -> 0% of each run, Pallas kernels for 11% -> 14%
where the time goes in v3:
time: 50.1 us; the launch traced here: 49.9 us
  waiting for transfers between devices  18.1 us (36%)
  starting transfers between devices  16.3 us (33%)
  Pallas kernels  15.4 us (31%)
    ppermute x9, waiting for transfers between devices, send_along(): return lax.ppermute(x, 'gy', [(i, i ^ k) for i in range(ny)])  18 us
    pallas_call x8, Pallas kernels, call(): pl.pallas_call(kernel, out_shape=shapes, in_specs=[pl.BlockSpec(memory_sp...  15.4 us
    ppermute x9, starting transfers between devices, send_along(): return lax.ppermute(x, 'gy', [(i, i ^ k) for i in range(ny)])  14.2 us
    ppermute x12, starting transfers between devices, swap_pair(): return lax.ppermute(x, 'gz', [(0, 1), (1, 0)])  2.05 us
  transfers between devices with their start and end apart: 21, of which 7 were waited for; matrix products, arithmetic and copies ran while one was open for 0% of the time, Pallas kernels for 14%

profile of v3, /device:TPU:0, one launch (start us, length us, event | category | flops | bytes accessed | tf_op | source)
XLA Modules:
  0.0 49.9 jit_solution(9859353581696124884)
XLA Ops:
  0.0 0.0 copy-start
  0.0 1.8 %shard_map.100 = (bf16[336,128]{1,0:T(8,128)(2,1)S(1)}, bf16[336,256]{1,0:T(8,128)(2,1)S(1)}, bf16[192,256]{1,0:T(8,128)(2,1)S(1)}, f32[5,32,512]{2,1,0:T(8,128)S(1)}, bf16[512,384]{1,0:T(8,128)(2,1)S(1)}) custom-call(f32[5,32,512]{2,1,0:T(8,128)} %bitcast.13, s32[1,128]{1,0:T(1,128)} %send_hbm.1, s32[1,2,16]{2,1,0:T(2,128)} %conf_hbm.1, ...), custom_call_target="tpu_custom_call" | custom-call | tf_op jit(solution)/shard_map/pallas_call | solution.py:382
  1.8 0.6 %collective-permute-start = (bf16[336,256]{1,0:T(8,128)(2,1)S(1)}, bf16[336,256]{1,0:T(8,128)(2,1)S(1)}, u32[]{:S(2)}, u32[]{:S(2)}) collective-permute-start(bf16[336,256]{1,0:T(8,128)(2,1)S(1)} %get-tuple-element.23.own_ref), channel_id=1, source_target_pairs={{0,1},{1,0},{2,3},{3,2},{4,5},{5,4},{6,7},{7,6},{8,9},{9,8},{10,11... | collective-permute-start | bytes 516104 | tf_op jit(solution)/shard_map/ppermute | solution.py:402
  2.4 4.7 %collective-permute-start.5 = (bf16[336,128]{1,0:T(8,128)(2,1)S(1)}, bf16[336,128]{1,0:T(8,128)(2,1)S(1)}, u32[]{:S(2)}, u32[]{:S(2)}) collective-permute-start(bf16[336,128]{1,0:T(8,128)(2,1)S(1)} %get-tuple-element.22.refs_0_.refs_8_), channel_id=1, source_target_pairs={{0,6},{2,4},{4,2},{6,0},{1,7},{3,5},{5,3},{7,1},{8,14},{10,12},{12... | collective-permute-start | bytes 258056 | tf_op jit(solution)/shard_map/ppermute | solution.py:407
  7.0 0.0 collective-permute-start.3
  7.0 0.6 %collective-permute-start.1 = (bf16[336,128]{1,0:T(8,128)(2,1)S(1)}, bf16[336,128]{1,0:T(8,128)(2,1)S(1)}, u32[]{:S(2)}, u32[]{:S(2)}) collective-permute-start(bf16[336,128]{1,0:T(8,128)(2,1)S(1)} %get-tuple-element.22.refs_0_.refs_8_), channel_id=1, source_target_pairs={{0,2},{2,0},{4,6},{6,4},{1,3},{3,1},{5,7},{7,5},{8,10},{10,8},{12,... | collective-permute-start | bytes 258056 | tf_op jit(solution)/shard_map/ppermute | solution.py:407
  7.7 2.8 %collective-permute-done.5.refs_6_ = bf16[336,128]{1,0:T(8,128)(2,1)S(1)} collective-permute-done((bf16[336,128]{1,0:T(8,128)(2,1)S(1)}, bf16[336,128]{1,0:T(8,128)(2,1)S(1)}, u32[]{:S(2)}, u32[]{:S(2)}) %collective-permute-start.5) | collective-permute-done | bytes 86048 | tf_op jit(solution)/shard_map/ppermute | solution.py:407
  10.5 0.0 collective-permute-start.6
  10.5 4.3 %collective-permute-done.3.refs_4_ = bf16[336,128]{1,0:T(8,128)(2,1)S(1)} collective-permute-done((bf16[336,128]{1,0:T(8,128)(2,1)S(1)}, bf16[336,128]{1,0:T(8,128)(2,1)S(1)}, u32[]{:S(2)}, u32[]{:S(2)}) %collective-permute-start.3) | collective-permute-done | bytes 86048 | tf_op jit(solution)/shard_map/ppermute | solution.py:407
  14.9 0.0 collective-permute-start.4
  14.9 0.0 collective-permute-done.1.refs_2_
  14.9 0.5 %collective-permute-start.2 = (bf16[336,128]{1,0:T(8,128)(2,1)S(1)}, bf16[336,128]{1,0:T(8,128)(2,1)S(1)}, u32[]{:S(2)}, u32[]{:S(2)}) collective-permute-start(bf16[336,128]{1,0:T(8,128)(2,1)S(1)} %collective-permute-done.1.refs_2_), channel_id=1, source_target_pairs={{0,1},{1,0},{2,3},{3,2},{4,5},{5,4},{6,7},{7,6},{8,9},{9,8},{10,11... | collective-permute-start | bytes 258056 | tf_op jit(solution)/shard_map/ppermute | solution.py:402
  15.4 2.4 %shard_map.101 = (bf16[3,320,256]{2,1,0:T(8,128)(2,1)S(1)}, bf16[3,5,32,512]{3,2,1,0:T(8,128)(2,1)S(1)}, bf16[3,512,512]{2,1,0:T(8,128)(2,1)S(1)}, bf16[256,128]{1,0:T(8,128)(2,1)S(1)}, bf16[256,192]{1,0:T(8,128)(2,1)S(1)}) custom-call(bf16[3,5,32,512]{3,2,1,0:T(8,128)(2,1)} %bitcast.12, bf16[3,512,512]{2,1,0:T(8,128)(2,1)} %stiff_hbm.1, ...), custom_call_target="tpu_custom_call" | custom-call | tf_op jit(solution)/shard_map/pallas_call | solution.py:382
  17.8 0.0 collective-permute-done.near_ref.refs_1_
  17.8 0.0 copy-done
  17.8 1.5 %shard_map.102.refs_9_ = f32[5,32,512]{2,1,0:T(8,128)S(1)} custom-call(f32[5,32,512]{2,1,0:T(8,128)S(1)} %get-tuple-element.24.lam_ref, bf16[3,5,32,512]{3,2,1,0:T(8,128)(2,1)S(1)} %get-tuple-element.27.saved_ref, bf16[3,512,512]{2,1,0:T(8,128)(2,1)S(1)} %get-tuple-element.28.stiff_ref, f32[1,32]{1,0:T(1,128)S(1)} %bitcast.6, ...), custom_call_target="tpu_custom_call" | custom-call | tf_op jit(solution)/shard_map/pallas_call | solution.py:382
  19.3 0.0 collective-permute-done.6.refs_7_
  19.3 0.0 collective-permute-done.4.refs_5_
  19.3 0.0 collective-permute-done.2.refs_3_
  19.3 2.3 %shard_map.103 = (s32[16,128]{1,0:T(8,128)S(1)}, f32[5,32,512]{2,1,0:T(8,128)S(1)}, bf16[320,128]{1,0:T(8,128)(2,1)S(1)}, bf16[320,256]{1,0:T(8,128)(2,1)S(1)}) custom-call(bf16[336,128]{1,0:T(8,128)(2,1)S(1)} %get-tuple-element.22.refs_0_.refs_8_, bf16[336,256]{1,0:T(8,128)(2,1)S(1)} %collective-permute-done.near_ref.refs_1_, ...), custom_call_target="tpu_custom_call" | custom-call | tf_op jit(solution)/shard_map/pallas_call | solution.py:382
  21.6 2.5 %collective-permute-start.12 = (bf16[320,128]{1,0:T(8,128)(2,1)S(1)}, bf16[320,128]{1,0:T(8,128)(2,1)S(1)}, u32[]{:S(2)}, u32[]{:S(2)}) collective-permute-start(bf16[320,128]{1,0:T(8,128)(2,1)S(1)} %get-tuple-element.32.refs_0_.refs_8_), channel_id=1, source_target_pairs={{0,6},{2,4},{4,2},{6,0},{1,7},{3,5},{5,3},{7,1},{8,14},{10,12},{12... | collective-permute-start | bytes 245768 | tf_op jit(solution)/shard_map/ppermute | solution.py:407
  24.2 0.0 collective-permute-start.7
  24.2 0.0 collective-permute-start.10
  24.2 1.9 %collective-permute-start.8 = (bf16[320,128]{1,0:T(8,128)(2,1)S(1)}, bf16[320,128]{1,0:T(8,128)(2,1)S(1)}, u32[]{:S(2)}, u32[]{:S(2)}) collective-permute-start(bf16[320,128]{1,0:T(8,128)(2,1)S(1)} %get-tuple-element.32.refs_0_.refs_8_), channel_id=1, source_target_pairs={{0,2},{2,0},{4,6},{6,4},{1,3},{3,1},{5,7},{7,5},{8,10},{10,8},{12,... | collective-permute-start | bytes 245768 | tf_op jit(solution)/shard_map/ppermute | solution.py:407
  26.1 2.8 %collective-permute-done.12.refs_6_ = bf16[320,128]{1,0:T(8,128)(2,1)S(1)} collective-permute-done((bf16[320,128]{1,0:T(8,128)(2,1)S(1)}, bf16[320,128]{1,0:T(8,128)(2,1)S(1)}, u32[]{:S(2)}, u32[]{:S(2)}) %collective-permute-start.12) | collective-permute-done | bytes 81952 | tf_op jit(solution)/shard_map/ppermute | solution.py:407
  28.9 0.0 collective-permute-start.13
  28.9 2.7 %collective-permute-done.10.refs_4_ = bf16[320,128]{1,0:T(8,128)(2,1)S(1)} collective-permute-done((bf16[320,128]{1,0:T(8,128)(2,1)S(1)}, bf16[320,128]{1,0:T(8,128)(2,1)S(1)}, u32[]{:S(2)}, u32[]{:S(2)}) %collective-permute-start.10) | collective-permute-done | bytes 81952 | tf_op jit(solution)/shard_map/ppermute | solution.py:407
  31.6 0.0 collective-permute-start.11
  31.6 0.0 collective-permute-done.8.refs_2_
  31.6 0.5 %collective-permute-start.9 = (bf16[320,128]{1,0:T(8,128)(2,1)S(1)}, bf16[320,128]{1,0:T(8,128)(2,1)S(1)}, u32[]{:S(2)}, u32[]{:S(2)}) collective-permute-start(bf16[320,128]{1,0:T(8,128)(2,1)S(1)} %collective-permute-done.8.refs_2_), channel_id=1, source_target_pairs={{0,1},{1,0},{2,3},{3,2},{4,5},{5,4},{6,7},{7,6},{8,9},{9,8},{10,11... | collective-permute-start | bytes 245768 | tf_op jit(solution)/shard_map/ppermute | solution.py:402
  32.1 0.0 collective-permute-done.7.near_ref.refs_1_
  32.1 1.4 %shard_map.104.refs_9_ = f32[5,32,512]{2,1,0:T(8,128)S(1)} custom-call(f32[5,32,512]{2,1,0:T(8,128)S(1)} %get-tuple-element.34.lam_ref, bf16[3,5,32,512]{3,2,1,0:T(8,128)(2,1)S(1)} %get-tuple-element.27.saved_ref, bf16[3,512,512]{2,1,0:T(8,128)(2,1)S(1)} %get-tuple-element.28.stiff_ref, f32[1,32]{1,0:T(1,128)S(1)} %bitcast.8, ...), custom_call_target="tpu_custom_call" | custom-call | tf_op jit(solution)/shard_map/pallas_call | solution.py:382
  33.6 0.0 collective-permute-done.13.refs_7_
  33.6 0.0 collective-permute-done.11.refs_5_
  33.6 0.0 collective-permute-done.9.refs_3_
  33.6 2.2 %shard_map.105 = (f32[5,32,512]{2,1,0:T(8,128)S(1)}, bf16[320,128]{1,0:T(8,128)(2,1)S(1)}, bf16[320,256]{1,0:T(8,128)(2,1)S(1)}) custom-call(bf16[320,128]{1,0:T(8,128)(2,1)S(1)} %get-tuple-element.32.refs_0_.refs_8_, bf16[320,256]{1,0:T(8,128)(2,1)S(1)} %collective-permute-done.7.near_ref.refs_1_, bf16[320,128]{1,0:T(8,128)(2,1)S(1)} %collective-permute-done.8.refs_2_, ...), custom_call_target="tpu_custom_call" | custom-call | tf_op jit(solution)/shard_map/pallas_call | solution.py:382
  35.8 2.3 %collective-permute-start.19 = (bf16[320,128]{1,0:T(8,128)(2,1)S(1)}, bf16[320,128]{1,0:T(8,128)(2,1)S(1)}, u32[]{:S(2)}, u32[]{:S(2)}) collective-permute-start(bf16[320,128]{1,0:T(8,128)(2,1)S(1)} %get-tuple-element.36.refs_0_.refs_8_), channel_id=1, source_target_pairs={{0,6},{2,4},{4,2},{6,0},{1,7},{3,5},{5,3},{7,1},{8,14},{10,12},{12... | collective-permute-start | bytes 245768 | tf_op jit(solution)/shard_map/ppermute | solution.py:407
  38.1 0.0 collective-permute-start.14
  38.1 0.0 collective-permute-start.17
  38.1 2.2 %collective-permute-start.15 = (bf16[320,128]{1,0:T(8,128)(2,1)S(1)}, bf16[320,128]{1,0:T(8,128)(2,1)S(1)}, u32[]{:S(2)}, u32[]{:S(2)}) collective-permute-start(bf16[320,128]{1,0:T(8,128)(2,1)S(1)} %get-tuple-element.36.refs_0_.refs_8_), channel_id=1, source_target_pairs={{0,2},{2,0},{4,6},{6,4},{1,3},{3,1},{5,7},{7,5},{8,10},{10,8},{12,... | collective-permute-start | bytes 245768 | tf_op jit(solution)/shard_map/ppermute | solution.py:407
  40.2 2.7 %collective-permute-done.19.refs_6_ = bf16[320,128]{1,0:T(8,128)(2,1)S(1)} collective-permute-done((bf16[320,128]{1,0:T(8,128)(2,1)S(1)}, bf16[320,128]{1,0:T(8,128)(2,1)S(1)}, u32[]{:S(2)}, u32[]{:S(2)}) %collective-permute-start.19) | collective-permute-done | bytes 81952 | tf_op jit(solution)/shard_map/ppermute | solution.py:407
  43.0 0.0 collective-permute-start.20
  43.0 2.5 %collective-permute-done.17.refs_4_ = bf16[320,128]{1,0:T(8,128)(2,1)S(1)} collective-permute-done((bf16[320,128]{1,0:T(8,128)(2,1)S(1)}, bf16[320,128]{1,0:T(8,128)(2,1)S(1)}, u32[]{:S(2)}, u32[]{:S(2)}) %collective-permute-start.17) | collective-permute-done | bytes 81952 | tf_op jit(solution)/shard_map/ppermute | solution.py:407
  45.5 0.1 collective-permute-start.18
  45.6 0.1 collective-permute-done.15.refs_2_
  45.6 0.4 collective-permute-start.16
  46.0 0.0 collective-permute-done.14.near_ref.refs_1_
  46.0 1.4 %shard_map.106.refs_9_ = f32[5,32,512]{2,1,0:T(8,128)S(1)} custom-call(f32[5,32,512]{2,1,0:T(8,128)S(1)} %get-tuple-element.38.lam_ref, bf16[3,5,32,512]{3,2,1,0:T(8,128)(2,1)S(1)} %get-tuple-element.27.saved_ref, bf16[3,512,512]{2,1,0:T(8,128)(2,1)S(1)} %get-tuple-element.28.stiff_ref, f32[1,32]{1,0:T(1,128)S(1)} %bitcast.10, ...), custom_call_target="tpu_custom_call" | custom-call | tf_op jit(solution)/shard_map/pallas_call | solution.py:382
  47.5 0.0 collective-permute-done.20.refs_7_
  47.5 0.0 collective-permute-done.18.refs_5_
  47.5 0.0 collective-permute-done.16.refs_3_
  47.5 2.4 %shard_map.107 = f32[5,32,512]{2,1,0:T(8,128)} custom-call(bf16[320,128]{1,0:T(8,128)(2,1)S(1)} %get-tuple-element.36.refs_0_.refs_8_, bf16[320,256]{1,0:T(8,128)(2,1)S(1)} %collective-permute-done.14.near_ref.refs_1_, bf16[320,128]{1,0:T(8,128)(2,1)S(1)} %collective-permute-done.15.refs_2_, bf16[320,128]{1,0:T(8,128)(2,1)S(1)} %collective-permute-done.16.refs_3_, ...), custom_call_target="tpu_custom_call" | custom-call | tf_op jit(solution)/shard_map/pallas_call | solution.py:382
Async XLA Ops:
  0.0 17.8 %copy-start = (f32[32]{0:T(128)S(1)}, f32[32]{0:T(128)}, u32[]{:S(2)}) copy-start(f32[32]{0:T(128)} %param.12) | copy-start | bytes 388
  1.8 16.0 %collective-permute-start = (bf16[336,256]{1,0:T(8,128)(2,1)S(1)}, bf16[336,256]{1,0:T(8,128)(2,1)S(1)}, u32[]{:S(2)}, u32[]{:S(2)}) collective-permute-start(bf16[336,256]{1,0:T(8,128)(2,1)S(1)} %get-tuple-element.23.own_ref), channel_id=1, source_target_pairs={{0,1},{1,0},{2,3},{3,2},{4,5},{5,4},{6,7},{7,6},{8,9},{9,8},{10,11... | collective-permute-start | bytes 516104 | tf_op jit(solution)/shard_map/ppermute | solution.py:402
  2.4 8.1 %collective-permute-start.5 = (bf16[336,128]{1,0:T(8,128)(2,1)S(1)}, bf16[336,128]{1,0:T(8,128)(2,1)S(1)}, u32[]{:S(2)}, u32[]{:S(2)}) collective-permute-start(bf16[336,128]{1,0:T(8,128)(2,1)S(1)} %get-tuple-element.22.refs_0_.refs_8_), channel_id=1, source_target_pairs={{0,6},{2,4},{4,2},{6,0},{1,7},{3,5},{5,3},{7,1},{8,14},{10,12},{12... | collective-permute-start | bytes 258056 | tf_op jit(solution)/shard_map/ppermute | solution.py:407
  7.0 7.8 %collective-permute-start.3 = (bf16[336,128]{1,0:T(8,128)(2,1)S(1)}, bf16[336,128]{1,0:T(8,128)(2,1)S(1)}, u32[]{:S(2)}, u32[]{:S(2)}) collective-permute-start(bf16[336,128]{1,0:T(8,128)(2,1)S(1)} %get-tuple-element.22.refs_0_.refs_8_), channel_id=1, source_target_pairs={{0,4},{2,6},{4,0},{6,2},{1,5},{3,7},{5,1},{7,3},{8,12},{10,14},{12... | collective-permute-start | bytes 258056 | tf_op jit(solution)/shard_map/ppermute | solution.py:407
  7.0 7.8 %collective-permute-start.1 = (bf16[336,128]{1,0:T(8,128)(2,1)S(1)}, bf16[336,128]{1,0:T(8,128)(2,1)S(1)}, u32[]{:S(2)}, u32[]{:S(2)}) collective-permute-start(bf16[336,128]{1,0:T(8,128)(2,1)S(1)} %get-tuple-element.22.refs_0_.refs_8_), channel_id=1, source_target_pairs={{0,2},{2,0},{4,6},{6,4},{1,3},{3,1},{5,7},{7,5},{8,10},{10,8},{12,... | collective-permute-start | bytes 258056 | tf_op jit(solution)/shard_map/ppermute | solution.py:407
  10.5 8.8 %collective-permute-start.6 = (bf16[336,128]{1,0:T(8,128)(2,1)S(1)}, bf16[336,128]{1,0:T(8,128)(2,1)S(1)}, u32[]{:S(2)}, u32[]{:S(2)}) collective-permute-start(bf16[336,128]{1,0:T(8,128)(2,1)S(1)} %collective-permute-done.5.refs_6_), channel_id=1, source_target_pairs={{0,1},{1,0},{2,3},{3,2},{4,5},{5,4},{6,7},{7,6},{8,9},{9,8},{10,11... | collective-permute-start | bytes 258056 | tf_op jit(solution)/shard_map/ppermute | solution.py:402
  14.9 4.4 %collective-permute-start.4 = (bf16[336,128]{1,0:T(8,128)(2,1)S(1)}, bf16[336,128]{1,0:T(8,128)(2,1)S(1)}, u32[]{:S(2)}, u32[]{:S(2)}) collective-permute-start(bf16[336,128]{1,0:T(8,128)(2,1)S(1)} %collective-permute-done.3.refs_4_), channel_id=1, source_target_pairs={{0,1},{1,0},{2,3},{3,2},{4,5},{5,4},{6,7},{7,6},{8,9},{9,8},{10,11... | collective-permute-start | bytes 258056 | tf_op jit(solution)/shard_map/ppermute | solution.py:402
  14.9 4.5 %collective-permute-start.2 = (bf16[336,128]{1,0:T(8,128)(2,1)S(1)}, bf16[336,128]{1,0:T(8,128)(2,1)S(1)}, u32[]{:S(2)}, u32[]{:S(2)}) collective-permute-start(bf16[336,128]{1,0:T(8,128)(2,1)S(1)} %collective-permute-done.1.refs_2_), channel_id=1, source_target_pairs={{0,1},{1,0},{2,3},{3,2},{4,5},{5,4},{6,7},{7,6},{8,9},{9,8},{10,11... | collective-permute-start | bytes 258056 | tf_op jit(solution)/shard_map/ppermute | solution.py:402
  21.6 7.3 %collective-permute-start.12 = (bf16[320,128]{1,0:T(8,128)(2,1)S(1)}, bf16[320,128]{1,0:T(8,128)(2,1)S(1)}, u32[]{:S(2)}, u32[]{:S(2)}) collective-permute-start(bf16[320,128]{1,0:T(8,128)(2,1)S(1)} %get-tuple-element.32.refs_0_.refs_8_), channel_id=1, source_target_pairs={{0,6},{2,4},{4,2},{6,0},{1,7},{3,5},{5,3},{7,1},{8,14},{10,12},{12... | collective-permute-start | bytes 245768 | tf_op jit(solution)/shard_map/ppermute | solution.py:407
  24.2 8.0 %collective-permute-start.7 = (bf16[320,256]{1,0:T(8,128)(2,1)S(1)}, bf16[320,256]{1,0:T(8,128)(2,1)S(1)}, u32[]{:S(2)}, u32[]{:S(2)}) collective-permute-start(bf16[320,256]{1,0:T(8,128)(2,1)S(1)} %get-tuple-element.33.own_ref), channel_id=1, source_target_pairs={{0,1},{1,0},{2,3},{3,2},{4,5},{5,4},{6,7},{7,6},{8,9},{9,8},{10,11... | collective-permute-start | bytes 491528 | tf_op jit(solution)/shard_map/ppermute | solution.py:402
  24.2 7.4 %collective-permute-start.10 = (bf16[320,128]{1,0:T(8,128)(2,1)S(1)}, bf16[320,128]{1,0:T(8,128)(2,1)S(1)}, u32[]{:S(2)}, u32[]{:S(2)}) collective-permute-start(bf16[320,128]{1,0:T(8,128)(2,1)S(1)} %get-tuple-element.32.refs_0_.refs_8_), channel_id=1, source_target_pairs={{0,4},{2,6},{4,0},{6,2},{1,5},{3,7},{5,1},{7,3},{8,12},{10,14},{12... | collective-permute-start | bytes 245768 | tf_op jit(solution)/shard_map/ppermute | solution.py:407
  24.2 7.4 %collective-permute-start.8 = (bf16[320,128]{1,0:T(8,128)(2,1)S(1)}, bf16[320,128]{1,0:T(8,128)(2,1)S(1)}, u32[]{:S(2)}, u32[]{:S(2)}) collective-permute-start(bf16[320,128]{1,0:T(8,128)(2,1)S(1)} %get-tuple-element.32.refs_0_.refs_8_), channel_id=1, source_target_pairs={{0,2},{2,0},{4,6},{6,4},{1,3},{3,1},{5,7},{7,5},{8,10},{10,8},{12,... | collective-permute-start | bytes 245768 | tf_op jit(solution)/shard_map/ppermute | solution.py:407
  28.9 4.6 %collective-permute-start.13 = (bf16[320,128]{1,0:T(8,128)(2,1)S(1)}, bf16[320,128]{1,0:T(8,128)(2,1)S(1)}, u32[]{:S(2)}, u32[]{:S(2)}) collective-permute-start(bf16[320,128]{1,0:T(8,128)(2,1)S(1)} %collective-permute-done.12.refs_6_), channel_id=1, source_target_pairs={{0,1},{1,0},{2,3},{3,2},{4,5},{5,4},{6,7},{7,6},{8,9},{9,8},{10,11... | collective-permute-start | bytes 245768 | tf_op jit(solution)/shard_map/ppermute | solution.py:402
  31.6 2.0 %collective-permute-start.11 = (bf16[320,128]{1,0:T(8,128)(2,1)S(1)}, bf16[320,128]{1,0:T(8,128)(2,1)S(1)}, u32[]{:S(2)}, u32[]{:S(2)}) collective-permute-start(bf16[320,128]{1,0:T(8,128)(2,1)S(1)} %collective-permute-done.10.refs_4_), channel_id=1, source_target_pairs={{0,1},{1,0},{2,3},{3,2},{4,5},{5,4},{6,7},{7,6},{8,9},{9,8},{10,11... | collective-permute-start | bytes 245768 | tf_op jit(solution)/shard_map/ppermute | solution.py:402
  31.6 2.0 %collective-permute-start.9 = (bf16[320,128]{1,0:T(8,128)(2,1)S(1)}, bf16[320,128]{1,0:T(8,128)(2,1)S(1)}, u32[]{:S(2)}, u32[]{:S(2)}) collective-permute-start(bf16[320,128]{1,0:T(8,128)(2,1)S(1)} %collective-permute-done.8.refs_2_), channel_id=1, source_target_pairs={{0,1},{1,0},{2,3},{3,2},{4,5},{5,4},{6,7},{7,6},{8,9},{9,8},{10,11... | collective-permute-start | bytes 245768 | tf_op jit(solution)/shard_map/ppermute | solution.py:402
  35.8 7.2 %collective-permute-start.19 = (bf16[320,128]{1,0:T(8,128)(2,1)S(1)}, bf16[320,128]{1,0:T(8,128)(2,1)S(1)}, u32[]{:S(2)}, u32[]{:S(2)}) collective-permute-start(bf16[320,128]{1,0:T(8,128)(2,1)S(1)} %get-tuple-element.36.refs_0_.refs_8_), channel_id=1, source_target_pairs={{0,6},{2,4},{4,2},{6,0},{1,7},{3,5},{5,3},{7,1},{8,14},{10,12},{12... | collective-permute-start | bytes 245768 | tf_op jit(solution)/shard_map/ppermute | solution.py:407
  38.1 8.0 %collective-permute-start.14 = (bf16[320,256]{1,0:T(8,128)(2,1)S(1)}, bf16[320,256]{1,0:T(8,128)(2,1)S(1)}, u32[]{:S(2)}, u32[]{:S(2)}) collective-permute-start(bf16[320,256]{1,0:T(8,128)(2,1)S(1)} %get-tuple-element.37.own_ref), channel_id=1, source_target_pairs={{0,1},{1,0},{2,3},{3,2},{4,5},{5,4},{6,7},{7,6},{8,9},{9,8},{10,11... | collective-permute-start | bytes 491528 | tf_op jit(solution)/shard_map/ppermute | solution.py:402
  38.1 7.4 %collective-permute-start.17 = (bf16[320,128]{1,0:T(8,128)(2,1)S(1)}, bf16[320,128]{1,0:T(8,128)(2,1)S(1)}, u32[]{:S(2)}, u32[]{:S(2)}) collective-permute-start(bf16[320,128]{1,0:T(8,128)(2,1)S(1)} %get-tuple-element.36.refs_0_.refs_8_), channel_id=1, source_target_pairs={{0,4},{2,6},{4,0},{6,2},{1,5},{3,7},{5,1},{7,3},{8,12},{10,14},{12... | collective-permute-start | bytes 245768 | tf_op jit(solution)/shard_map/ppermute | solution.py:407
  38.1 7.6 %collective-permute-start.15 = (bf16[320,128]{1,0:T(8,128)(2,1)S(1)}, bf16[320,128]{1,0:T(8,128)(2,1)S(1)}, u32[]{:S(2)}, u32[]{:S(2)}) collective-permute-start(bf16[320,128]{1,0:T(8,128)(2,1)S(1)} %get-tuple-element.36.refs_0_.refs_8_), channel_id=1, source_target_pairs={{0,2},{2,0},{4,6},{6,4},{1,3},{3,1},{5,7},{7,5},{8,10},{10,8},{12,... | collective-permute-start | bytes 245768 | tf_op jit(solution)/shard_map/ppermute | solution.py:407
  43.0 4.5 %collective-permute-start.20 = (bf16[320,128]{1,0:T(8,128)(2,1)S(1)}, bf16[320,128]{1,0:T(8,128)(2,1)S(1)}, u32[]{:S(2)}, u32[]{:S(2)}) collective-permute-start(bf16[320,128]{1,0:T(8,128)(2,1)S(1)} %collective-permute-done.19.refs_6_), channel_id=1, source_target_pairs={{0,1},{1,0},{2,3},{3,2},{4,5},{5,4},{6,7},{7,6},{8,9},{9,8},{10,11... | collective-permute-start | bytes 245768 | tf_op jit(solution)/shard_map/ppermute | solution.py:402
  45.5 2.0 %collective-permute-start.18 = (bf16[320,128]{1,0:T(8,128)(2,1)S(1)}, bf16[320,128]{1,0:T(8,128)(2,1)S(1)}, u32[]{:S(2)}, u32[]{:S(2)}) collective-permute-start(bf16[320,128]{1,0:T(8,128)(2,1)S(1)} %collective-permute-done.17.refs_4_), channel_id=1, source_target_pairs={{0,1},{1,0},{2,3},{3,2},{4,5},{5,4},{6,7},{7,6},{8,9},{9,8},{10,11... | collective-permute-start | bytes 245768 | tf_op jit(solution)/shard_map/ppermute | solution.py:402
  45.6 1.8 %collective-permute-start.16 = (bf16[320,128]{1,0:T(8,128)(2,1)S(1)}, bf16[320,128]{1,0:T(8,128)(2,1)S(1)}, u32[]{:S(2)}, u32[]{:S(2)}) collective-permute-start(bf16[320,128]{1,0:T(8,128)(2,1)S(1)} %collective-permute-done.15.refs_2_), channel_id=1, source_target_pairs={{0,1},{1,0},{2,3},{3,2},{4,5},{5,4},{6,7},{7,6},{8,9},{9,8},{10,11... | collective-permute-start | bytes 245768 | tf_op jit(solution)/shard_map/ppermute | solution.py:402

commit v4 on v3

--- a/solution.py
+++ b/solution.py
@@ -148,8 +148,20 @@
 
 
 def slot_values(field_low, hot, table, elements):
-    faces = trace_faces(field_low, table, elements)
-    return dot(faces, hot, 0, 0).astype(BF16)[:ROWS]
+    return dot(trace_faces(field_low, table, elements), hot, 0, 0)[:ROWS]
+
+
+def pack_halves(values):
+    low = low_lanes(ROWS // 2)
+    out = []
+    for tile in range(values.shape[1] // TILE):
+        part = values[:, tile * TILE : (tile + 1) * TILE]
+        out += [x.astype(BF16) for x in exchange(part[: ROWS // 2], part[ROWS // 2 :], low)]
+    return out
+
+
+def unpack_halves(a, b):
+    return jnp.concatenate(exchange(a.astype(F32), b.astype(F32), low_lanes(ROWS // 2)), axis=0).astype(BF16)
 
 
 def fetch(pairs, sems):
@@ -194,23 +206,26 @@
     for copy in copies[3:]:
         copy.wait()
     lam_low = lam_ref[...].astype(BF16).reshape(5 * elements, ELEM)
-    values = slot_values(lam_low, hot, table_ref[...], elements)
+    values = slot_values(lam_low, hot, table_ref[...], elements).astype(BF16)
     out_ref[0:ROWS] = values[:, :slots]
     pair_ref[0:ROWS] = values
 
 
-def state_kernel(saved_hbm, stiff_hbm, forward_hbm, backward_hbm, hot_ref, table_ref, out_ref, saved_ref, stiff_ref, forward_ref, backward_ref, sems):
-    pairs = ((saved_hbm, saved_ref), (stiff_hbm, stiff_ref), (forward_hbm, forward_ref), (backward_hbm, backward_ref))
+def state_kernel(saved_hbm, stiff_hbm, forward_hbm, backward_hbm, hot_ref, table_ref, out_ref, stiff_ref, forward_ref, backward_ref, saved_ref, sems):
+    pairs = ((saved_hbm, saved_ref), (stiff_hbm.at[0 : stiff_ref.shape[0]], stiff_ref), (forward_hbm, forward_ref), (backward_hbm, backward_ref))
     copies = fetch(pairs, sems)
     copies[0].wait()
     elements = saved_ref.shape[2]
     for s in range(saved_ref.shape[0]):
-        out_ref[s] = slot_values(saved_ref[s].reshape(5 * elements, ELEM), hot_ref[...], table_ref[...], elements)
+        values = slot_values(saved_ref[s].reshape(5 * elements, ELEM), hot_ref[...], table_ref[...], elements)
+        out_ref[s] = values.astype(BF16)
     for copy in copies[1:]:
         copy.wait()
 
 
-def volume_kernel(section, slots, faces, lam_ref, saved_ref, stiff_ref, jac_ref, own_ref, near_ref, state_ref, hot_ref, table_ref, base_ref, slope_ref, smooth_ref):
+def volume_kernel(section, slots, faces, saved_hbm, stiff_hbm, lam_ref, held_ref, jac_ref, own_ref, near_ref, state_ref, hot_ref, table_ref, base_ref, slope_ref, smooth_ref, saved_ref, stiff_ref, sems):
+    held = held_ref.shape[0]
+    copies = fetch(((stiff_hbm.at[held], stiff_ref), (saved_hbm.at[section], saved_ref)), sems)
     elements = lam_ref.shape[1]
     coef = step_size * section_weights[section]
     lam_low = lam_ref[...].astype(BF16).reshape(5 * elements, ELEM)
@@ -232,16 +247,20 @@
     total = viscosity * -1.0
     smooth = lift_slots(grads, hot_ref[:, slots:], table_ref[...], elements)
     for d in range(3):
-        slopes = dot(lam_low, stiff_ref[d])
+        if d == held:
+            copies[0].wait()
+        stiff = held_ref[d] if d < held else stiff_ref[...]
+        slopes = dot(lam_low, stiff)
         slope_ref[d] = slopes
-        smooth = smooth + total * dot(slopes.astype(BF16), stiff_ref[d], 1, 1)
+        smooth = smooth + total * dot(slopes.astype(BF16), stiff, 1, 1)
     smooth_ref[...] = smooth
+    copies[1].wait()
     jac = column_of(jac_ref[...]) * coef
     step = 16
     for r in range(0, elements, step):
         scale = jnp.broadcast_to(jac[r : r + step], (step, 128))
         for c in range(0, ELEM, 128):
-            u = [saved_ref[section, v, r : r + step, c : c + 128].astype(F32) for v in range(5)]
+            u = [saved_ref[v, r : r + step, c : c + 128].astype(F32) for v in range(5)]
             inv = 1.0 / u[0]
             vel = [u[i] * inv for i in (1, 2, 3)]
             kin = 0.5 * (vel[0] * vel[0] + vel[1] * vel[1] + vel[2] * vel[2])
@@ -308,32 +327,124 @@
     return jnp.where(field == 0, code, info)
 
 
+def route(pieces, me, cap):
+    slots, devices = pieces[0].shape[1], len(pieces)
+    half = slots // 2
+    lane = lax.broadcasted_iota(jnp.int32, (devices, slots), 1)
+    device = devices - 1 - lax.broadcasted_iota(jnp.int32, (devices, slots), 0)
+    partner = jnp.zeros((devices, slots), F32)
+    for p, piece in enumerate(pieces):
+        owner = me ^ p
+        fields = piece[ROWS:].astype(F32)
+        mine = jnp.where(fields[3:4] == 1.0, fields[0:1], float(slots))
+        turned = pltpu.roll(jnp.broadcast_to(mine, (devices, slots)), lax.rem((owner + 1) * cap, slots), 1)
+        moved = pltpu.roll(turned, 0, 1, stride=cap, stride_axis=0)
+        partner = jnp.where(lane // cap == owner, moved, partner)
+    partner = partner.astype(jnp.int32)
+    chip = partner // (2 * cap)
+    wanted = [(partner < slots) & (chip == t) & (device // 2 != t) for t in range(devices // 2)]
+    wanted = jnp.concatenate([jnp.where(x, 1.0, 0.0) for x in wanted], axis=0)
+    before = lax.broadcasted_iota(jnp.int32, (slots, slots), 0) < lax.broadcasted_iota(jnp.int32, (slots, slots), 1)
+    rank = dot(wanted.astype(BF16), jnp.where(before, 1.0, 0.0).astype(BF16))
+    most = jnp.max(jnp.sum(wanted, axis=1, keepdims=True))
+    index = lax.broadcasted_iota(jnp.int32, wanted.shape, 0)
+
+    def row(x, t, q):
+        return jnp.sum(jnp.where(index == t * devices + devices - 1 - q, x, 0.0), axis=0, keepdims=True)
+
+    here = me // 2
+    place = lax.broadcasted_iota(jnp.int32, (half, slots), 0).astype(F32)
+    picks, rests = [], []
+    for k in range(1, devices // 2):
+        mine = jnp.where(row(wanted, here ^ k, me) > 0.0, row(rank, here ^ k, me), -1.0)
+        picks.append(jnp.where(place == mine, 1.0, 0.0))
+        rests.append(jnp.where(place + half == mine, 1.0, 0.0))
+    picks.append(jnp.zeros_like(picks[0]))
+    rests.append(jnp.zeros_like(picks[0]))
+    coming = [row(rank, here, me ^ p) for p in range(devices)]
+    return jnp.concatenate(picks, axis=0).astype(BF16), jnp.concatenate(rests, axis=0).astype(BF16), coming, most
+
+
+def gather_lanes(blocks, codes, start=0):
+    out = None
+    for block in blocks:
+        width = block.shape[1]
+        place = lax.broadcasted_iota(jnp.int32, (width, codes.shape[1]), 0) + start
+        part = dot(block, jnp.where(place == codes, 1.0, 0.0).astype(BF16))
+        out = part if out is None else out + part
+        start += width
+    return out
+
+
+def flag_kernel(excess_ref, flag_ref):
+    flag_ref[0] = (jnp.max(excess_ref[...]) > 0.0).astype(jnp.int32)
+
+
+def rest_kernel(sent_ref, rests_ref, *outs):
+    for out, value in zip(outs, pack_halves(dot(sent_ref[...], rests_ref[...], 1, 1))):
+        out[...] = value
+
+
+def rest_gather_kernel(info_ref, *refs):
+    blocks = [unpack_halves(refs[i][...], refs[i + 1][...]) for i in range(0, len(refs) - 1, 2)]
+    refs[-1][...] = gather_lanes(blocks, info_ref[6:7]).astype(BF16)
+
+
 def mortar_update(section, relative, first, last, count, *refs):
-    refs = list(refs)
+    compact = relative and not first
     slots = refs[count].shape[1]
-    pieces = [r[...] if len(r.shape) == 3 else r[:, :slots] for r in refs[:count]]
+    half = slots // 2
+    pieces = [r[...] if len(r.shape) == 3 or r.shape[0] < ROWS else r[:, :slots] for r in refs[:count]]
     own_ref = refs[count]
-    base_ref, state_ref, hot_ref, table_ref, jac_ref, forward_ref, backward_ref, me_ref = refs[count + 1 : count + 9]
-    outs = refs[count + 9 :]
+    base_ref, state_ref, hot_ref, table_ref, jac_ref, forward_ref, backward_ref = refs[count + 1 : count + 8]
+    me_ref, *outs = refs[count + 8 :] if first else (None,) + refs[count + 8 :]
     elements = base_ref.shape[1]
     if len(pieces) == 1 and pieces[0].ndim == 3:
         pieces = [pieces[0][p] for p in range(pieces[0].shape[0])]
     cap = slots // len(pieces)
+    hot = hot_ref[...]
     if first:
         info = read_table(pieces, me_ref, cap, relative)
-        outs[0][...] = info
-        outs = outs[1:]
     else:
         info = outs[0][...]
         outs = outs[1:]
-    _, child, axis, live, left = (jnp.broadcast_to(info[k : k + 1], (FACE, slots)) for k in range(5))
-    row = lax.broadcasted_iota(jnp.int32, (slots, slots), 0)
-    partner = None
-    for p in range(0, len(pieces), 2):
-        both = jnp.concatenate([pieces[p][:ROWS], pieces[p + 1][:ROWS]], axis=1)
-        hits = [jnp.where(row + (p + i) * slots == info[0:1], 1.0, 0.0).astype(BF16) for i in range(2)]
-        part = dot(both, jnp.concatenate(hits, axis=0))
-        partner = part if partner is None else partner + part
+    if first and relative:
+        picks, rests, coming, most = route(pieces, me_ref[0], cap)
+        extended = []
+        for piece, ranks in zip(pieces, coming):
+            extra = jnp.broadcast_to(ranks, (EXTRA, slots)).astype(BF16)
+            extended.append(jnp.concatenate([piece[:ROWS], extra], axis=0))
+        blocks = [jnp.concatenate(extended[p : p + 2], axis=1) for p in range(0, len(pieces), 2)]
+        partner = gather_lanes(blocks, info[0:1])
+        rank = partner[ROWS : ROWS + 1].astype(jnp.int32)
+        partner = partner[:ROWS]
+        piece_of = info[0:1] // slots
+        far = (piece_of >= 2) & (info[3:4] == 1)
+        packed = (piece_of - 2) * half + rank
+        near_code = jnp.where(far & (rank < half), 2 * slots + packed, jnp.where(far, -1, info[0:1]))
+        rest_code = jnp.where(far & (rank >= half), packed - half, -1)
+        field = lax.broadcasted_iota(jnp.int32, info.shape, 0)
+        info = jnp.where(field == 5, near_code, jnp.where(field == 6, rest_code, info))
+        chosen = dot(hot[:, :slots], picks, 1, 1).astype(BF16)
+        outs[1][...] = chosen
+        outs[2][...] = rests
+        outs[3][...] = jnp.full(outs[3].shape, most - half, F32)
+    elif compact:
+        blocks = [jnp.concatenate([pieces[0][:ROWS], pieces[1][:ROWS]], axis=1)]
+        blocks += [unpack_halves(pieces[p], pieces[p + 1]) for p in range(2, len(pieces), 2)]
+        partner = gather_lanes(blocks, info[5:6])
+        partner = partner + outs[0][...].astype(F32)
+        outs = outs[1:]
+        if not last:
+            chosen = outs[0][...]
+            outs = outs[1:]
+    else:
+        blocks = [jnp.concatenate([pieces[p][:ROWS], pieces[p + 1][:ROWS]], axis=1) for p in range(0, len(pieces), 2)]
+        partner = gather_lanes(blocks, info[0:1])
+    if first:
+        outs[0][...] = info
+        outs = outs[4:] if relative else outs[1:]
+    child, axis, live, left = (jnp.broadcast_to(info[k : k + 1], (FACE, slots)) for k in range(1, 5))
     is_left = left == 1
     alive = live == 1
     child = [child == c + 1 for c in range(4)]
@@ -361,29 +472,37 @@
     grads = choose(pull, spread, child, is_left)
 
     table = table_ref[...]
-    lifted = lift_slots(grads, hot_ref[:, :slots], table, elements)
+    lifted = lift_slots(grads, hot[:, :slots], table, elements)
     jac = column_of(jac_ref[...]) * (step_size * section_weights[section])
     lam = [base_ref[v] + jac * lifted[v * elements : (v + 1) * elements] for v in range(5)]
     for v in range(5):
         outs[0][v] = lam[v]
     if not last:
         lam_low = jnp.concatenate([x.astype(BF16) for x in lam], axis=0)
-        values = slot_values(lam_low, hot_ref[...], table, elements)
-        outs[1][...] = values[:, :slots]
-        outs[2][...] = values
-
-
-def call(kernel, outs, args, scratch=(), scalars=(), far=0, last=False):
+        if relative:
+            hot = jnp.concatenate([hot, chosen], axis=1)
+        values = slot_values(lam_low, hot, table, elements)
+        both = outs[2].shape[1]
+        outs[1][...] = values[:, :slots].astype(BF16)
+        outs[2][...] = values[:, :both].astype(BF16)
+        if relative:
+            for out, value in zip(outs[3:], pack_halves(values[:, both:])):
+                out[...] = value
+
+
+def call(kernel, outs, args, scratch=(), scalars=(), far=(), plain=False, final=False):
     def space(i):
-        return pltpu.HBM if i < far else pltpu.SMEM if i in scalars else pltpu.VMEM
-
-    args = [a if i in scalars else pltpu.with_memory_space_constraint(a, space(i)) for i, a in enumerate(args)]
-    shapes = [jax.ShapeDtypeStruct(o, t) if last else pltpu.VMEM(o, t) for o, t in outs]
+        return pltpu.HBM if i in far else pltpu.SMEM if i in scalars else pltpu.VMEM
+
+    if not plain:
+        args = [a if i in scalars else pltpu.with_memory_space_constraint(a, space(i)) for i, a in enumerate(args)]
+    small = [o == (1,) for o, _ in outs]
+    shapes = [jax.ShapeDtypeStruct(o, t) if plain or final or tiny else pltpu.VMEM(o, t) for (o, t), tiny in zip(outs, small)]
     return pl.pallas_call(
         kernel,
         out_shape=shapes,
         in_specs=[pl.BlockSpec(memory_space=space(i)) for i in range(len(args))],
-        out_specs=[pl.BlockSpec(memory_space=pltpu.VMEM)] * len(outs),
+        out_specs=[pl.BlockSpec(memory_space=pltpu.SMEM if tiny else pltpu.VMEM) for tiny in small],
         scratch_shapes=list(scratch),
         compiler_params=pltpu.CompilerParams(vmem_limit_bytes=VMEM_GRANT),
     )(*args)
@@ -405,6 +524,24 @@
 def send_along(x, k):
     ny = lax.axis_size("gy")
     return lax.ppermute(x, "gy", [(i, i ^ k) for i in range(ny)])
+
+
+def send_rest(sent, rests, info):
+    count = lax.axis_size("gy")
+    parts = call(rest_kernel, [((ROWS // 2, sent.shape[1]), BF16)] * (count - 1), [sent, rests], plain=True)
+    pieces = []
+    for k in range(1, count):
+        here = send_along(parts[k - 1], k)
+        pieces += [here, swap_pair(here)]
+    return call(rest_gather_kernel, [(sent.shape, BF16)], [info] + pieces, plain=True)[0]
+
+
+def clear_kernel(out_ref):
+    out_ref[...] = jnp.zeros(out_ref.shape, out_ref.dtype)
+
+
+def no_rest(sent, rests, info):
+    return call(clear_kernel, [(sent.shape, sent.dtype)], [], plain=True)[0]
 
 
 def neighbours(payload, slots, faces):
@@ -447,31 +584,42 @@
             pltpu.VMEM((8, slots + shared), jnp.int32),
             pltpu.SemaphoreType.DMA((5,)),
         ),
-        far=5,
+        far=range(5),
         scalars=(5,),
     )
-    values, states, stiffness, forward, backward = call(
+    values, held_stiff, forward, backward = call(
         state_kernel,
-        [((sections, ROWS, slots + shared), BF16), held(states), held(stiffness), held(forward), held(backward)],
+        [((sections, ROWS, slots + shared), BF16), ((2,) + stiffness.shape[1:], BF16), held(forward), held(backward)],
         [states, stiffness, forward, backward, hot, table],
-        scratch=(pltpu.SemaphoreType.DMA((4,)),),
-        far=4,
+        scratch=(pltpu.VMEM(states.shape, BF16), pltpu.SemaphoreType.DMA((4,))),
+        far=range(4),
     )
-    info = None
+    count = lax.axis_size("gy")
+    parts = [outgoing] * (count - 1)
+    packed = ((ROWS // 2, slots), BF16)
+    chosen_shape = ((6 * elements, count * slots // 2), BF16)
+    rests_shape = ((count * slots // 2, slots), BF16)
     for section in (2, 1, 0):
         relative = paired()
         if relative:
-            column = [None] * (lax.axis_size("gy") - 1)
+            column = [None] * (count - 1)
             for k in reversed(range(len(column))):
-                column[k] = send_along(outgoing, k + 1)
+                column[k] = send_along(parts[k], k + 1)
             near = swap_pair(both)
         else:
             near = neighbours(both, slots, faces)
         (base,) = call(
             functools.partial(volume_kernel, section, slots, faces),
             [rows],
-            [lam, states, stiffness, jac, both, near, values, hot, table],
-            scratch=(pltpu.VMEM((3, 5 * elements, ELEM), F32), pltpu.VMEM((5 * elements, ELEM), F32)),
+            [states, stiffness, lam, held_stiff, jac, both, near, values, hot, table],
+            scratch=(
+                pltpu.VMEM((3, 5 * elements, ELEM), F32),
+                pltpu.VMEM((5 * elements, ELEM), F32),
+                pltpu.VMEM(states.shape[1:], BF16),
+                pltpu.VMEM(stiffness.shape[1:], BF16),
+                pltpu.SemaphoreType.DMA((2,)),
+            ),
+            far=(0, 1),
         )
         if relative:
             pieces = [outgoing, near]
@@ -480,17 +628,29 @@
         else:
             pieces = [lax.all_gather(outgoing, ("gy", "gz"), axis=0, tiled=False)]
         first, last = section == sections - 1, section == 0
-        outs = ([info_shape] if first else []) + [rows] + ([] if last else [sent, pair])
-        args = pieces + [outgoing, base, values, hot, table, jac, forward, backward, me] + ([] if first else [info])
+        outs = [rows]
+        if not last:
+            outs += [sent, pair] + ([packed] * (count - 1) if relative else [])
+        if first:
+            outs = [info_shape] + ([chosen_shape, rests_shape, ((8, 128), F32)] if relative else []) + outs
+        args = pieces + [outgoing, base, values, hot, table, jac, forward, backward]
+        scalars = (len(args),) if first else ()
+        args.append(me if first else info)
+        if relative and not first:
+            args.append(lax.cond(flag[0] > 0, send_rest, no_rest, outgoing, rests, info))
+            args += [] if last else [chosen]
         out = call(
             functools.partial(mortar_update, section, relative, first, last, len(pieces)),
-            outs, args, scalars=(len(pieces) + 8,), last=last,
+            outs, args, scalars=scalars, final=last,
         )
         if first:
             info, out = out[0], out[1:]
+            if relative:
+                (chosen, rests, excess), out = out[:3], out[3:]
+                (flag,) = call(flag_kernel, [((1,), jnp.int32)], [excess])
         lam = out[0]
         if not last:
-            outgoing, both = out[1:]
+            outgoing, both, parts = out[1], out[2], out[3:]
     return jnp.transpose(lam, (1, 0, 2))
 
 

time: 50.1 us -> 49.2 us (0.982)
  waiting for transfers between devices: 18.1 us -> 15 us
  Pallas kernels: 15.4 us -> 17 us
  between operations: 0.15 us -> 0.84 us
    ppermute x9, waiting for transfers between devices: 18 us -> 14.9 us  [send_along(): return lax.ppermute(x, 'gy', [(i, i ^ k) for i in range(ny)])]
    pallas_call x8 -> x11, Pallas kernels: 15.4 us -> 17 us  [call(): pl.pallas_call(kernel, out_shape=shapes, in_specs=[pl.BlockSpec(memory_sp...]
  transfers between devices with their start and end apart: 21 -> 21, of which waited for: 7 -> 6; matrix products, arithmetic and copies ran while one was open for 0% -> 0% of each run, Pallas kernels for 14% -> 17%
where the time goes in v4:
time: 49.2 us; the launch traced here: 49 us
  Pallas kernels  17 us (35%)
  starting transfers between devices  16 us (33%)
  waiting for transfers between devices  15 us (30%)
  between operations  0.84 us (2%)
    pallas_call x11, Pallas kernels, call(): pl.pallas_call(kernel, out_shape=shapes, in_specs=[pl.BlockSpec(memory_sp...  17 us
    ppermute x9, waiting for transfers between devices, send_along(): return lax.ppermute(x, 'gy', [(i, i ^ k) for i in range(ny)])  14.9 us
    ppermute x9, starting transfers between devices, send_along(): return lax.ppermute(x, 'gy', [(i, i ^ k) for i in range(ny)])  14.3 us
    ppermute x12, starting transfers between devices, swap_pair(): return lax.ppermute(x, 'gz', [(0, 1), (1, 0)])  1.73 us
  transfers between devices with their start and end apart: 21, of which 6 were waited for; matrix products, arithmetic and copies ran while one was open for 0% of the time, Pallas kernels for 17%

profile of v4, /device:TPU:0, one launch (start us, length us, event | category | flops | bytes accessed | tf_op | source)
XLA Modules:
  0.0 49.0 jit_solution(6916145692507359710)
XLA Ops:
  0.0 0.0 copy-start
  0.0 1.8 %shard_map.100 = (bf16[336,128]{1,0:T(8,128)(2,1)S(1)}, bf16[336,256]{1,0:T(8,128)(2,1)S(1)}, bf16[192,256]{1,0:T(8,128)(2,1)S(1)}, f32[5,32,512]{2,1,0:T(8,128)S(1)}, bf16[512,384]{1,0:T(8,128)(2,1)S(1)}) custom-call(f32[5,32,512]{2,1,0:T(8,128)} %bitcast.17, s32[1,128]{1,0:T(1,128)} %send_hbm.1, s32[1,2,16]{2,1,0:T(2,128)} %conf_hbm.1, ...), custom_call_target="tpu_custom_call" | custom-call | tf_op jit(solution)/shard_map/pallas_call | solution.py:501
  1.8 0.6 %collective-permute-start.12 = (bf16[336,256]{1,0:T(8,128)(2,1)S(1)}, bf16[336,256]{1,0:T(8,128)(2,1)S(1)}, u32[]{:S(2)}, u32[]{:S(2)}) collective-permute-start(bf16[336,256]{1,0:T(8,128)(2,1)S(1)} %get-tuple-element.61.own_ref), channel_id=1, source_target_pairs={{0,1},{1,0},{2,3},{3,2},{4,5},{5,4},{6,7},{7,6},{8,9},{9,8},{10,11... | collective-permute-start | bytes 516104 | tf_op jit(solution)/shard_map/ppermute | solution.py:521
  2.4 4.7 %collective-permute-start.17 = (bf16[336,128]{1,0:T(8,128)(2,1)S(1)}, bf16[336,128]{1,0:T(8,128)(2,1)S(1)}, u32[]{:S(2)}, u32[]{:S(2)}) collective-permute-start(bf16[336,128]{1,0:T(8,128)(2,1)S(1)} %get-tuple-element.60.refs_0_.refs_8_), channel_id=1, source_target_pairs={{0,6},{2,4},{4,2},{6,0},{1,7},{3,5},{5,3},{7,1},{8,14},{10,12},{12... | collective-permute-start | bytes 258056 | tf_op jit(solution)/shard_map/ppermute | solution.py:526
  7.0 0.0 collective-permute-start.15
  7.0 0.6 %collective-permute-start.13 = (bf16[336,128]{1,0:T(8,128)(2,1)S(1)}, bf16[336,128]{1,0:T(8,128)(2,1)S(1)}, u32[]{:S(2)}, u32[]{:S(2)}) collective-permute-start(bf16[336,128]{1,0:T(8,128)(2,1)S(1)} %get-tuple-element.60.refs_0_.refs_8_), channel_id=1, source_target_pairs={{0,2},{2,0},{4,6},{6,4},{1,3},{3,1},{5,7},{7,5},{8,10},{10,8},{12,... | collective-permute-start | bytes 258056 | tf_op jit(solution)/shard_map/ppermute | solution.py:526
  7.7 2.8 %collective-permute-done.17.refs_6_ = bf16[336,128]{1,0:T(8,128)(2,1)S(1)} collective-permute-done((bf16[336,128]{1,0:T(8,128)(2,1)S(1)}, bf16[336,128]{1,0:T(8,128)(2,1)S(1)}, u32[]{:S(2)}, u32[]{:S(2)}) %collective-permute-start.17) | collective-permute-done | bytes 86048 | tf_op jit(solution)/shard_map/ppermute | solution.py:526
  10.5 0.0 collective-permute-start.18
  10.5 4.3 %collective-permute-done.15.refs_4_ = bf16[336,128]{1,0:T(8,128)(2,1)S(1)} collective-permute-done((bf16[336,128]{1,0:T(8,128)(2,1)S(1)}, bf16[336,128]{1,0:T(8,128)(2,1)S(1)}, u32[]{:S(2)}, u32[]{:S(2)}) %collective-permute-start.15) | collective-permute-done | bytes 86048 | tf_op jit(solution)/shard_map/ppermute | solution.py:526
  14.9 0.0 collective-permute-start.16
  14.9 0.0 collective-permute-done.13.refs_2_
  14.9 0.5 %collective-permute-start.14 = (bf16[336,128]{1,0:T(8,128)(2,1)S(1)}, bf16[336,128]{1,0:T(8,128)(2,1)S(1)}, u32[]{:S(2)}, u32[]{:S(2)}) collective-permute-start(bf16[336,128]{1,0:T(8,128)(2,1)S(1)} %collective-permute-done.13.refs_2_), channel_id=1, source_target_pairs={{0,1},{1,0},{2,3},{3,2},{4,5},{5,4},{6,7},{7,6},{8,9},{9,8},{10,11... | collective-permute-start | bytes 258056 | tf_op jit(solution)/shard_map/ppermute | solution.py:521
  15.4 2.4 %shard_map.101 = (bf16[3,320,256]{2,1,0:T(8,128)(2,1)S(1)}, bf16[2,512,512]{2,1,0:T(8,128)(2,1)S(1)}, bf16[256,128]{1,0:T(8,128)(2,1)S(1)}, bf16[256,192]{1,0:T(8,128)(2,1)S(1)}) custom-call(bf16[3,5,32,512]{3,2,1,0:T(8,128)(2,1)} %bitcast.13, bf16[3,512,512]{2,1,0:T(8,128)(2,1)} %stiff_hbm.7, bf16[256,128]{1,0:T(8,128)(2,1)} %constant.20.clone.forward_hbm, ...), custom_call_target="tpu_custom_call" | custom-call | tf_op jit(solution)/shard_map/pallas_call | solution.py:501
  17.8 0.0 collective-permute-done.12.near_ref.refs_1_
  17.8 0.0 copy-done
  17.8 1.8 %shard_map.102.refs_9_ = f32[5,32,512]{2,1,0:T(8,128)S(1)} custom-call(bf16[3,5,32,512]{3,2,1,0:T(8,128)(2,1)} %bitcast.14, bf16[3,512,512]{2,1,0:T(8,128)(2,1)} %stiff_hbm.7, f32[5,32,512]{2,1,0:T(8,128)S(1)} %get-tuple-element.62.lam_ref, bf16[2,512,512]{2,1,0:T(8,128)(2,1)S(1)} %get-tuple-element.65.held_ref, f32[1,32]{1,0:T(1,128)S(1)} %bitcast.7, ...), custom_call_target="tpu_custom_call" | custom-call | tf_op jit(solution)/shard_map/pallas_call | solution.py:501
  19.6 0.0 collective-permute-done.18.refs_7_
  19.7 0.0 collective-permute-done.16.refs_5_
  19.7 0.0 collective-permute-done.14.refs_3_
  19.7 2.5 %shard_map.103 = (s32[16,128]{1,0:T(8,128)S(1)}, bf16[192,256]{1,0:T(8,128)(2,1)S(1)}, bf16[256,128]{1,0:T(8,128)(2,1)S(1)}, f32[8,128]{1,0:T(8,128)S(1)}, f32[5...) custom-call(bf16[336,128]{1,0:T(8,128)(2,1)S(1)} %get-tuple-element., ...), custom_call_target="tpu_custom_call" | custom-call | tf_op jit(solution)/shard_map/pallas_call | solution.py:501
  22.2 0.1 collective-permute-start.19
  22.3 0.6 %shard_map.105 = s32[1]{0:T(128)} custom-call(f32[8,128]{1,0:T(8,128)S(1)} %get-tuple-element.76.excess_ref), custom_call_target="tpu_custom_call" | custom-call | tf_op jit(solution)/shard_map/pallas_call | solution.py:501
  23.6 0.8 %collective-permute-start.20 = (bf16[160,128]{1,0:T(8,128)(2,1)S(1)}, bf16[160,128]{1,0:T(8,128)(2,1)S(1)}, u32[]{:S(2)}, u32[]{:S(2)}) collective-permute-start(bf16[160,128]{1,0:T(8,128)(2,1)S(1)} %get-tuple-element.71), channel_id=1, source_target_pairs={{0,2},{2,0},{4,6},{6,4},{1,3},{3,1},{5,7},{7,5},{8,10},{10,8},{12,... | collective-permute-start | bytes 122888 | tf_op jit(solution)/shard_map/ppermute | solution.py:526
  24.5 2.3 %collective-permute-start.22 = (bf16[160,128]{1,0:T(8,128)(2,1)S(1)}, bf16[160,128]{1,0:T(8,128)(2,1)S(1)}, u32[]{:S(2)}, u32[]{:S(2)}) collective-permute-start(bf16[160,128]{1,0:T(8,128)(2,1)S(1)} %get-tuple-element.72), channel_id=1, source_target_pairs={{0,4},{2,6},{4,0},{6,2},{1,5},{3,7},{5,1},{7,3},{8,12},{10,14},{12... | collective-permute-start | bytes 122888 | tf_op jit(solution)/shard_map/ppermute | solution.py:526
  26.8 1.3 %collective-permute-start.24 = (bf16[160,128]{1,0:T(8,128)(2,1)S(1)}, bf16[160,128]{1,0:T(8,128)(2,1)S(1)}, u32[]{:S(2)}, u32[]{:S(2)}) collective-permute-start(bf16[160,128]{1,0:T(8,128)(2,1)S(1)} %get-tuple-element.73), channel_id=1, source_target_pairs={{0,6},{2,4},{4,2},{6,0},{1,7},{3,5},{5,3},{7,1},{8,14},{10,12},{12... | collective-permute-start | bytes 122888 | tf_op jit(solution)/shard_map/ppermute | solution.py:526
  28.1 0.0 collective-permute-done.20.refs_2_
  28.1 0.0 collective-permute-start.21
  28.1 2.5 %collective-permute-done.22.refs_4_ = bf16[160,128]{1,0:T(8,128)(2,1)S(1)} collective-permute-done((bf16[160,128]{1,0:T(8,128)(2,1)S(1)}, bf16[160,128]{1,0:T(8,128)(2,1)S(1)}, u32[]{:S(2)}, u32[]{:S(2)}) %collective-permute-start.22) | collective-permute-done | bytes 40992 | tf_op jit(solution)/shard_map/ppermute | solution.py:526
  30.7 0.0 collective-permute-start.23
  30.7 1.9 %collective-permute-done.24.refs_6_ = bf16[160,128]{1,0:T(8,128)(2,1)S(1)} collective-permute-done((bf16[160,128]{1,0:T(8,128)(2,1)S(1)}, bf16[160,128]{1,0:T(8,128)(2,1)S(1)}, u32[]{:S(2)}, u32[]{:S(2)}) %collective-permute-start.24) | collective-permute-done | bytes 40992 | tf_op jit(solution)/shard_map/ppermute | solution.py:526
  32.6 0.0 collective-permute-start.25
  32.6 0.0 collective-permute-done.19.near_ref.refs_1_
  32.6 1.8 %shard_map.104.refs_9_ = f32[5,32,512]{2,1,0:T(8,128)S(1)} custom-call(bf16[3,5,32,512]{3,2,1,0:T(8,128)(2,1)} %bitcast.15, bf16[3,512,512]{2,1,0:T(8,128)(2,1)} %stiff_hbm.7, f32[5,32,512]{2,1,0:T(8,128)S(1)} %get-tuple-element.74.lam_ref, bf16[2,512,512]{2,1,0:T(8,128)(2,1)S(1)} %get-tuple-element.65.held_ref, f32[1,32]{1,0:T(1,128)S(1)} %bitcast.9, ...), custom_call_target="tpu_custom_call" | custom-call | tf_op jit(solution)/shard_map/pallas_call | solution.py:501
  34.4 0.0 collective-permute-done.21.refs_3_
  34.4 0.0 collective-permute-done.23.refs_5_
  34.4 0.0 collective-permute-done.25.refs_7_
  34.4 2.0 %shard_map.106 = (f32[5,32,512]{2,1,0:T(8,128)S(1)}, bf16[320,128]{1,0:T(8,128)(2,1)S(1)}, bf16[320,256]{1,0:T(8,128)(2,1)S(1)}, bf16[160,128]{1,0:T(8,128)(2,1)...) custom-call(bf16[320,128]{1,0:T(8,128)(2,1)S(1)} %get-tuple-element.69.refs_0_.refs_8_, ...), custom_call_target="tpu_custom_call" | custom-call | tf_op jit(solution)/shard_map/pallas_call | solution.py:501
  36.4 0.6 %collective-permute-start.26 = (bf16[320,256]{1,0:T(8,128)(2,1)S(1)}, bf16[320,256]{1,0:T(8,128)(2,1)S(1)}, u32[]{:S(2)}, u32[]{:S(2)}) collective-permute-start(bf16[320,256]{1,0:T(8,128)(2,1)S(1)} %get-tuple-element.80.own_ref), channel_id=1, source_target_pairs={{0,1},{1,0},{2,3},{3,2},{4,5},{5,4},{6,7},{7,6},{8,9},{9,8},{10,11... | collective-permute-start | bytes 491528 | tf_op jit(solution)/shard_map/ppermute | solution.py:521
  37.0 0.0 collective-permute-start.27
  37.0 0.2 conditional.3
  37.2 2.0 %collective-permute-start.29 = (bf16[160,128]{1,0:T(8,128)(2,1)S(1)}, bf16[160,128]{1,0:T(8,128)(2,1)S(1)}, u32[]{:S(2)}, u32[]{:S(2)}) collective-permute-start(bf16[160,128]{1,0:T(8,128)(2,1)S(1)} %get-tuple-element.82), channel_id=1, source_target_pairs={{0,4},{2,6},{4,0},{6,2},{1,5},{3,7},{5,1},{7,3},{8,12},{10,14},{12... | collective-permute-start | bytes 122888 | tf_op jit(solution)/shard_map/ppermute | solution.py:526
  39.2 2.5 %collective-permute-start.31 = (bf16[160,128]{1,0:T(8,128)(2,1)S(1)}, bf16[160,128]{1,0:T(8,128)(2,1)S(1)}, u32[]{:S(2)}, u32[]{:S(2)}) collective-permute-start(bf16[160,128]{1,0:T(8,128)(2,1)S(1)} %get-tuple-element.83), channel_id=1, source_target_pairs={{0,6},{2,4},{4,2},{6,0},{1,7},{3,5},{5,3},{7,1},{8,14},{10,12},{12... | collective-permute-start | bytes 122888 | tf_op jit(solution)/shard_map/ppermute | solution.py:526
  41.7 0.0 collective-permute-done.27.refs_2_
  41.7 0.0 collective-permute-start.28
  41.7 1.0 %collective-permute-done.29.refs_4_ = bf16[160,128]{1,0:T(8,128)(2,1)S(1)} collective-permute-done((bf16[160,128]{1,0:T(8,128)(2,1)S(1)}, bf16[160,128]{1,0:T(8,128)(2,1)S(1)}, u32[]{:S(2)}, u32[]{:S(2)}) %collective-permute-start.29) | collective-permute-done | bytes 40992 | tf_op jit(solution)/shard_map/ppermute | solution.py:526
  42.6 0.0 collective-permute-start.30
  42.6 2.4 %collective-permute-done.31.refs_6_ = bf16[160,128]{1,0:T(8,128)(2,1)S(1)} collective-permute-done((bf16[160,128]{1,0:T(8,128)(2,1)S(1)}, bf16[160,128]{1,0:T(8,128)(2,1)S(1)}, u32[]{:S(2)}, u32[]{:S(2)}) %collective-permute-start.31) | collective-permute-done | bytes 40992 | tf_op jit(solution)/shard_map/ppermute | solution.py:526
  45.0 0.0 collective-permute-start.32
  45.0 0.0 collective-permute-done.26.near_ref.refs_1_
  45.0 1.8 %shard_map.107.refs_9_ = f32[5,32,512]{2,1,0:T(8,128)S(1)} custom-call(bf16[3,5,32,512]{3,2,1,0:T(8,128)(2,1)} %bitcast.16, bf16[3,512,512]{2,1,0:T(8,128)(2,1)} %stiff_hbm.7, f32[5,32,512]{2,1,0:T(8,128)S(1)} %get-tuple-element.84.lam_ref, bf16[2,512,512]{2,1,0:T(8,128)(2,1)S(1)} %get-tuple-element.65.held_ref, f32[1,32]{1,0:T(1,128)S(1)} %bitcast.11, ...), custom_call_target="tpu_custom_call" | custom-call | tf_op jit(solution)/shard_map/pallas_call | solution.py:501
  46.8 0.0 collective-permute-done.28.refs_3_
  46.8 0.0 collective-permute-done.30.refs_5_
  46.8 0.0 collective-permute-done.32.refs_7_
  46.8 2.1 %shard_map.108 = f32[5,32,512]{2,1,0:T(8,128)} custom-call(bf16[320,128]{1,0:T(8,128)(2,1)S(1)} %get-tuple-element.79.refs_0_.refs_8_, bf16[320,256]{1,0:T(8,128)(2,1)S(1)} %collective-permute-done.26.near_ref.refs_1_, bf16[160,128]{1,0:T(8,128)(2,1)S(1)} %collective-permute-done.27.refs_2_, bf16[160,128]{1,0:T(8,128)(2,1)S(1)} %collective-permute-done.28.refs_3_, ...), custom_call_target="tpu_custom_call" | custom-call | tf_op jit(solution)/shard_map/pallas_call | solution.py:501
  (3 shorter events, 0.0 us)
Async XLA Ops:
  0.0 17.8 %copy-start = (f32[32]{0:T(128)S(1)}, f32[32]{0:T(128)}, u32[]{:S(2)}) copy-start(f32[32]{0:T(128)} %param.16) | copy-start | bytes 388
  1.8 16.0 %collective-permute-start.12 = (bf16[336,256]{1,0:T(8,128)(2,1)S(1)}, bf16[336,256]{1,0:T(8,128)(2,1)S(1)}, u32[]{:S(2)}, u32[]{:S(2)}) collective-permute-start(bf16[336,256]{1,0:T(8,128)(2,1)S(1)} %get-tuple-element.61.own_ref), channel_id=1, source_target_pairs={{0,1},{1,0},{2,3},{3,2},{4,5},{5,4},{6,7},{7,6},{8,9},{9,8},{10,11... | collective-permute-start | bytes 516104 | tf_op jit(solution)/shard_map/ppermute | solution.py:521
  2.4 8.2 %collective-permute-start.17 = (bf16[336,128]{1,0:T(8,128)(2,1)S(1)}, bf16[336,128]{1,0:T(8,128)(2,1)S(1)}, u32[]{:S(2)}, u32[]{:S(2)}) collective-permute-start(bf16[336,128]{1,0:T(8,128)(2,1)S(1)} %get-tuple-element.60.refs_0_.refs_8_), channel_id=1, source_target_pairs={{0,6},{2,4},{4,2},{6,0},{1,7},{3,5},{5,3},{7,1},{8,14},{10,12},{12... | collective-permute-start | bytes 258056 | tf_op jit(solution)/shard_map/ppermute | solution.py:526
  7.0 7.8 %collective-permute-start.15 = (bf16[336,128]{1,0:T(8,128)(2,1)S(1)}, bf16[336,128]{1,0:T(8,128)(2,1)S(1)}, u32[]{:S(2)}, u32[]{:S(2)}) collective-permute-start(bf16[336,128]{1,0:T(8,128)(2,1)S(1)} %get-tuple-element.60.refs_0_.refs_8_), channel_id=1, source_target_pairs={{0,4},{2,6},{4,0},{6,2},{1,5},{3,7},{5,1},{7,3},{8,12},{10,14},{12... | collective-permute-start | bytes 258056 | tf_op jit(solution)/shard_map/ppermute | solution.py:526
  7.0 7.8 %collective-permute-start.13 = (bf16[336,128]{1,0:T(8,128)(2,1)S(1)}, bf16[336,128]{1,0:T(8,128)(2,1)S(1)}, u32[]{:S(2)}, u32[]{:S(2)}) collective-permute-start(bf16[336,128]{1,0:T(8,128)(2,1)S(1)} %get-tuple-element.60.refs_0_.refs_8_), channel_id=1, source_target_pairs={{0,2},{2,0},{4,6},{6,4},{1,3},{3,1},{5,7},{7,5},{8,10},{10,8},{12,... | collective-permute-start | bytes 258056 | tf_op jit(solution)/shard_map/ppermute | solution.py:526
  10.5 9.1 %collective-permute-start.18 = (bf16[336,128]{1,0:T(8,128)(2,1)S(1)}, bf16[336,128]{1,0:T(8,128)(2,1)S(1)}, u32[]{:S(2)}, u32[]{:S(2)}) collective-permute-start(bf16[336,128]{1,0:T(8,128)(2,1)S(1)} %collective-permute-done.17.refs_6_), channel_id=1, source_target_pairs={{0,1},{1,0},{2,3},{3,2},{4,5},{5,4},{6,7},{7,6},{8,9},{9,8},{10,11... | collective-permute-start | bytes 258056 | tf_op jit(solution)/shard_map/ppermute | solution.py:521
  14.9 4.8 %collective-permute-start.16 = (bf16[336,128]{1,0:T(8,128)(2,1)S(1)}, bf16[336,128]{1,0:T(8,128)(2,1)S(1)}, u32[]{:S(2)}, u32[]{:S(2)}) collective-permute-start(bf16[336,128]{1,0:T(8,128)(2,1)S(1)} %collective-permute-done.15.refs_4_), channel_id=1, source_target_pairs={{0,1},{1,0},{2,3},{3,2},{4,5},{5,4},{6,7},{7,6},{8,9},{9,8},{10,11... | collective-permute-start | bytes 258056 | tf_op jit(solution)/shard_map/ppermute | solution.py:521
  14.9 4.8 %collective-permute-start.14 = (bf16[336,128]{1,0:T(8,128)(2,1)S(1)}, bf16[336,128]{1,0:T(8,128)(2,1)S(1)}, u32[]{:S(2)}, u32[]{:S(2)}) collective-permute-start(bf16[336,128]{1,0:T(8,128)(2,1)S(1)} %collective-permute-done.13.refs_2_), channel_id=1, source_target_pairs={{0,1},{1,0},{2,3},{3,2},{4,5},{5,4},{6,7},{7,6},{8,9},{9,8},{10,11... | collective-permute-start | bytes 258056 | tf_op jit(solution)/shard_map/ppermute | solution.py:521
  22.2 10.4 %collective-permute-start.19 = (bf16[320,256]{1,0:T(8,128)(2,1)S(1)}, bf16[320,256]{1,0:T(8,128)(2,1)S(1)}, u32[]{:S(2)}, u32[]{:S(2)}) collective-permute-start(bf16[320,256]{1,0:T(8,128)(2,1)S(1)} %get-tuple-element.70.own_ref), channel_id=1, source_target_pairs={{0,1},{1,0},{2,3},{3,2},{4,5},{5,4},{6,7},{7,6},{8,9},{9,8},{10,11... | collective-permute-start | bytes 491528 | tf_op jit(solution)/shard_map/ppermute | solution.py:521
  23.6 4.5 %collective-permute-start.20 = (bf16[160,128]{1,0:T(8,128)(2,1)S(1)}, bf16[160,128]{1,0:T(8,128)(2,1)S(1)}, u32[]{:S(2)}, u32[]{:S(2)}) collective-permute-start(bf16[160,128]{1,0:T(8,128)(2,1)S(1)} %get-tuple-element.71), channel_id=1, source_target_pairs={{0,2},{2,0},{4,6},{6,4},{1,3},{3,1},{5,7},{7,5},{8,10},{10,8},{12,... | collective-permute-start | bytes 122888 | tf_op jit(solution)/shard_map/ppermute | solution.py:526
  24.5 6.2 %collective-permute-start.22 = (bf16[160,128]{1,0:T(8,128)(2,1)S(1)}, bf16[160,128]{1,0:T(8,128)(2,1)S(1)}, u32[]{:S(2)}, u32[]{:S(2)}) collective-permute-start(bf16[160,128]{1,0:T(8,128)(2,1)S(1)} %get-tuple-element.72), channel_id=1, source_target_pairs={{0,4},{2,6},{4,0},{6,2},{1,5},{3,7},{5,1},{7,3},{8,12},{10,14},{12... | collective-permute-start | bytes 122888 | tf_op jit(solution)/shard_map/ppermute | solution.py:526
  26.8 5.8 %collective-permute-start.24 = (bf16[160,128]{1,0:T(8,128)(2,1)S(1)}, bf16[160,128]{1,0:T(8,128)(2,1)S(1)}, u32[]{:S(2)}, u32[]{:S(2)}) collective-permute-start(bf16[160,128]{1,0:T(8,128)(2,1)S(1)} %get-tuple-element.73), channel_id=1, source_target_pairs={{0,6},{2,4},{4,2},{6,0},{1,7},{3,5},{5,3},{7,1},{8,14},{10,12},{12... | collective-permute-start | bytes 122888 | tf_op jit(solution)/shard_map/ppermute | solution.py:526
  28.1 6.3 %collective-permute-start.21 = (bf16[160,128]{1,0:T(8,128)(2,1)S(1)}, bf16[160,128]{1,0:T(8,128)(2,1)S(1)}, u32[]{:S(2)}, u32[]{:S(2)}) collective-permute-start(bf16[160,128]{1,0:T(8,128)(2,1)S(1)} %collective-permute-done.20.refs_2_), channel_id=1, source_target_pairs={{0,1},{1,0},{2,3},{3,2},{4,5},{5,4},{6,7},{7,6},{8,9},{9,8},{10,11... | collective-permute-start | bytes 122888 | tf_op jit(solution)/shard_map/ppermute | solution.py:521
  30.7 3.7 %collective-permute-start.23 = (bf16[160,128]{1,0:T(8,128)(2,1)S(1)}, bf16[160,128]{1,0:T(8,128)(2,1)S(1)}, u32[]{:S(2)}, u32[]{:S(2)}) collective-permute-start(bf16[160,128]{1,0:T(8,128)(2,1)S(1)} %collective-permute-done.22.refs_4_), channel_id=1, source_target_pairs={{0,1},{1,0},{2,3},{3,2},{4,5},{5,4},{6,7},{7,6},{8,9},{9,8},{10,11... | collective-permute-start | bytes 122888 | tf_op jit(solution)/shard_map/ppermute | solution.py:521
  32.6 1.8 %collective-permute-start.25 = (bf16[160,128]{1,0:T(8,128)(2,1)S(1)}, bf16[160,128]{1,0:T(8,128)(2,1)S(1)}, u32[]{:S(2)}, u32[]{:S(2)}) collective-permute-start(bf16[160,128]{1,0:T(8,128)(2,1)S(1)} %collective-permute-done.24.refs_6_), channel_id=1, source_target_pairs={{0,1},{1,0},{2,3},{3,2},{4,5},{5,4},{6,7},{7,6},{8,9},{9,8},{10,11... | collective-permute-start | bytes 122888 | tf_op jit(solution)/shard_map/ppermute | solution.py:521
  36.4 8.6 %collective-permute-start.26 = (bf16[320,256]{1,0:T(8,128)(2,1)S(1)}, bf16[320,256]{1,0:T(8,128)(2,1)S(1)}, u32[]{:S(2)}, u32[]{:S(2)}) collective-permute-start(bf16[320,256]{1,0:T(8,128)(2,1)S(1)} %get-tuple-element.80.own_ref), channel_id=1, source_target_pairs={{0,1},{1,0},{2,3},{3,2},{4,5},{5,4},{6,7},{7,6},{8,9},{9,8},{10,11... | collective-permute-start | bytes 491528 | tf_op jit(solution)/shard_map/ppermute | solution.py:521
  37.0 4.7 %collective-permute-start.27 = (bf16[160,128]{1,0:T(8,128)(2,1)S(1)}, bf16[160,128]{1,0:T(8,128)(2,1)S(1)}, u32[]{:S(2)}, u32[]{:S(2)}) collective-permute-start(bf16[160,128]{1,0:T(8,128)(2,1)S(1)} %get-tuple-element.81), channel_id=1, source_target_pairs={{0,2},{2,0},{4,6},{6,4},{1,3},{3,1},{5,7},{7,5},{8,10},{10,8},{12,... | collective-permute-start | bytes 122888 | tf_op jit(solution)/shard_map/ppermute | solution.py:526
  37.2 5.4 %collective-permute-start.29 = (bf16[160,128]{1,0:T(8,128)(2,1)S(1)}, bf16[160,128]{1,0:T(8,128)(2,1)S(1)}, u32[]{:S(2)}, u32[]{:S(2)}) collective-permute-start(bf16[160,128]{1,0:T(8,128)(2,1)S(1)} %get-tuple-element.82), channel_id=1, source_target_pairs={{0,4},{2,6},{4,0},{6,2},{1,5},{3,7},{5,1},{7,3},{8,12},{10,14},{12... | collective-permute-start | bytes 122888 | tf_op jit(solution)/shard_map/ppermute | solution.py:526
  39.2 5.8 %collective-permute-start.31 = (bf16[160,128]{1,0:T(8,128)(2,1)S(1)}, bf16[160,128]{1,0:T(8,128)(2,1)S(1)}, u32[]{:S(2)}, u32[]{:S(2)}) collective-permute-start(bf16[160,128]{1,0:T(8,128)(2,1)S(1)} %get-tuple-element.83), channel_id=1, source_target_pairs={{0,6},{2,4},{4,2},{6,0},{1,7},{3,5},{5,3},{7,1},{8,14},{10,12},{12... | collective-permute-start | bytes 122888 | tf_op jit(solution)/shard_map/ppermute | solution.py:526
  41.7 5.1 %collective-permute-start.28 = (bf16[160,128]{1,0:T(8,128)(2,1)S(1)}, bf16[160,128]{1,0:T(8,128)(2,1)S(1)}, u32[]{:S(2)}, u32[]{:S(2)}) collective-permute-start(bf16[160,128]{1,0:T(8,128)(2,1)S(1)} %collective-permute-done.27.refs_2_), channel_id=1, source_target_pairs={{0,1},{1,0},{2,3},{3,2},{4,5},{5,4},{6,7},{7,6},{8,9},{9,8},{10,11... | collective-permute-start | bytes 122888 | tf_op jit(solution)/shard_map/ppermute | solution.py:521
  42.6 4.2 %collective-permute-start.30 = (bf16[160,128]{1,0:T(8,128)(2,1)S(1)}, bf16[160,128]{1,0:T(8,128)(2,1)S(1)}, u32[]{:S(2)}, u32[]{:S(2)}) collective-permute-start(bf16[160,128]{1,0:T(8,128)(2,1)S(1)} %collective-permute-done.29.refs_4_), channel_id=1, source_target_pairs={{0,1},{1,0},{2,3},{3,2},{4,5},{5,4},{6,7},{7,6},{8,9},{9,8},{10,11... | collective-permute-start | bytes 122888 | tf_op jit(solution)/shard_map/ppermute | solution.py:521
  45.0 1.8 %collective-permute-start.32 = (bf16[160,128]{1,0:T(8,128)(2,1)S(1)}, bf16[160,128]{1,0:T(8,128)(2,1)S(1)}, u32[]{:S(2)}, u32[]{:S(2)}) collective-permute-start(bf16[160,128]{1,0:T(8,128)(2,1)S(1)} %collective-permute-done.31.refs_6_), channel_id=1, source_target_pairs={{0,1},{1,0},{2,3},{3,2},{4,5},{5,4},{6,7},{7,6},{8,9},{9,8},{10,11... | collective-permute-start | bytes 122888 | tf_op jit(solution)/shard_map/ppermute | solution.py:521

commit v5 on v4

--- a/solution.py
+++ b/solution.py
@@ -390,6 +390,31 @@
     refs[-1][...] = gather_lanes(blocks, info_ref[6:7]).astype(BF16)
 
 
+def unpack_all(pieces):
+    pieces = pieces + pieces[-1:] * (len(pieces) % 2)
+    return [unpack_halves(pieces[p], pieces[p + 1]) for p in range(0, len(pieces), 2)]
+
+
+def early_kernel(section, own_ref, near_ref, info_ref, state_ref, forward_ref, *refs):
+    slots = own_ref.shape[1]
+    part_ref, left_ref, here_ref = refs[-3:]
+    info = info_ref[...]
+    pieces = [r[...] for r in refs[:-3]]
+    blocks = [jnp.concatenate([own_ref[...], near_ref[:, :slots]], axis=1)] + unpack_all(pieces)
+    part_ref[...] = gather_lanes(blocks, info[5:6]).astype(BF16)
+    child, left = (jnp.broadcast_to(info[k : k + 1], (FACE, slots)) for k in (1, 4))
+    child = [child == c + 1 for c in range(4)]
+    raw = [own_ref[v * FACE : (v + 1) * FACE] for v in range(5)]
+    raw += [state_ref[section, v * FACE : (v + 1) * FACE, :slots] for v in range(5)]
+    stacked = jnp.concatenate(raw, axis=1)
+    spread = spread_children(forward_ref[...], [stacked, stacked])
+    values = [x.astype(F32) for x in raw]
+    for v, x in enumerate(choose(values[:5], spread, child)):
+        left_ref[v * FACE : (v + 1) * FACE] = x
+    for v, x in enumerate(choose(values[5:], spread[:, 5 * slots :], child, left == 1)):
+        here_ref[v * FACE : (v + 1) * FACE] = x
+
+
 def mortar_update(section, relative, first, last, count, *refs):
     compact = relative and not first
     slots = refs[count].shape[1]
@@ -401,9 +426,9 @@
     elements = base_ref.shape[1]
     if len(pieces) == 1 and pieces[0].ndim == 3:
         pieces = [pieces[0][p] for p in range(pieces[0].shape[0])]
-    cap = slots // len(pieces)
     hot = hot_ref[...]
     if first:
+        cap = slots // len(pieces)
         info = read_table(pieces, me_ref, cap, relative)
     else:
         info = outs[0][...]
@@ -420,9 +445,10 @@
         partner = partner[:ROWS]
         piece_of = info[0:1] // slots
         far = (piece_of >= 2) & (info[3:4] == 1)
-        packed = (piece_of - 2) * half + rank
-        near_code = jnp.where(far & (rank < half), 2 * slots + packed, jnp.where(far, -1, info[0:1]))
-        rest_code = jnp.where(far & (rank >= half), packed - half, -1)
+        passed = piece_of % 2
+        packed = 2 * slots + (passed * (len(pieces) // 2) + piece_of // 2 - 1) * half + rank
+        near_code = jnp.where(far & (rank < half), packed, jnp.where(far, -1, info[0:1]))
+        rest_code = jnp.where(far & (rank >= half), (piece_of - 3) * half + rank, -1)
         field = lax.broadcasted_iota(jnp.int32, info.shape, 0)
         info = jnp.where(field == 5, near_code, jnp.where(field == 6, rest_code, info))
         chosen = dot(hot[:, :slots], picks, 1, 1).astype(BF16)
@@ -430,11 +456,10 @@
         outs[2][...] = rests
         outs[3][...] = jnp.full(outs[3].shape, most - half, F32)
     elif compact:
-        blocks = [jnp.concatenate([pieces[0][:ROWS], pieces[1][:ROWS]], axis=1)]
-        blocks += [unpack_halves(pieces[p], pieces[p + 1]) for p in range(2, len(pieces), 2)]
-        partner = gather_lanes(blocks, info[5:6])
-        partner = partner + outs[0][...].astype(F32)
-        outs = outs[1:]
+        start = 2 * slots + (len(pieces) + 1) * half
+        partner = gather_lanes(unpack_all(pieces), info[5:6], start)
+        more_ref, part_ref, left_ref, state_here_ref, *outs = outs
+        partner = partner + part_ref[...].astype(F32) + more_ref[...].astype(F32)
         if not last:
             chosen = outs[0][...]
             outs = outs[1:]
@@ -453,13 +478,20 @@
     def variables(x):
         return [x[v * FACE : (v + 1) * FACE].astype(F32) for v in range(5)]
 
-    own, partner, state = variables(own_ref[:ROWS]), variables(partner), variables(state_ref[section][:, :slots])
-    left_lam = [jnp.where(is_left, a, b) for a, b in zip(own, partner)]
+    own, partner = variables(own_ref[:ROWS]), variables(partner)
     right_lam = [jnp.where(is_left, b, a) for a, b in zip(own, partner)]
-    stacked = jnp.concatenate([x.astype(BF16) for x in left_lam + state], axis=1)
-    spread = spread_children(forward_ref[...], [stacked, stacked])
-    left_lam = choose(left_lam, spread, child)
-    u = choose(state, spread[:, 5 * slots :], child, is_left)
+    if compact:
+        stacked = jnp.concatenate([x.astype(BF16) for x in partner], axis=1)
+        projected = choose(partner, spread_children(forward_ref[...], [stacked, stacked]), child)
+        left_lam = [jnp.where(is_left, a, b) for a, b in zip(variables(left_ref[...]), projected)]
+        u = variables(state_here_ref[...])
+    else:
+        state = variables(state_ref[section][:, :slots])
+        left_lam = [jnp.where(is_left, a, b) for a, b in zip(own, partner)]
+        stacked = jnp.concatenate([x.astype(BF16) for x in left_lam + state], axis=1)
+        spread = spread_children(forward_ref[...], [stacked, stacked])
+        left_lam = choose(left_lam, spread, child)
+        u = choose(state, spread[:, 5 * slots :], child, is_left)
     w = [jnp.where(alive, b - a, 0.0) for a, b in zip(left_lam, right_lam)]
     u = [jnp.where(alive, u[v], REST[v]) for v in range(5)]
     g = flux_pull(u, w, picks)
@@ -633,12 +665,21 @@
             outs += [sent, pair] + ([packed] * (count - 1) if relative else [])
         if first:
             outs = [info_shape] + ([chosen_shape, rests_shape, ((8, 128), F32)] if relative else []) + outs
+        compact = relative and not first
+        if compact:
+            wide = ((ROWS, slots), F32)
+            early = call(
+                functools.partial(early_kernel, section),
+                [sent, wide, wide],
+                [outgoing, near, info, values, forward] + column,
+            )
+            pieces = pieces[3::2]
         args = pieces + [outgoing, base, values, hot, table, jac, forward, backward]
         scalars = (len(args),) if first else ()
         args.append(me if first else info)
-        if relative and not first:
+        if compact:
             args.append(lax.cond(flag[0] > 0, send_rest, no_rest, outgoing, rests, info))
-            args += [] if last else [chosen]
+            args += list(early) + ([] if last else [chosen])
         out = call(
             functools.partial(mortar_update, section, relative, first, last, len(pieces)),
             outs, args, scalars=scalars, final=last,

time: 49.2 us -> 49.9 us (1.014)
  Pallas kernels: 17 us -> 17.6 us
    pallas_call x11 -> x13, Pallas kernels: 17 us -> 17.6 us  [call(): pl.pallas_call(kernel, out_shape=shapes, in_specs=[pl.BlockSpec(memory_sp...]
  transfers between devices with their start and end apart: 21 -> 21, of which waited for: 6 -> 6; matrix products, arithmetic and copies ran while one was open for 0% -> 0% of each run, Pallas kernels for 17% -> 19%
where the time goes in v5:
time: 49.9 us; the launch traced here: 49.6 us
  Pallas kernels  17.6 us (35%)
  starting transfers between devices  16 us (32%)
  waiting for transfers between devices  15 us (30%)
  between operations  0.85 us (2%)
    pallas_call x13, Pallas kernels, call(): pl.pallas_call(kernel, out_shape=shapes, in_specs=[pl.BlockSpec(memory_sp...  17.6 us
    ppermute x9, waiting for transfers between devices, send_along(): return lax.ppermute(x, 'gy', [(i, i ^ k) for i in range(ny)])  14.9 us
    ppermute x9, starting transfers between devices, send_along(): return lax.ppermute(x, 'gy', [(i, i ^ k) for i in range(ny)])  14.3 us
    ppermute x12, starting transfers between devices, swap_pair(): return lax.ppermute(x, 'gz', [(0, 1), (1, 0)])  1.74 us
  transfers between devices with their start and end apart: 21, of which 6 were waited for; matrix products, arithmetic and copies ran while one was open for 0% of the time, Pallas kernels for 19%

profile of v5, /device:TPU:0, one launch (start us, length us, event | category | flops | bytes accessed | tf_op | source)
XLA Modules:
  0.0 49.6 jit_solution(3682183184166277402)
XLA Ops:
  0.0 0.0 copy-start
  0.0 1.8 %shard_map.100 = (bf16[336,128]{1,0:T(8,128)(2,1)S(1)}, bf16[336,256]{1,0:T(8,128)(2,1)S(1)}, bf16[192,256]{1,0:T(8,128)(2,1)S(1)}, f32[5,32,512]{2,1,0:T(8,128)S(1)}, bf16[512,384]{1,0:T(8,128)(2,1)S(1)}) custom-call(f32[5,32,512]{2,1,0:T(8,128)} %bitcast.17, s32[1,128]{1,0:T(1,128)} %send_hbm.1, s32[1,2,16]{2,1,0:T(2,128)} %conf_hbm.1, ...), custom_call_target="tpu_custom_call" | custom-call | tf_op jit(solution)/shard_map/pallas_call | solution.py:533
  1.8 0.6 %collective-permute-start.12 = (bf16[336,256]{1,0:T(8,128)(2,1)S(1)}, bf16[336,256]{1,0:T(8,128)(2,1)S(1)}, u32[]{:S(2)}, u32[]{:S(2)}) collective-permute-start(bf16[336,256]{1,0:T(8,128)(2,1)S(1)} %get-tuple-element.67.own_ref), channel_id=1, source_target_pairs={{0,1},{1,0},{2,3},{3,2},{4,5},{5,4},{6,7},{7,6},{8,9},{9,8},{10,11... | collective-permute-start | bytes 516104 | tf_op jit(solution)/shard_map/ppermute | solution.py:553
  2.4 4.7 %collective-permute-start.17 = (bf16[336,128]{1,0:T(8,128)(2,1)S(1)}, bf16[336,128]{1,0:T(8,128)(2,1)S(1)}, u32[]{:S(2)}, u32[]{:S(2)}) collective-permute-start(bf16[336,128]{1,0:T(8,128)(2,1)S(1)} %get-tuple-element.66.refs_0_.refs_8_), channel_id=1, source_target_pairs={{0,6},{2,4},{4,2},{6,0},{1,7},{3,5},{5,3},{7,1},{8,14},{10,12},{12... | collective-permute-start | bytes 258056 | tf_op jit(solution)/shard_map/ppermute | solution.py:558
  7.0 0.0 collective-permute-start.15
  7.0 0.6 %collective-permute-start.13 = (bf16[336,128]{1,0:T(8,128)(2,1)S(1)}, bf16[336,128]{1,0:T(8,128)(2,1)S(1)}, u32[]{:S(2)}, u32[]{:S(2)}) collective-permute-start(bf16[336,128]{1,0:T(8,128)(2,1)S(1)} %get-tuple-element.66.refs_0_.refs_8_), channel_id=1, source_target_pairs={{0,2},{2,0},{4,6},{6,4},{1,3},{3,1},{5,7},{7,5},{8,10},{10,8},{12,... | collective-permute-start | bytes 258056 | tf_op jit(solution)/shard_map/ppermute | solution.py:558
  7.7 2.8 %collective-permute-done.17.refs_6_ = bf16[336,128]{1,0:T(8,128)(2,1)S(1)} collective-permute-done((bf16[336,128]{1,0:T(8,128)(2,1)S(1)}, bf16[336,128]{1,0:T(8,128)(2,1)S(1)}, u32[]{:S(2)}, u32[]{:S(2)}) %collective-permute-start.17) | collective-permute-done | bytes 86048 | tf_op jit(solution)/shard_map/ppermute | solution.py:558
  10.5 0.0 collective-permute-start.18
  10.5 4.3 %collective-permute-done.15.refs_4_ = bf16[336,128]{1,0:T(8,128)(2,1)S(1)} collective-permute-done((bf16[336,128]{1,0:T(8,128)(2,1)S(1)}, bf16[336,128]{1,0:T(8,128)(2,1)S(1)}, u32[]{:S(2)}, u32[]{:S(2)}) %collective-permute-start.15) | collective-permute-done | bytes 86048 | tf_op jit(solution)/shard_map/ppermute | solution.py:558
  14.9 0.0 collective-permute-start.16
  14.9 0.0 collective-permute-done.13.refs_2_
  14.9 0.5 %collective-permute-start.14 = (bf16[336,128]{1,0:T(8,128)(2,1)S(1)}, bf16[336,128]{1,0:T(8,128)(2,1)S(1)}, u32[]{:S(2)}, u32[]{:S(2)}) collective-permute-start(bf16[336,128]{1,0:T(8,128)(2,1)S(1)} %collective-permute-done.13.refs_2_), channel_id=1, source_target_pairs={{0,1},{1,0},{2,3},{3,2},{4,5},{5,4},{6,7},{7,6},{8,9},{9,8},{10,11... | collective-permute-start | bytes 258056 | tf_op jit(solution)/shard_map/ppermute | solution.py:553
  15.4 2.4 %shard_map.101 = (bf16[3,320,256]{2,1,0:T(8,128)(2,1)S(1)}, bf16[2,512,512]{2,1,0:T(8,128)(2,1)S(1)}, bf16[256,128]{1,0:T(8,128)(2,1)S(1)}, bf16[256,192]{1,0:T(8,128)(2,1)S(1)}) custom-call(bf16[3,5,32,512]{3,2,1,0:T(8,128)(2,1)} %bitcast.13, bf16[3,512,512]{2,1,0:T(8,128)(2,1)} %stiff_hbm.7, bf16[256,128]{1,0:T(8,128)(2,1)} %constant.20.clone.forward_hbm, ...), custom_call_target="tpu_custom_call" | custom-call | tf_op jit(solution)/shard_map/pallas_call | solution.py:533
  17.8 0.0 collective-permute-done.12.near_ref.refs_1_
  17.8 0.0 copy-done
  17.8 1.8 %shard_map.102.refs_9_ = f32[5,32,512]{2,1,0:T(8,128)S(1)} custom-call(bf16[3,5,32,512]{3,2,1,0:T(8,128)(2,1)} %bitcast.14, bf16[3,512,512]{2,1,0:T(8,128)(2,1)} %stiff_hbm.7, f32[5,32,512]{2,1,0:T(8,128)S(1)} %get-tuple-element.68.lam_ref, bf16[2,512,512]{2,1,0:T(8,128)(2,1)S(1)} %get-tuple-element.71.held_ref, f32[1,32]{1,0:T(1,128)S(1)} %bitcast.7, ...), custom_call_target="tpu_custom_call" | custom-call | tf_op jit(solution)/shard_map/pallas_call | solution.py:533
  19.6 0.0 collective-permute-done.18.refs_7_
  19.7 0.0 collective-permute-done.16.refs_5_
  19.7 0.0 collective-permute-done.14.refs_3_
  19.7 2.5 %shard_map.103 = (s32[16,128]{1,0:T(8,128)S(1)}, bf16[192,256]{1,0:T(8,128)(2,1)S(1)}, bf16[256,128]{1,0:T(8,128)(2,1)S(1)}, f32[8,128]{1,0:T(8,128)S(1)}, f32[5...) custom-call(bf16[336,128]{1,0:T(8,128)(2,1)S(1)} %get-tuple-element., ...), custom_call_target="tpu_custom_call" | custom-call | tf_op jit(solution)/shard_map/pallas_call | solution.py:533
  22.2 0.1 collective-permute-start.25
  22.3 0.6 %shard_map.105 = s32[1]{0:T(128)} custom-call(f32[8,128]{1,0:T(8,128)S(1)} %get-tuple-element.82.excess_ref), custom_call_target="tpu_custom_call" | custom-call | tf_op jit(solution)/shard_map/pallas_call | solution.py:533
  23.6 0.8 %collective-permute-start.19 = (bf16[160,128]{1,0:T(8,128)(2,1)S(1)}, bf16[160,128]{1,0:T(8,128)(2,1)S(1)}, u32[]{:S(2)}, u32[]{:S(2)}) collective-permute-start(bf16[160,128]{1,0:T(8,128)(2,1)S(1)} %get-tuple-element.75), channel_id=1, source_target_pairs={{0,2},{2,0},{4,6},{6,4},{1,3},{3,1},{5,7},{7,5},{8,10},{10,8},{12,... | collective-permute-start | bytes 122888 | tf_op jit(solution)/shard_map/ppermute | solution.py:558
  24.5 2.3 %collective-permute-start.21 = (bf16[160,128]{1,0:T(8,128)(2,1)S(1)}, bf16[160,128]{1,0:T(8,128)(2,1)S(1)}, u32[]{:S(2)}, u32[]{:S(2)}) collective-permute-start(bf16[160,128]{1,0:T(8,128)(2,1)S(1)} %get-tuple-element.76), channel_id=1, source_target_pairs={{0,4},{2,6},{4,0},{6,2},{1,5},{3,7},{5,1},{7,3},{8,12},{10,14},{12... | collective-permute-start | bytes 122888 | tf_op jit(solution)/shard_map/ppermute | solution.py:558
  26.8 1.3 %collective-permute-start.23 = (bf16[160,128]{1,0:T(8,128)(2,1)S(1)}, bf16[160,128]{1,0:T(8,128)(2,1)S(1)}, u32[]{:S(2)}, u32[]{:S(2)}) collective-permute-start(bf16[160,128]{1,0:T(8,128)(2,1)S(1)} %get-tuple-element.77), channel_id=1, source_target_pairs={{0,6},{2,4},{4,2},{6,0},{1,7},{3,5},{5,3},{7,1},{8,14},{10,12},{12... | collective-permute-start | bytes 122888 | tf_op jit(solution)/shard_map/ppermute | solution.py:558
  28.1 0.0 collective-permute-done.19.refs_0_
  28.1 0.0 collective-permute-start.20
  28.1 2.5 %collective-permute-done.21.refs_1_ = bf16[160,128]{1,0:T(8,128)(2,1)S(1)} collective-permute-done((bf16[160,128]{1,0:T(8,128)(2,1)S(1)}, bf16[160,128]{1,0:T(8,128)(2,1)S(1)}, u32[]{:S(2)}, u32[]{:S(2)}) %collective-permute-start.21) | collective-permute-done | bytes 40992 | tf_op jit(solution)/shard_map/ppermute | solution.py:558
  30.7 0.0 collective-permute-start.22
  30.7 1.9 %collective-permute-done.23.refs_2_ = bf16[160,128]{1,0:T(8,128)(2,1)S(1)} collective-permute-done((bf16[160,128]{1,0:T(8,128)(2,1)S(1)}, bf16[160,128]{1,0:T(8,128)(2,1)S(1)}, u32[]{:S(2)}, u32[]{:S(2)}) %collective-permute-start.23) | collective-permute-done | bytes 40992 | tf_op jit(solution)/shard_map/ppermute | solution.py:558
  32.6 0.0 collective-permute-start.24
  32.6 0.0 collective-permute-done.25.near_ref
  32.6 0.5 shard_map.106
  33.1 1.8 %shard_map.104.refs_4_ = f32[5,32,512]{2,1,0:T(8,128)S(1)} custom-call(bf16[3,5,32,512]{3,2,1,0:T(8,128)(2,1)} %bitcast.15, bf16[3,512,512]{2,1,0:T(8,128)(2,1)} %stiff_hbm.7, f32[5,32,512]{2,1,0:T(8,128)S(1)} %get-tuple-element.79.lam_ref, bf16[2,512,512]{2,1,0:T(8,128)(2,1)S(1)} %get-tuple-element.71.held_ref, f32[1,32]{1,0:T(1,128)S(1)} %bitcast.9, ...), custom_call_target="tpu_custom_call" | custom-call | tf_op jit(solution)/shard_map/pallas_call | solution.py:533
  34.9 0.0 collective-permute-done.20.refs_0_
  34.9 0.0 collective-permute-done.22.refs_1_
  34.9 0.0 collective-permute-done.24.refs_2_
  34.9 1.9 %shard_map.107 = (f32[5,32,512]{2,1,0:T(8,128)S(1)}, bf16[320,128]{1,0:T(8,128)(2,1)S(1)}, bf16[320,256]{1,0:T(8,128)(2,1)S(1)}, bf16[160,128]{1,0:T(8,128)(2,1)...) custom-call(bf16[160,128]{1,0:T(8,128)(2,1)S(1)} %collective-permute-done.20.refs_0_, ...), custom_call_target="tpu_custom_call" | custom-call | tf_op jit(solution)/shard_map/pallas_call | solution.py:533
  36.8 0.6 %collective-permute-start.32 = (bf16[320,256]{1,0:T(8,128)(2,1)S(1)}, bf16[320,256]{1,0:T(8,128)(2,1)S(1)}, u32[]{:S(2)}, u32[]{:S(2)}) collective-permute-start(bf16[320,256]{1,0:T(8,128)(2,1)S(1)} %get-tuple-element.93.own_ref), channel_id=1, source_target_pairs={{0,1},{1,0},{2,3},{3,2},{4,5},{5,4},{6,7},{7,6},{8,9},{9,8},{10,11... | collective-permute-start | bytes 491528 | tf_op jit(solution)/shard_map/ppermute | solution.py:553
  37.4 0.0 collective-permute-start.26
  37.4 0.2 conditional.3
  37.6 2.0 %collective-permute-start.28 = (bf16[160,128]{1,0:T(8,128)(2,1)S(1)}, bf16[160,128]{1,0:T(8,128)(2,1)S(1)}, u32[]{:S(2)}, u32[]{:S(2)}) collective-permute-start(bf16[160,128]{1,0:T(8,128)(2,1)S(1)} %get-tuple-element.89), channel_id=1, source_target_pairs={{0,4},{2,6},{4,0},{6,2},{1,5},{3,7},{5,1},{7,3},{8,12},{10,14},{12... | collective-permute-start | bytes 122888 | tf_op jit(solution)/shard_map/ppermute | solution.py:558
  39.6 2.5 %collective-permute-start.30 = (bf16[160,128]{1,0:T(8,128)(2,1)S(1)}, bf16[160,128]{1,0:T(8,128)(2,1)S(1)}, u32[]{:S(2)}, u32[]{:S(2)}) collective-permute-start(bf16[160,128]{1,0:T(8,128)(2,1)S(1)} %get-tuple-element.90), channel_id=1, source_target_pairs={{0,6},{2,4},{4,2},{6,0},{1,7},{3,5},{5,3},{7,1},{8,14},{10,12},{12... | collective-permute-start | bytes 122888 | tf_op jit(solution)/shard_map/ppermute | solution.py:558
  42.0 0.0 collective-permute-done.26.refs_0_
  42.0 0.0 collective-permute-start.27
  42.0 1.0 %collective-permute-done.28.refs_1_ = bf16[160,128]{1,0:T(8,128)(2,1)S(1)} collective-permute-done((bf16[160,128]{1,0:T(8,128)(2,1)S(1)}, bf16[160,128]{1,0:T(8,128)(2,1)S(1)}, u32[]{:S(2)}, u32[]{:S(2)}) %collective-permute-start.28) | collective-permute-done | bytes 40992 | tf_op jit(solution)/shard_map/ppermute | solution.py:558
  43.0 0.0 collective-permute-start.29
  43.0 2.3 %collective-permute-done.30.refs_2_ = bf16[160,128]{1,0:T(8,128)(2,1)S(1)} collective-permute-done((bf16[160,128]{1,0:T(8,128)(2,1)S(1)}, bf16[160,128]{1,0:T(8,128)(2,1)S(1)}, u32[]{:S(2)}, u32[]{:S(2)}) %collective-permute-start.30) | collective-permute-done | bytes 40992 | tf_op jit(solution)/shard_map/ppermute | solution.py:558
  45.4 0.0 collective-permute-start.31
  45.4 0.0 collective-permute-done.32.near_ref
  45.4 0.5 shard_map.109
  45.8 1.8 %shard_map.108.refs_4_ = f32[5,32,512]{2,1,0:T(8,128)S(1)} custom-call(bf16[3,5,32,512]{3,2,1,0:T(8,128)(2,1)} %bitcast.16, bf16[3,512,512]{2,1,0:T(8,128)(2,1)} %stiff_hbm.7, f32[5,32,512]{2,1,0:T(8,128)S(1)} %get-tuple-element.92.lam_ref, bf16[2,512,512]{2,1,0:T(8,128)(2,1)S(1)} %get-tuple-element.71.held_ref, f32[1,32]{1,0:T(1,128)S(1)} %bitcast.11, ...), custom_call_target="tpu_custom_call" | custom-call | tf_op jit(solution)/shard_map/pallas_call | solution.py:533
  47.7 0.0 collective-permute-done.27.refs_0_
  47.7 0.0 collective-permute-done.29.refs_1_
  47.7 0.0 collective-permute-done.31.refs_2_
  47.7 2.0 %shard_map.110 = f32[5,32,512]{2,1,0:T(8,128)} custom-call(bf16[160,128]{1,0:T(8,128)(2,1)S(1)} %collective-permute-done.27.refs_0_, bf16[160,128]{1,0:T(8,128)(2,1)S(1)} %collective-permute-done.29.refs_1_, bf16[160,128]{1,0:T(8,128)(2,1)S(1)} %collective-permute-done.31.refs_2_, bf16[320,128]{1,0:T(8,128)(2,1)S(1)} %get-tuple-element.91.own_ref.refs_3_, ...), custom_call_target="tpu_custom_call" | custom-call | tf_op jit(solution)/shard_map/pallas_call | solution.py:533
  (3 shorter events, 0.0 us)
Async XLA Ops:
  0.0 17.8 %copy-start = (f32[32]{0:T(128)S(1)}, f32[32]{0:T(128)}, u32[]{:S(2)}) copy-start(f32[32]{0:T(128)} %param.16) | copy-start | bytes 388
  1.8 16.0 %collective-permute-start.12 = (bf16[336,256]{1,0:T(8,128)(2,1)S(1)}, bf16[336,256]{1,0:T(8,128)(2,1)S(1)}, u32[]{:S(2)}, u32[]{:S(2)}) collective-permute-start(bf16[336,256]{1,0:T(8,128)(2,1)S(1)} %get-tuple-element.67.own_ref), channel_id=1, source_target_pairs={{0,1},{1,0},{2,3},{3,2},{4,5},{5,4},{6,7},{7,6},{8,9},{9,8},{10,11... | collective-permute-start | bytes 516104 | tf_op jit(solution)/shard_map/ppermute | solution.py:553
  2.4 8.2 %collective-permute-start.17 = (bf16[336,128]{1,0:T(8,128)(2,1)S(1)}, bf16[336,128]{1,0:T(8,128)(2,1)S(1)}, u32[]{:S(2)}, u32[]{:S(2)}) collective-permute-start(bf16[336,128]{1,0:T(8,128)(2,1)S(1)} %get-tuple-element.66.refs_0_.refs_8_), channel_id=1, source_target_pairs={{0,6},{2,4},{4,2},{6,0},{1,7},{3,5},{5,3},{7,1},{8,14},{10,12},{12... | collective-permute-start | bytes 258056 | tf_op jit(solution)/shard_map/ppermute | solution.py:558
  7.0 7.8 %collective-permute-start.15 = (bf16[336,128]{1,0:T(8,128)(2,1)S(1)}, bf16[336,128]{1,0:T(8,128)(2,1)S(1)}, u32[]{:S(2)}, u32[]{:S(2)}) collective-permute-start(bf16[336,128]{1,0:T(8,128)(2,1)S(1)} %get-tuple-element.66.refs_0_.refs_8_), channel_id=1, source_target_pairs={{0,4},{2,6},{4,0},{6,2},{1,5},{3,7},{5,1},{7,3},{8,12},{10,14},{12... | collective-permute-start | bytes 258056 | tf_op jit(solution)/shard_map/ppermute | solution.py:558
  7.0 7.8 %collective-permute-start.13 = (bf16[336,128]{1,0:T(8,128)(2,1)S(1)}, bf16[336,128]{1,0:T(8,128)(2,1)S(1)}, u32[]{:S(2)}, u32[]{:S(2)}) collective-permute-start(bf16[336,128]{1,0:T(8,128)(2,1)S(1)} %get-tuple-element.66.refs_0_.refs_8_), channel_id=1, source_target_pairs={{0,2},{2,0},{4,6},{6,4},{1,3},{3,1},{5,7},{7,5},{8,10},{10,8},{12,... | collective-permute-start | bytes 258056 | tf_op jit(solution)/shard_map/ppermute | solution.py:558
  10.5 9.1 %collective-permute-start.18 = (bf16[336,128]{1,0:T(8,128)(2,1)S(1)}, bf16[336,128]{1,0:T(8,128)(2,1)S(1)}, u32[]{:S(2)}, u32[]{:S(2)}) collective-permute-start(bf16[336,128]{1,0:T(8,128)(2,1)S(1)} %collective-permute-done.17.refs_6_), channel_id=1, source_target_pairs={{0,1},{1,0},{2,3},{3,2},{4,5},{5,4},{6,7},{7,6},{8,9},{9,8},{10,11... | collective-permute-start | bytes 258056 | tf_op jit(solution)/shard_map/ppermute | solution.py:553
  14.9 4.8 %collective-permute-start.16 = (bf16[336,128]{1,0:T(8,128)(2,1)S(1)}, bf16[336,128]{1,0:T(8,128)(2,1)S(1)}, u32[]{:S(2)}, u32[]{:S(2)}) collective-permute-start(bf16[336,128]{1,0:T(8,128)(2,1)S(1)} %collective-permute-done.15.refs_4_), channel_id=1, source_target_pairs={{0,1},{1,0},{2,3},{3,2},{4,5},{5,4},{6,7},{7,6},{8,9},{9,8},{10,11... | collective-permute-start | bytes 258056 | tf_op jit(solution)/shard_map/ppermute | solution.py:553
  14.9 4.8 %collective-permute-start.14 = (bf16[336,128]{1,0:T(8,128)(2,1)S(1)}, bf16[336,128]{1,0:T(8,128)(2,1)S(1)}, u32[]{:S(2)}, u32[]{:S(2)}) collective-permute-start(bf16[336,128]{1,0:T(8,128)(2,1)S(1)} %collective-permute-done.13.refs_2_), channel_id=1, source_target_pairs={{0,1},{1,0},{2,3},{3,2},{4,5},{5,4},{6,7},{7,6},{8,9},{9,8},{10,11... | collective-permute-start | bytes 258056 | tf_op jit(solution)/shard_map/ppermute | solution.py:553
  22.2 10.4 %collective-permute-start.25 = (bf16[320,256]{1,0:T(8,128)(2,1)S(1)}, bf16[320,256]{1,0:T(8,128)(2,1)S(1)}, u32[]{:S(2)}, u32[]{:S(2)}) collective-permute-start(bf16[320,256]{1,0:T(8,128)(2,1)S(1)} %get-tuple-element.80.own_ref), channel_id=1, source_target_pairs={{0,1},{1,0},{2,3},{3,2},{4,5},{5,4},{6,7},{7,6},{8,9},{9,8},{10,11... | collective-permute-start | bytes 491528 | tf_op jit(solution)/shard_map/ppermute | solution.py:553
  23.6 4.5 %collective-permute-start.19 = (bf16[160,128]{1,0:T(8,128)(2,1)S(1)}, bf16[160,128]{1,0:T(8,128)(2,1)S(1)}, u32[]{:S(2)}, u32[]{:S(2)}) collective-permute-start(bf16[160,128]{1,0:T(8,128)(2,1)S(1)} %get-tuple-element.75), channel_id=1, source_target_pairs={{0,2},{2,0},{4,6},{6,4},{1,3},{3,1},{5,7},{7,5},{8,10},{10,8},{12,... | collective-permute-start | bytes 122888 | tf_op jit(solution)/shard_map/ppermute | solution.py:558
  24.5 6.2 %collective-permute-start.21 = (bf16[160,128]{1,0:T(8,128)(2,1)S(1)}, bf16[160,128]{1,0:T(8,128)(2,1)S(1)}, u32[]{:S(2)}, u32[]{:S(2)}) collective-permute-start(bf16[160,128]{1,0:T(8,128)(2,1)S(1)} %get-tuple-element.76), channel_id=1, source_target_pairs={{0,4},{2,6},{4,0},{6,2},{1,5},{3,7},{5,1},{7,3},{8,12},{10,14},{12... | collective-permute-start | bytes 122888 | tf_op jit(solution)/shard_map/ppermute | solution.py:558
  26.8 5.8 %collective-permute-start.23 = (bf16[160,128]{1,0:T(8,128)(2,1)S(1)}, bf16[160,128]{1,0:T(8,128)(2,1)S(1)}, u32[]{:S(2)}, u32[]{:S(2)}) collective-permute-start(bf16[160,128]{1,0:T(8,128)(2,1)S(1)} %get-tuple-element.77), channel_id=1, source_target_pairs={{0,6},{2,4},{4,2},{6,0},{1,7},{3,5},{5,3},{7,1},{8,14},{10,12},{12... | collective-permute-start | bytes 122888 | tf_op jit(solution)/shard_map/ppermute | solution.py:558
  28.1 6.7 %collective-permute-start.20 = (bf16[160,128]{1,0:T(8,128)(2,1)S(1)}, bf16[160,128]{1,0:T(8,128)(2,1)S(1)}, u32[]{:S(2)}, u32[]{:S(2)}) collective-permute-start(bf16[160,128]{1,0:T(8,128)(2,1)S(1)} %collective-permute-done.19.refs_0_), channel_id=1, source_target_pairs={{0,1},{1,0},{2,3},{3,2},{4,5},{5,4},{6,7},{7,6},{8,9},{9,8},{10,11... | collective-permute-start | bytes 122888 | tf_op jit(solution)/shard_map/ppermute | solution.py:553
  30.7 4.2 %collective-permute-start.22 = (bf16[160,128]{1,0:T(8,128)(2,1)S(1)}, bf16[160,128]{1,0:T(8,128)(2,1)S(1)}, u32[]{:S(2)}, u32[]{:S(2)}) collective-permute-start(bf16[160,128]{1,0:T(8,128)(2,1)S(1)} %collective-permute-done.21.refs_1_), channel_id=1, source_target_pairs={{0,1},{1,0},{2,3},{3,2},{4,5},{5,4},{6,7},{7,6},{8,9},{9,8},{10,11... | collective-permute-start | bytes 122888 | tf_op jit(solution)/shard_map/ppermute | solution.py:553
  32.6 2.3 %collective-permute-start.24 = (bf16[160,128]{1,0:T(8,128)(2,1)S(1)}, bf16[160,128]{1,0:T(8,128)(2,1)S(1)}, u32[]{:S(2)}, u32[]{:S(2)}) collective-permute-start(bf16[160,128]{1,0:T(8,128)(2,1)S(1)} %collective-permute-done.23.refs_2_), channel_id=1, source_target_pairs={{0,1},{1,0},{2,3},{3,2},{4,5},{5,4},{6,7},{7,6},{8,9},{9,8},{10,11... | collective-permute-start | bytes 122888 | tf_op jit(solution)/shard_map/ppermute | solution.py:553
  36.8 8.6 %collective-permute-start.32 = (bf16[320,256]{1,0:T(8,128)(2,1)S(1)}, bf16[320,256]{1,0:T(8,128)(2,1)S(1)}, u32[]{:S(2)}, u32[]{:S(2)}) collective-permute-start(bf16[320,256]{1,0:T(8,128)(2,1)S(1)} %get-tuple-element.93.own_ref), channel_id=1, source_target_pairs={{0,1},{1,0},{2,3},{3,2},{4,5},{5,4},{6,7},{7,6},{8,9},{9,8},{10,11... | collective-permute-start | bytes 491528 | tf_op jit(solution)/shard_map/ppermute | solution.py:553
  37.4 4.7 %collective-permute-start.26 = (bf16[160,128]{1,0:T(8,128)(2,1)S(1)}, bf16[160,128]{1,0:T(8,128)(2,1)S(1)}, u32[]{:S(2)}, u32[]{:S(2)}) collective-permute-start(bf16[160,128]{1,0:T(8,128)(2,1)S(1)} %get-tuple-element.88), channel_id=1, source_target_pairs={{0,2},{2,0},{4,6},{6,4},{1,3},{3,1},{5,7},{7,5},{8,10},{10,8},{12,... | collective-permute-start | bytes 122888 | tf_op jit(solution)/shard_map/ppermute | solution.py:558
  37.6 5.4 %collective-permute-start.28 = (bf16[160,128]{1,0:T(8,128)(2,1)S(1)}, bf16[160,128]{1,0:T(8,128)(2,1)S(1)}, u32[]{:S(2)}, u32[]{:S(2)}) collective-permute-start(bf16[160,128]{1,0:T(8,128)(2,1)S(1)} %get-tuple-element.89), channel_id=1, source_target_pairs={{0,4},{2,6},{4,0},{6,2},{1,5},{3,7},{5,1},{7,3},{8,12},{10,14},{12... | collective-permute-start | bytes 122888 | tf_op jit(solution)/shard_map/ppermute | solution.py:558
  39.6 5.8 %collective-permute-start.30 = (bf16[160,128]{1,0:T(8,128)(2,1)S(1)}, bf16[160,128]{1,0:T(8,128)(2,1)S(1)}, u32[]{:S(2)}, u32[]{:S(2)}) collective-permute-start(bf16[160,128]{1,0:T(8,128)(2,1)S(1)} %get-tuple-element.90), channel_id=1, source_target_pairs={{0,6},{2,4},{4,2},{6,0},{1,7},{3,5},{5,3},{7,1},{8,14},{10,12},{12... | collective-permute-start | bytes 122888 | tf_op jit(solution)/shard_map/ppermute | solution.py:558
  42.0 5.6 %collective-permute-start.27 = (bf16[160,128]{1,0:T(8,128)(2,1)S(1)}, bf16[160,128]{1,0:T(8,128)(2,1)S(1)}, u32[]{:S(2)}, u32[]{:S(2)}) collective-permute-start(bf16[160,128]{1,0:T(8,128)(2,1)S(1)} %collective-permute-done.26.refs_0_), channel_id=1, source_target_pairs={{0,1},{1,0},{2,3},{3,2},{4,5},{5,4},{6,7},{7,6},{8,9},{9,8},{10,11... | collective-permute-start | bytes 122888 | tf_op jit(solution)/shard_map/ppermute | solution.py:553
  43.0 4.7 %collective-permute-start.29 = (bf16[160,128]{1,0:T(8,128)(2,1)S(1)}, bf16[160,128]{1,0:T(8,128)(2,1)S(1)}, u32[]{:S(2)}, u32[]{:S(2)}) collective-permute-start(bf16[160,128]{1,0:T(8,128)(2,1)S(1)} %collective-permute-done.28.refs_1_), channel_id=1, source_target_pairs={{0,1},{1,0},{2,3},{3,2},{4,5},{5,4},{6,7},{7,6},{8,9},{9,8},{10,11... | collective-permute-start | bytes 122888 | tf_op jit(solution)/shard_map/ppermute | solution.py:553
  45.4 2.3 %collective-permute-start.31 = (bf16[160,128]{1,0:T(8,128)(2,1)S(1)}, bf16[160,128]{1,0:T(8,128)(2,1)S(1)}, u32[]{:S(2)}, u32[]{:S(2)}) collective-permute-start(bf16[160,128]{1,0:T(8,128)(2,1)S(1)} %collective-permute-done.30.refs_2_), channel_id=1, source_target_pairs={{0,1},{1,0},{2,3},{3,2},{4,5},{5,4},{6,7},{7,6},{8,9},{9,8},{10,11... | collective-permute-start | bytes 122888 | tf_op jit(solution)/shard_map/ppermute | solution.py:553

commit v6 on v5

--- a/solution.py
+++ b/solution.py
@@ -51,7 +51,7 @@
     children = [np.kron(halves[c // 2], halves[c % 2]) for c in range(4)]
     fh, fl = split_low(np.concatenate(children, axis=0))
     bh, bl = split_low(np.concatenate([m.T for m in children], axis=0))
-    return np.concatenate([fh, fl], axis=1), np.concatenate([bh, bh, bl], axis=1)
+    return np.concatenate([fh, fl], axis=1), np.concatenate([bh, bl], axis=1)
 
 
 def restriction_table():
@@ -469,38 +469,55 @@
     if first:
         outs[0][...] = info
         outs = outs[4:] if relative else outs[1:]
-    child, axis, live, left = (jnp.broadcast_to(info[k : k + 1], (FACE, slots)) for k in range(1, 5))
+    step = FACE // 4
+    child, axis, live, left = (jnp.broadcast_to(info[k : k + 1], (step, slots)) for k in range(1, 5))
     is_left = left == 1
     alive = live == 1
     child = [child == c + 1 for c in range(4)]
     picks = [axis == n for n in range(3)]
-
-    def variables(x):
-        return [x[v * FACE : (v + 1) * FACE].astype(F32) for v in range(5)]
-
-    own, partner = variables(own_ref[:ROWS]), variables(partner)
-    right_lam = [jnp.where(is_left, b, a) for a, b in zip(own, partner)]
+    side = jnp.where(is_left, 0.5 * penalty, -0.5 * penalty)
+    partner = partner.astype(BF16)
     if compact:
-        stacked = jnp.concatenate([x.astype(BF16) for x in partner], axis=1)
-        projected = choose(partner, spread_children(forward_ref[...], [stacked, stacked]), child)
-        left_lam = [jnp.where(is_left, a, b) for a, b in zip(variables(left_ref[...]), projected)]
-        u = variables(state_here_ref[...])
+        projecting = [partner[v * FACE : (v + 1) * FACE] for v in range(5)]
     else:
-        state = variables(state_ref[section][:, :slots])
-        left_lam = [jnp.where(is_left, a, b) for a, b in zip(own, partner)]
-        stacked = jnp.concatenate([x.astype(BF16) for x in left_lam + state], axis=1)
-        spread = spread_children(forward_ref[...], [stacked, stacked])
-        left_lam = choose(left_lam, spread, child)
-        u = choose(state, spread[:, 5 * slots :], child, is_left)
-    w = [jnp.where(alive, b - a, 0.0) for a, b in zip(left_lam, right_lam)]
-    u = [jnp.where(alive, u[v], REST[v]) for v in range(5)]
-    g = flux_pull(u, w, picks)
-    side = jnp.where(is_left, 0.5 * penalty, -0.5 * penalty)
-    pull = [0.5 * g[v] + side * w[v] for v in range(5)]
+        whole = jnp.broadcast_to(info[4:5], (FACE, slots)) == 1
+        mixed = [jnp.where(whole, own_ref[v * FACE : (v + 1) * FACE].astype(F32), partner[v * FACE : (v + 1) * FACE].astype(F32)).astype(BF16) for v in range(5)]
+        projecting = mixed + [state_ref[section, v * FACE : (v + 1) * FACE, :slots] for v in range(5)]
+    stacked = jnp.concatenate(projecting, axis=1)
+    spread = spread_children(forward_ref[...], [stacked, stacked])
+
+    def project(raw, v, r, keep=None):
+        picked = raw
+        for c in range(4):
+            hit = child[c] if keep is None else child[c] & keep
+            picked = jnp.where(hit, spread[c * FACE + r : c * FACE + r + step, v * slots : (v + 1) * slots], picked)
+        return picked
+
+    chunks = [[] for _ in range(5)]
+    for r in range(0, FACE, step):
+        w, u = [], []
+        for v in range(5):
+            rows = slice(v * FACE + r, v * FACE + r + step)
+            mine, other = own_ref[rows].astype(F32), partner[rows].astype(F32)
+            right = jnp.where(is_left, other, mine)
+            if compact:
+                near_left = jnp.where(is_left, left_ref[rows], project(other, v, r))
+                here = state_here_ref[rows]
+            else:
+                near_left = project(jnp.where(is_left, mine, other), v, r)
+                here = project(state_ref[section, rows, :slots].astype(F32), 5 + v, r, is_left)
+            w.append(jnp.where(alive, right - near_left, 0.0))
+            u.append(jnp.where(alive, here, REST[v]))
+        g = flux_pull(u, w, picks)
+        for v in range(5):
+            chunks[v].append(0.5 * g[v] + side * w[v])
+    pull = [jnp.concatenate(parts, axis=0) for parts in chunks]
+    child, left = (jnp.broadcast_to(info[k : k + 1], (FACE, slots)) for k in (1, 4))
+    is_left = left == 1
+    child = [child == c + 1 for c in range(4)]
     stacked = jnp.concatenate(pull, axis=1)
     high = stacked.astype(BF16)
-    rest = (stacked - high.astype(F32)).astype(BF16)
-    spread = spread_children(backward_ref[...], [high, rest, high])
+    spread = spread_children(backward_ref[...], [high, high])
     grads = choose(pull, spread, child, is_left)
 
     table = table_ref[...]

time: 49.9 us -> 49.8 us (level)
  no operation moved by 1% of the time
where the time goes in v6:
time: 49.8 us; the launch traced here: 49.6 us
  Pallas kernels  17.6 us (35%)
  starting transfers between devices  16 us (32%)
  waiting for transfers between devices  15 us (30%)
  between operations  0.85 us (2%)
    pallas_call x13, Pallas kernels, call(): pl.pallas_call(kernel, out_shape=shapes, in_specs=[pl.BlockSpec(memory_sp...  17.6 us
    ppermute x9, waiting for transfers between devices, send_along(): return lax.ppermute(x, 'gy', [(i, i ^ k) for i in range(ny)])  14.9 us
    ppermute x9, starting transfers between devices, send_along(): return lax.ppermute(x, 'gy', [(i, i ^ k) for i in range(ny)])  14.3 us
    ppermute x12, starting transfers between devices, swap_pair(): return lax.ppermute(x, 'gz', [(0, 1), (1, 0)])  1.74 us
  transfers between devices with their start and end apart: 21, of which 6 were waited for; matrix products, arithmetic and copies ran while one was open for 0% of the time, Pallas kernels for 19%

profile of v6, /device:TPU:0, one launch (start us, length us, event | category | flops | bytes accessed | tf_op | source)
XLA Modules:
  0.0 49.6 jit_solution(8918446329458481289)
XLA Ops:
  0.0 0.0 copy-start
  0.0 1.8 %shard_map.100 = (bf16[336,128]{1,0:T(8,128)(2,1)S(1)}, bf16[336,256]{1,0:T(8,128)(2,1)S(1)}, bf16[192,256]{1,0:T(8,128)(2,1)S(1)}, f32[5,32,512]{2,1,0:T(8,128)S(1)}, bf16[512,384]{1,0:T(8,128)(2,1)S(1)}) custom-call(f32[5,32,512]{2,1,0:T(8,128)} %bitcast.17, s32[1,128]{1,0:T(1,128)} %send_hbm.1, s32[1,2,16]{2,1,0:T(2,128)} %conf_hbm.1, ...), custom_call_target="tpu_custom_call" | custom-call | tf_op jit(solution)/shard_map/pallas_call | solution.py:550
  1.8 0.6 %collective-permute-start.12 = (bf16[336,256]{1,0:T(8,128)(2,1)S(1)}, bf16[336,256]{1,0:T(8,128)(2,1)S(1)}, u32[]{:S(2)}, u32[]{:S(2)}) collective-permute-start(bf16[336,256]{1,0:T(8,128)(2,1)S(1)} %get-tuple-element.67.own_ref), channel_id=1, source_target_pairs={{0,1},{1,0},{2,3},{3,2},{4,5},{5,4},{6,7},{7,6},{8,9},{9,8},{10,11... | collective-permute-start | bytes 516104 | tf_op jit(solution)/shard_map/ppermute | solution.py:570
  2.4 4.7 %collective-permute-start.17 = (bf16[336,128]{1,0:T(8,128)(2,1)S(1)}, bf16[336,128]{1,0:T(8,128)(2,1)S(1)}, u32[]{:S(2)}, u32[]{:S(2)}) collective-permute-start(bf16[336,128]{1,0:T(8,128)(2,1)S(1)} %get-tuple-element.66.refs_0_.refs_8_), channel_id=1, source_target_pairs={{0,6},{2,4},{4,2},{6,0},{1,7},{3,5},{5,3},{7,1},{8,14},{10,12},{12... | collective-permute-start | bytes 258056 | tf_op jit(solution)/shard_map/ppermute | solution.py:575
  7.0 0.0 collective-permute-start.15
  7.0 0.6 %collective-permute-start.13 = (bf16[336,128]{1,0:T(8,128)(2,1)S(1)}, bf16[336,128]{1,0:T(8,128)(2,1)S(1)}, u32[]{:S(2)}, u32[]{:S(2)}) collective-permute-start(bf16[336,128]{1,0:T(8,128)(2,1)S(1)} %get-tuple-element.66.refs_0_.refs_8_), channel_id=1, source_target_pairs={{0,2},{2,0},{4,6},{6,4},{1,3},{3,1},{5,7},{7,5},{8,10},{10,8},{12,... | collective-permute-start | bytes 258056 | tf_op jit(solution)/shard_map/ppermute | solution.py:575
  7.7 2.8 %collective-permute-done.17.refs_6_ = bf16[336,128]{1,0:T(8,128)(2,1)S(1)} collective-permute-done((bf16[336,128]{1,0:T(8,128)(2,1)S(1)}, bf16[336,128]{1,0:T(8,128)(2,1)S(1)}, u32[]{:S(2)}, u32[]{:S(2)}) %collective-permute-start.17) | collective-permute-done | bytes 86048 | tf_op jit(solution)/shard_map/ppermute | solution.py:575
  10.5 0.0 collective-permute-start.18
  10.5 4.3 %collective-permute-done.15.refs_4_ = bf16[336,128]{1,0:T(8,128)(2,1)S(1)} collective-permute-done((bf16[336,128]{1,0:T(8,128)(2,1)S(1)}, bf16[336,128]{1,0:T(8,128)(2,1)S(1)}, u32[]{:S(2)}, u32[]{:S(2)}) %collective-permute-start.15) | collective-permute-done | bytes 86048 | tf_op jit(solution)/shard_map/ppermute | solution.py:575
  14.9 0.0 collective-permute-start.16
  14.9 0.0 collective-permute-done.13.refs_2_
  14.9 0.5 %collective-permute-start.14 = (bf16[336,128]{1,0:T(8,128)(2,1)S(1)}, bf16[336,128]{1,0:T(8,128)(2,1)S(1)}, u32[]{:S(2)}, u32[]{:S(2)}) collective-permute-start(bf16[336,128]{1,0:T(8,128)(2,1)S(1)} %collective-permute-done.13.refs_2_), channel_id=1, source_target_pairs={{0,1},{1,0},{2,3},{3,2},{4,5},{5,4},{6,7},{7,6},{8,9},{9,8},{10,11... | collective-permute-start | bytes 258056 | tf_op jit(solution)/shard_map/ppermute | solution.py:570
  15.4 2.4 %shard_map.101 = (bf16[3,320,256]{2,1,0:T(8,128)(2,1)S(1)}, bf16[2,512,512]{2,1,0:T(8,128)(2,1)S(1)}, bf16[256,128]{1,0:T(8,128)(2,1)S(1)}, bf16[256,128]{1,0:T(8,128)(2,1)S(1)}) custom-call(bf16[3,5,32,512]{3,2,1,0:T(8,128)(2,1)} %bitcast.13, bf16[3,512,512]{2,1,0:T(8,128)(2,1)} %stiff_hbm.7, bf16[256,128]{1,0:T(8,128)(2,1)} %constant.20.clone.forward_hbm, ...), custom_call_target="tpu_custom_call" | custom-call | tf_op jit(solution)/shard_map/pallas_call | solution.py:550
  17.8 0.0 collective-permute-done.12.near_ref.refs_1_
  17.8 0.0 copy-done
  17.8 1.8 %shard_map.102.refs_9_ = f32[5,32,512]{2,1,0:T(8,128)S(1)} custom-call(bf16[3,5,32,512]{3,2,1,0:T(8,128)(2,1)} %bitcast.14, bf16[3,512,512]{2,1,0:T(8,128)(2,1)} %stiff_hbm.7, f32[5,32,512]{2,1,0:T(8,128)S(1)} %get-tuple-element.68.lam_ref, bf16[2,512,512]{2,1,0:T(8,128)(2,1)S(1)} %get-tuple-element.71.held_ref, f32[1,32]{1,0:T(1,128)S(1)} %bitcast.7, ...), custom_call_target="tpu_custom_call" | custom-call | tf_op jit(solution)/shard_map/pallas_call | solution.py:550
  19.6 0.0 collective-permute-done.18.refs_7_
  19.7 0.0 collective-permute-done.16.refs_5_
  19.7 0.0 collective-permute-done.14.refs_3_
  19.7 2.5 %shard_map.103 = (s32[16,128]{1,0:T(8,128)S(1)}, bf16[192,256]{1,0:T(8,128)(2,1)S(1)}, bf16[256,128]{1,0:T(8,128)(2,1)S(1)}, f32[8,128]{1,0:T(8,128)S(1)}, f32[5...) custom-call(bf16[336,128]{1,0:T(8,128)(2,1)S(1)} %get-tuple-element., ...), custom_call_target="tpu_custom_call" | custom-call | tf_op jit(solution)/shard_map/pallas_call | solution.py:550
  22.2 0.1 collective-permute-start.25
  22.3 0.6 %shard_map.105 = s32[1]{0:T(128)} custom-call(f32[8,128]{1,0:T(8,128)S(1)} %get-tuple-element.82.excess_ref), custom_call_target="tpu_custom_call" | custom-call | tf_op jit(solution)/shard_map/pallas_call | solution.py:550
  23.6 0.8 %collective-permute-start.19 = (bf16[160,128]{1,0:T(8,128)(2,1)S(1)}, bf16[160,128]{1,0:T(8,128)(2,1)S(1)}, u32[]{:S(2)}, u32[]{:S(2)}) collective-permute-start(bf16[160,128]{1,0:T(8,128)(2,1)S(1)} %get-tuple-element.75), channel_id=1, source_target_pairs={{0,2},{2,0},{4,6},{6,4},{1,3},{3,1},{5,7},{7,5},{8,10},{10,8},{12,... | collective-permute-start | bytes 122888 | tf_op jit(solution)/shard_map/ppermute | solution.py:575
  24.4 2.3 %collective-permute-start.21 = (bf16[160,128]{1,0:T(8,128)(2,1)S(1)}, bf16[160,128]{1,0:T(8,128)(2,1)S(1)}, u32[]{:S(2)}, u32[]{:S(2)}) collective-permute-start(bf16[160,128]{1,0:T(8,128)(2,1)S(1)} %get-tuple-element.76), channel_id=1, source_target_pairs={{0,4},{2,6},{4,0},{6,2},{1,5},{3,7},{5,1},{7,3},{8,12},{10,14},{12... | collective-permute-start | bytes 122888 | tf_op jit(solution)/shard_map/ppermute | solution.py:575
  26.8 1.3 %collective-permute-start.23 = (bf16[160,128]{1,0:T(8,128)(2,1)S(1)}, bf16[160,128]{1,0:T(8,128)(2,1)S(1)}, u32[]{:S(2)}, u32[]{:S(2)}) collective-permute-start(bf16[160,128]{1,0:T(8,128)(2,1)S(1)} %get-tuple-element.77), channel_id=1, source_target_pairs={{0,6},{2,4},{4,2},{6,0},{1,7},{3,5},{5,3},{7,1},{8,14},{10,12},{12... | collective-permute-start | bytes 122888 | tf_op jit(solution)/shard_map/ppermute | solution.py:575
  28.1 0.0 collective-permute-done.19.refs_0_
  28.1 0.0 collective-permute-start.20
  28.1 2.5 %collective-permute-done.21.refs_1_ = bf16[160,128]{1,0:T(8,128)(2,1)S(1)} collective-permute-done((bf16[160,128]{1,0:T(8,128)(2,1)S(1)}, bf16[160,128]{1,0:T(8,128)(2,1)S(1)}, u32[]{:S(2)}, u32[]{:S(2)}) %collective-permute-start.21) | collective-permute-done | bytes 40992 | tf_op jit(solution)/shard_map/ppermute | solution.py:575
  30.6 0.0 collective-permute-start.22
  30.6 1.9 %collective-permute-done.23.refs_2_ = bf16[160,128]{1,0:T(8,128)(2,1)S(1)} collective-permute-done((bf16[160,128]{1,0:T(8,128)(2,1)S(1)}, bf16[160,128]{1,0:T(8,128)(2,1)S(1)}, u32[]{:S(2)}, u32[]{:S(2)}) %collective-permute-start.23) | collective-permute-done | bytes 40992 | tf_op jit(solution)/shard_map/ppermute | solution.py:575
  32.6 0.0 collective-permute-start.24
  32.6 0.0 collective-permute-done.25.near_ref
  32.6 0.5 shard_map.106
  33.0 1.8 %shard_map.104.refs_4_ = f32[5,32,512]{2,1,0:T(8,128)S(1)} custom-call(bf16[3,5,32,512]{3,2,1,0:T(8,128)(2,1)} %bitcast.15, bf16[3,512,512]{2,1,0:T(8,128)(2,1)} %stiff_hbm.7, f32[5,32,512]{2,1,0:T(8,128)S(1)} %get-tuple-element.79.lam_ref, bf16[2,512,512]{2,1,0:T(8,128)(2,1)S(1)} %get-tuple-element.71.held_ref, f32[1,32]{1,0:T(1,128)S(1)} %bitcast.9, ...), custom_call_target="tpu_custom_call" | custom-call | tf_op jit(solution)/shard_map/pallas_call | solution.py:550
  34.9 0.0 collective-permute-done.20.refs_0_
  34.9 0.0 collective-permute-done.22.refs_1_
  34.9 0.0 collective-permute-done.24.refs_2_
  34.9 1.8 %shard_map.107 = (f32[5,32,512]{2,1,0:T(8,128)S(1)}, bf16[320,128]{1,0:T(8,128)(2,1)S(1)}, bf16[320,256]{1,0:T(8,128)(2,1)S(1)}, bf16[160,128]{1,0:T(8,128)(2,1)...) custom-call(bf16[160,128]{1,0:T(8,128)(2,1)S(1)} %collective-permute-done.20.refs_0_, ...), custom_call_target="tpu_custom_call" | custom-call | tf_op jit(solution)/shard_map/pallas_call | solution.py:550
  36.7 0.6 %collective-permute-start.32 = (bf16[320,256]{1,0:T(8,128)(2,1)S(1)}, bf16[320,256]{1,0:T(8,128)(2,1)S(1)}, u32[]{:S(2)}, u32[]{:S(2)}) collective-permute-start(bf16[320,256]{1,0:T(8,128)(2,1)S(1)} %get-tuple-element.93.own_ref), channel_id=1, source_target_pairs={{0,1},{1,0},{2,3},{3,2},{4,5},{5,4},{6,7},{7,6},{8,9},{9,8},{10,11... | collective-permute-start | bytes 491528 | tf_op jit(solution)/shard_map/ppermute | solution.py:570
  37.3 0.0 collective-permute-start.26
  37.3 0.2 conditional.3
  37.5 2.0 %collective-permute-start.28 = (bf16[160,128]{1,0:T(8,128)(2,1)S(1)}, bf16[160,128]{1,0:T(8,128)(2,1)S(1)}, u32[]{:S(2)}, u32[]{:S(2)}) collective-permute-start(bf16[160,128]{1,0:T(8,128)(2,1)S(1)} %get-tuple-element.89), channel_id=1, source_target_pairs={{0,4},{2,6},{4,0},{6,2},{1,5},{3,7},{5,1},{7,3},{8,12},{10,14},{12... | collective-permute-start | bytes 122888 | tf_op jit(solution)/shard_map/ppermute | solution.py:575
  39.5 2.5 %collective-permute-start.30 = (bf16[160,128]{1,0:T(8,128)(2,1)S(1)}, bf16[160,128]{1,0:T(8,128)(2,1)S(1)}, u32[]{:S(2)}, u32[]{:S(2)}) collective-permute-start(bf16[160,128]{1,0:T(8,128)(2,1)S(1)} %get-tuple-element.90), channel_id=1, source_target_pairs={{0,6},{2,4},{4,2},{6,0},{1,7},{3,5},{5,3},{7,1},{8,14},{10,12},{12... | collective-permute-start | bytes 122888 | tf_op jit(solution)/shard_map/ppermute | solution.py:575
  42.0 0.0 collective-permute-done.26.refs_0_
  42.0 0.0 collective-permute-start.27
  42.0 1.0 %collective-permute-done.28.refs_1_ = bf16[160,128]{1,0:T(8,128)(2,1)S(1)} collective-permute-done((bf16[160,128]{1,0:T(8,128)(2,1)S(1)}, bf16[160,128]{1,0:T(8,128)(2,1)S(1)}, u32[]{:S(2)}, u32[]{:S(2)}) %collective-permute-start.28) | collective-permute-done | bytes 40992 | tf_op jit(solution)/shard_map/ppermute | solution.py:575
  42.9 0.0 collective-permute-start.29
  42.9 2.4 %collective-permute-done.30.refs_2_ = bf16[160,128]{1,0:T(8,128)(2,1)S(1)} collective-permute-done((bf16[160,128]{1,0:T(8,128)(2,1)S(1)}, bf16[160,128]{1,0:T(8,128)(2,1)S(1)}, u32[]{:S(2)}, u32[]{:S(2)}) %collective-permute-start.30) | collective-permute-done | bytes 40992 | tf_op jit(solution)/shard_map/ppermute | solution.py:575
  45.3 0.0 collective-permute-start.31
  45.3 0.0 collective-permute-done.32.near_ref
  45.3 0.5 shard_map.109
  45.8 1.8 %shard_map.108.refs_4_ = f32[5,32,512]{2,1,0:T(8,128)S(1)} custom-call(bf16[3,5,32,512]{3,2,1,0:T(8,128)(2,1)} %bitcast.16, bf16[3,512,512]{2,1,0:T(8,128)(2,1)} %stiff_hbm.7, f32[5,32,512]{2,1,0:T(8,128)S(1)} %get-tuple-element.92.lam_ref, bf16[2,512,512]{2,1,0:T(8,128)(2,1)S(1)} %get-tuple-element.71.held_ref, f32[1,32]{1,0:T(1,128)S(1)} %bitcast.11, ...), custom_call_target="tpu_custom_call" | custom-call | tf_op jit(solution)/shard_map/pallas_call | solution.py:550
  47.6 0.0 collective-permute-done.27.refs_0_
  47.6 0.0 collective-permute-done.29.refs_1_
  47.6 0.0 collective-permute-done.31.refs_2_
  47.6 2.0 %shard_map.110 = f32[5,32,512]{2,1,0:T(8,128)} custom-call(bf16[160,128]{1,0:T(8,128)(2,1)S(1)} %collective-permute-done.27.refs_0_, bf16[160,128]{1,0:T(8,128)(2,1)S(1)} %collective-permute-done.29.refs_1_, bf16[160,128]{1,0:T(8,128)(2,1)S(1)} %collective-permute-done.31.refs_2_, bf16[320,128]{1,0:T(8,128)(2,1)S(1)} %get-tuple-element.91.own_ref.refs_3_, ...), custom_call_target="tpu_custom_call" | custom-call | tf_op jit(solution)/shard_map/pallas_call | solution.py:550
  (3 shorter events, 0.0 us)
Async XLA Ops:
  0.0 17.8 %copy-start = (f32[32]{0:T(128)S(1)}, f32[32]{0:T(128)}, u32[]{:S(2)}) copy-start(f32[32]{0:T(128)} %param.16) | copy-start | bytes 388
  1.8 16.0 %collective-permute-start.12 = (bf16[336,256]{1,0:T(8,128)(2,1)S(1)}, bf16[336,256]{1,0:T(8,128)(2,1)S(1)}, u32[]{:S(2)}, u32[]{:S(2)}) collective-permute-start(bf16[336,256]{1,0:T(8,128)(2,1)S(1)} %get-tuple-element.67.own_ref), channel_id=1, source_target_pairs={{0,1},{1,0},{2,3},{3,2},{4,5},{5,4},{6,7},{7,6},{8,9},{9,8},{10,11... | collective-permute-start | bytes 516104 | tf_op jit(solution)/shard_map/ppermute | solution.py:570
  2.4 8.2 %collective-permute-start.17 = (bf16[336,128]{1,0:T(8,128)(2,1)S(1)}, bf16[336,128]{1,0:T(8,128)(2,1)S(1)}, u32[]{:S(2)}, u32[]{:S(2)}) collective-permute-start(bf16[336,128]{1,0:T(8,128)(2,1)S(1)} %get-tuple-element.66.refs_0_.refs_8_), channel_id=1, source_target_pairs={{0,6},{2,4},{4,2},{6,0},{1,7},{3,5},{5,3},{7,1},{8,14},{10,12},{12... | collective-permute-start | bytes 258056 | tf_op jit(solution)/shard_map/ppermute | solution.py:575
  7.0 7.8 %collective-permute-start.15 = (bf16[336,128]{1,0:T(8,128)(2,1)S(1)}, bf16[336,128]{1,0:T(8,128)(2,1)S(1)}, u32[]{:S(2)}, u32[]{:S(2)}) collective-permute-start(bf16[336,128]{1,0:T(8,128)(2,1)S(1)} %get-tuple-element.66.refs_0_.refs_8_), channel_id=1, source_target_pairs={{0,4},{2,6},{4,0},{6,2},{1,5},{3,7},{5,1},{7,3},{8,12},{10,14},{12... | collective-permute-start | bytes 258056 | tf_op jit(solution)/shard_map/ppermute | solution.py:575
  7.0 7.8 %collective-permute-start.13 = (bf16[336,128]{1,0:T(8,128)(2,1)S(1)}, bf16[336,128]{1,0:T(8,128)(2,1)S(1)}, u32[]{:S(2)}, u32[]{:S(2)}) collective-permute-start(bf16[336,128]{1,0:T(8,128)(2,1)S(1)} %get-tuple-element.66.refs_0_.refs_8_), channel_id=1, source_target_pairs={{0,2},{2,0},{4,6},{6,4},{1,3},{3,1},{5,7},{7,5},{8,10},{10,8},{12,... | collective-permute-start | bytes 258056 | tf_op jit(solution)/shard_map/ppermute | solution.py:575
  10.5 9.1 %collective-permute-start.18 = (bf16[336,128]{1,0:T(8,128)(2,1)S(1)}, bf16[336,128]{1,0:T(8,128)(2,1)S(1)}, u32[]{:S(2)}, u32[]{:S(2)}) collective-permute-start(bf16[336,128]{1,0:T(8,128)(2,1)S(1)} %collective-permute-done.17.refs_6_), channel_id=1, source_target_pairs={{0,1},{1,0},{2,3},{3,2},{4,5},{5,4},{6,7},{7,6},{8,9},{9,8},{10,11... | collective-permute-start | bytes 258056 | tf_op jit(solution)/shard_map/ppermute | solution.py:570
  14.9 4.8 %collective-permute-start.16 = (bf16[336,128]{1,0:T(8,128)(2,1)S(1)}, bf16[336,128]{1,0:T(8,128)(2,1)S(1)}, u32[]{:S(2)}, u32[]{:S(2)}) collective-permute-start(bf16[336,128]{1,0:T(8,128)(2,1)S(1)} %collective-permute-done.15.refs_4_), channel_id=1, source_target_pairs={{0,1},{1,0},{2,3},{3,2},{4,5},{5,4},{6,7},{7,6},{8,9},{9,8},{10,11... | collective-permute-start | bytes 258056 | tf_op jit(solution)/shard_map/ppermute | solution.py:570
  14.9 4.8 %collective-permute-start.14 = (bf16[336,128]{1,0:T(8,128)(2,1)S(1)}, bf16[336,128]{1,0:T(8,128)(2,1)S(1)}, u32[]{:S(2)}, u32[]{:S(2)}) collective-permute-start(bf16[336,128]{1,0:T(8,128)(2,1)S(1)} %collective-permute-done.13.refs_2_), channel_id=1, source_target_pairs={{0,1},{1,0},{2,3},{3,2},{4,5},{5,4},{6,7},{7,6},{8,9},{9,8},{10,11... | collective-permute-start | bytes 258056 | tf_op jit(solution)/shard_map/ppermute | solution.py:570
  22.2 10.4 %collective-permute-start.25 = (bf16[320,256]{1,0:T(8,128)(2,1)S(1)}, bf16[320,256]{1,0:T(8,128)(2,1)S(1)}, u32[]{:S(2)}, u32[]{:S(2)}) collective-permute-start(bf16[320,256]{1,0:T(8,128)(2,1)S(1)} %get-tuple-element.80.own_ref), channel_id=1, source_target_pairs={{0,1},{1,0},{2,3},{3,2},{4,5},{5,4},{6,7},{7,6},{8,9},{9,8},{10,11... | collective-permute-start | bytes 491528 | tf_op jit(solution)/shard_map/ppermute | solution.py:570
  23.6 4.5 %collective-permute-start.19 = (bf16[160,128]{1,0:T(8,128)(2,1)S(1)}, bf16[160,128]{1,0:T(8,128)(2,1)S(1)}, u32[]{:S(2)}, u32[]{:S(2)}) collective-permute-start(bf16[160,128]{1,0:T(8,128)(2,1)S(1)} %get-tuple-element.75), channel_id=1, source_target_pairs={{0,2},{2,0},{4,6},{6,4},{1,3},{3,1},{5,7},{7,5},{8,10},{10,8},{12,... | collective-permute-start | bytes 122888 | tf_op jit(solution)/shard_map/ppermute | solution.py:575
  24.4 6.2 %collective-permute-start.21 = (bf16[160,128]{1,0:T(8,128)(2,1)S(1)}, bf16[160,128]{1,0:T(8,128)(2,1)S(1)}, u32[]{:S(2)}, u32[]{:S(2)}) collective-permute-start(bf16[160,128]{1,0:T(8,128)(2,1)S(1)} %get-tuple-element.76), channel_id=1, source_target_pairs={{0,4},{2,6},{4,0},{6,2},{1,5},{3,7},{5,1},{7,3},{8,12},{10,14},{12... | collective-permute-start | bytes 122888 | tf_op jit(solution)/shard_map/ppermute | solution.py:575
  26.8 5.8 %collective-permute-start.23 = (bf16[160,128]{1,0:T(8,128)(2,1)S(1)}, bf16[160,128]{1,0:T(8,128)(2,1)S(1)}, u32[]{:S(2)}, u32[]{:S(2)}) collective-permute-start(bf16[160,128]{1,0:T(8,128)(2,1)S(1)} %get-tuple-element.77), channel_id=1, source_target_pairs={{0,6},{2,4},{4,2},{6,0},{1,7},{3,5},{5,3},{7,1},{8,14},{10,12},{12... | collective-permute-start | bytes 122888 | tf_op jit(solution)/shard_map/ppermute | solution.py:575
  28.1 6.7 %collective-permute-start.20 = (bf16[160,128]{1,0:T(8,128)(2,1)S(1)}, bf16[160,128]{1,0:T(8,128)(2,1)S(1)}, u32[]{:S(2)}, u32[]{:S(2)}) collective-permute-start(bf16[160,128]{1,0:T(8,128)(2,1)S(1)} %collective-permute-done.19.refs_0_), channel_id=1, source_target_pairs={{0,1},{1,0},{2,3},{3,2},{4,5},{5,4},{6,7},{7,6},{8,9},{9,8},{10,11... | collective-permute-start | bytes 122888 | tf_op jit(solution)/shard_map/ppermute | solution.py:570
  30.6 4.2 %collective-permute-start.22 = (bf16[160,128]{1,0:T(8,128)(2,1)S(1)}, bf16[160,128]{1,0:T(8,128)(2,1)S(1)}, u32[]{:S(2)}, u32[]{:S(2)}) collective-permute-start(bf16[160,128]{1,0:T(8,128)(2,1)S(1)} %collective-permute-done.21.refs_1_), channel_id=1, source_target_pairs={{0,1},{1,0},{2,3},{3,2},{4,5},{5,4},{6,7},{7,6},{8,9},{9,8},{10,11... | collective-permute-start | bytes 122888 | tf_op jit(solution)/shard_map/ppermute | solution.py:570
  32.6 2.3 %collective-permute-start.24 = (bf16[160,128]{1,0:T(8,128)(2,1)S(1)}, bf16[160,128]{1,0:T(8,128)(2,1)S(1)}, u32[]{:S(2)}, u32[]{:S(2)}) collective-permute-start(bf16[160,128]{1,0:T(8,128)(2,1)S(1)} %collective-permute-done.23.refs_2_), channel_id=1, source_target_pairs={{0,1},{1,0},{2,3},{3,2},{4,5},{5,4},{6,7},{7,6},{8,9},{9,8},{10,11... | collective-permute-start | bytes 122888 | tf_op jit(solution)/shard_map/ppermute | solution.py:570
  36.7 8.6 %collective-permute-start.32 = (bf16[320,256]{1,0:T(8,128)(2,1)S(1)}, bf16[320,256]{1,0:T(8,128)(2,1)S(1)}, u32[]{:S(2)}, u32[]{:S(2)}) collective-permute-start(bf16[320,256]{1,0:T(8,128)(2,1)S(1)} %get-tuple-element.93.own_ref), channel_id=1, source_target_pairs={{0,1},{1,0},{2,3},{3,2},{4,5},{5,4},{6,7},{7,6},{8,9},{9,8},{10,11... | collective-permute-start | bytes 491528 | tf_op jit(solution)/shard_map/ppermute | solution.py:570
  37.3 4.7 %collective-permute-start.26 = (bf16[160,128]{1,0:T(8,128)(2,1)S(1)}, bf16[160,128]{1,0:T(8,128)(2,1)S(1)}, u32[]{:S(2)}, u32[]{:S(2)}) collective-permute-start(bf16[160,128]{1,0:T(8,128)(2,1)S(1)} %get-tuple-element.88), channel_id=1, source_target_pairs={{0,2},{2,0},{4,6},{6,4},{1,3},{3,1},{5,7},{7,5},{8,10},{10,8},{12,... | collective-permute-start | bytes 122888 | tf_op jit(solution)/shard_map/ppermute | solution.py:575
  37.5 5.4 %collective-permute-start.28 = (bf16[160,128]{1,0:T(8,128)(2,1)S(1)}, bf16[160,128]{1,0:T(8,128)(2,1)S(1)}, u32[]{:S(2)}, u32[]{:S(2)}) collective-permute-start(bf16[160,128]{1,0:T(8,128)(2,1)S(1)} %get-tuple-element.89), channel_id=1, source_target_pairs={{0,4},{2,6},{4,0},{6,2},{1,5},{3,7},{5,1},{7,3},{8,12},{10,14},{12... | collective-permute-start | bytes 122888 | tf_op jit(solution)/shard_map/ppermute | solution.py:575
  39.5 5.8 %collective-permute-start.30 = (bf16[160,128]{1,0:T(8,128)(2,1)S(1)}, bf16[160,128]{1,0:T(8,128)(2,1)S(1)}, u32[]{:S(2)}, u32[]{:S(2)}) collective-permute-start(bf16[160,128]{1,0:T(8,128)(2,1)S(1)} %get-tuple-element.90), channel_id=1, source_target_pairs={{0,6},{2,4},{4,2},{6,0},{1,7},{3,5},{5,3},{7,1},{8,14},{10,12},{12... | collective-permute-start | bytes 122888 | tf_op jit(solution)/shard_map/ppermute | solution.py:575
  42.0 5.6 %collective-permute-start.27 = (bf16[160,128]{1,0:T(8,128)(2,1)S(1)}, bf16[160,128]{1,0:T(8,128)(2,1)S(1)}, u32[]{:S(2)}, u32[]{:S(2)}) collective-permute-start(bf16[160,128]{1,0:T(8,128)(2,1)S(1)} %collective-permute-done.26.refs_0_), channel_id=1, source_target_pairs={{0,1},{1,0},{2,3},{3,2},{4,5},{5,4},{6,7},{7,6},{8,9},{9,8},{10,11... | collective-permute-start | bytes 122888 | tf_op jit(solution)/shard_map/ppermute | solution.py:570
  42.9 4.7 %collective-permute-start.29 = (bf16[160,128]{1,0:T(8,128)(2,1)S(1)}, bf16[160,128]{1,0:T(8,128)(2,1)S(1)}, u32[]{:S(2)}, u32[]{:S(2)}) collective-permute-start(bf16[160,128]{1,0:T(8,128)(2,1)S(1)} %collective-permute-done.28.refs_1_), channel_id=1, source_target_pairs={{0,1},{1,0},{2,3},{3,2},{4,5},{5,4},{6,7},{7,6},{8,9},{9,8},{10,11... | collective-permute-start | bytes 122888 | tf_op jit(solution)/shard_map/ppermute | solution.py:570
  45.3 2.3 %collective-permute-start.31 = (bf16[160,128]{1,0:T(8,128)(2,1)S(1)}, bf16[160,128]{1,0:T(8,128)(2,1)S(1)}, u32[]{:S(2)}, u32[]{:S(2)}) collective-permute-start(bf16[160,128]{1,0:T(8,128)(2,1)S(1)} %collective-permute-done.30.refs_2_), channel_id=1, source_target_pairs={{0,1},{1,0},{2,3},{3,2},{4,5},{5,4},{6,7},{7,6},{8,9},{9,8},{10,11... | collective-permute-start | bytes 122888 | tf_op jit(solution)/shard_map/ppermute | solution.py:570

commit v7 on v6

--- a/solution.py
+++ b/solution.py
@@ -172,13 +172,13 @@
 
 
 def start_kernel(lam_hbm, send_hbm, conf_hbm, map_hbm, table_hbm, me_ref, out_ref, pair_ref, hot_ref, lam_ref, table_ref, send_ref, conf_ref, map_ref, ids_ref, sems):
-    pairs = ((send_hbm, send_ref), (conf_hbm, conf_ref), (map_hbm, map_ref), (lam_hbm, lam_ref), (table_hbm, table_ref))
+    pairs = ((lam_hbm, lam_ref), (table_hbm, table_ref), (send_hbm, send_ref), (conf_hbm, conf_ref), (map_hbm, map_ref))
     copies = fetch(pairs, sems)
     elements = lam_ref.shape[1]
     slots = send_ref.shape[1]
     faces = conf_ref.shape[2]
     ids_ref[...] = jnp.full(ids_ref.shape, -1, jnp.int32)
-    for copy in copies[:3]:
+    for copy in copies[2:]:
         copy.wait()
     ids_ref[0:1, 0:slots] = send_ref[...]
     ids_ref[0:1, slots : slots + faces] = conf_ref[0, 0:1]
@@ -203,7 +203,7 @@
     out_ref[ROWS:] = info.astype(BF16)
     pair_ref[ROWS:, :slots] = info.astype(BF16)
     pair_ref[ROWS:, slots:] = jnp.zeros((EXTRA, pair_ref.shape[1] - slots), BF16)
-    for copy in copies[3:]:
+    for copy in copies[:2]:
         copy.wait()
     lam_low = lam_ref[...].astype(BF16).reshape(5 * elements, ELEM)
     values = slot_values(lam_low, hot, table_ref[...], elements).astype(BF16)

time: 49.8 us -> 49.8 us (level)
  no operation moved by 1% of the time
where the time goes in v7:
time: 49.8 us; the launch traced here: 49.6 us
  Pallas kernels  17.5 us (35%)
  starting transfers between devices  16 us (32%)
  waiting for transfers between devices  15 us (30%)
  between operations  0.85 us (2%)
    pallas_call x13, Pallas kernels, call(): pl.pallas_call(kernel, out_shape=shapes, in_specs=[pl.BlockSpec(memory_sp...  17.5 us
    ppermute x9, waiting for transfers between devices, send_along(): return lax.ppermute(x, 'gy', [(i, i ^ k) for i in range(ny)])  14.9 us
    ppermute x9, starting transfers between devices, send_along(): return lax.ppermute(x, 'gy', [(i, i ^ k) for i in range(ny)])  14.3 us
    ppermute x12, starting transfers between devices, swap_pair(): return lax.ppermute(x, 'gz', [(0, 1), (1, 0)])  1.74 us
  transfers between devices with their start and end apart: 21, of which 6 were waited for; matrix products, arithmetic and copies ran while one was open for 0% of the time, Pallas kernels for 19%

profile of v7, /device:TPU:0, one launch (start us, length us, event | category | flops | bytes accessed | tf_op | source)
XLA Modules:
  0.0 49.6 jit_solution(16310883601590620989)
XLA Ops:
  0.0 0.0 copy-start
  0.0 1.8 %shard_map.100 = (bf16[336,128]{1,0:T(8,128)(2,1)S(1)}, bf16[336,256]{1,0:T(8,128)(2,1)S(1)}, bf16[192,256]{1,0:T(8,128)(2,1)S(1)}, f32[5,32,512]{2,1,0:T(8,128)S(1)}, bf16[512,384]{1,0:T(8,128)(2,1)S(1)}) custom-call(f32[5,32,512]{2,1,0:T(8,128)} %bitcast.17, s32[1,128]{1,0:T(1,128)} %send_hbm.1, s32[1,2,16]{2,1,0:T(2,128)} %conf_hbm.1, ...), custom_call_target="tpu_custom_call" | custom-call | tf_op jit(solution)/shard_map/pallas_call | solution.py:550
  1.8 0.6 %collective-permute-start.12 = (bf16[336,256]{1,0:T(8,128)(2,1)S(1)}, bf16[336,256]{1,0:T(8,128)(2,1)S(1)}, u32[]{:S(2)}, u32[]{:S(2)}) collective-permute-start(bf16[336,256]{1,0:T(8,128)(2,1)S(1)} %get-tuple-element.67.own_ref), channel_id=1, source_target_pairs={{0,1},{1,0},{2,3},{3,2},{4,5},{5,4},{6,7},{7,6},{8,9},{9,8},{10,11... | collective-permute-start | bytes 516104 | tf_op jit(solution)/shard_map/ppermute | solution.py:570
  2.3 4.7 %collective-permute-start.17 = (bf16[336,128]{1,0:T(8,128)(2,1)S(1)}, bf16[336,128]{1,0:T(8,128)(2,1)S(1)}, u32[]{:S(2)}, u32[]{:S(2)}) collective-permute-start(bf16[336,128]{1,0:T(8,128)(2,1)S(1)} %get-tuple-element.66.refs_0_.refs_8_), channel_id=1, source_target_pairs={{0,6},{2,4},{4,2},{6,0},{1,7},{3,5},{5,3},{7,1},{8,14},{10,12},{12... | collective-permute-start | bytes 258056 | tf_op jit(solution)/shard_map/ppermute | solution.py:575
  7.0 0.0 collective-permute-start.15
  7.0 0.6 %collective-permute-start.13 = (bf16[336,128]{1,0:T(8,128)(2,1)S(1)}, bf16[336,128]{1,0:T(8,128)(2,1)S(1)}, u32[]{:S(2)}, u32[]{:S(2)}) collective-permute-start(bf16[336,128]{1,0:T(8,128)(2,1)S(1)} %get-tuple-element.66.refs_0_.refs_8_), channel_id=1, source_target_pairs={{0,2},{2,0},{4,6},{6,4},{1,3},{3,1},{5,7},{7,5},{8,10},{10,8},{12,... | collective-permute-start | bytes 258056 | tf_op jit(solution)/shard_map/ppermute | solution.py:575
  7.6 2.8 %collective-permute-done.17.refs_6_ = bf16[336,128]{1,0:T(8,128)(2,1)S(1)} collective-permute-done((bf16[336,128]{1,0:T(8,128)(2,1)S(1)}, bf16[336,128]{1,0:T(8,128)(2,1)S(1)}, u32[]{:S(2)}, u32[]{:S(2)}) %collective-permute-start.17) | collective-permute-done | bytes 86048 | tf_op jit(solution)/shard_map/ppermute | solution.py:575
  10.5 0.0 collective-permute-start.18
  10.5 4.3 %collective-permute-done.15.refs_4_ = bf16[336,128]{1,0:T(8,128)(2,1)S(1)} collective-permute-done((bf16[336,128]{1,0:T(8,128)(2,1)S(1)}, bf16[336,128]{1,0:T(8,128)(2,1)S(1)}, u32[]{:S(2)}, u32[]{:S(2)}) %collective-permute-start.15) | collective-permute-done | bytes 86048 | tf_op jit(solution)/shard_map/ppermute | solution.py:575
  14.8 0.0 collective-permute-start.16
  14.8 0.0 collective-permute-done.13.refs_2_
  14.8 0.5 %collective-permute-start.14 = (bf16[336,128]{1,0:T(8,128)(2,1)S(1)}, bf16[336,128]{1,0:T(8,128)(2,1)S(1)}, u32[]{:S(2)}, u32[]{:S(2)}) collective-permute-start(bf16[336,128]{1,0:T(8,128)(2,1)S(1)} %collective-permute-done.13.refs_2_), channel_id=1, source_target_pairs={{0,1},{1,0},{2,3},{3,2},{4,5},{5,4},{6,7},{7,6},{8,9},{9,8},{10,11... | collective-permute-start | bytes 258056 | tf_op jit(solution)/shard_map/ppermute | solution.py:570
  15.3 2.4 %shard_map.101 = (bf16[3,320,256]{2,1,0:T(8,128)(2,1)S(1)}, bf16[2,512,512]{2,1,0:T(8,128)(2,1)S(1)}, bf16[256,128]{1,0:T(8,128)(2,1)S(1)}, bf16[256,128]{1,0:T(8,128)(2,1)S(1)}) custom-call(bf16[3,5,32,512]{3,2,1,0:T(8,128)(2,1)} %bitcast.13, bf16[3,512,512]{2,1,0:T(8,128)(2,1)} %stiff_hbm.7, bf16[256,128]{1,0:T(8,128)(2,1)} %constant.20.clone.forward_hbm, ...), custom_call_target="tpu_custom_call" | custom-call | tf_op jit(solution)/shard_map/pallas_call | solution.py:550
  17.8 0.0 collective-permute-done.12.near_ref.refs_1_
  17.8 0.0 copy-done
  17.8 1.8 %shard_map.102.refs_9_ = f32[5,32,512]{2,1,0:T(8,128)S(1)} custom-call(bf16[3,5,32,512]{3,2,1,0:T(8,128)(2,1)} %bitcast.14, bf16[3,512,512]{2,1,0:T(8,128)(2,1)} %stiff_hbm.7, f32[5,32,512]{2,1,0:T(8,128)S(1)} %get-tuple-element.68.lam_ref, bf16[2,512,512]{2,1,0:T(8,128)(2,1)S(1)} %get-tuple-element.71.held_ref, f32[1,32]{1,0:T(1,128)S(1)} %bitcast.7, ...), custom_call_target="tpu_custom_call" | custom-call | tf_op jit(solution)/shard_map/pallas_call | solution.py:550
  19.6 0.0 collective-permute-done.18.refs_7_
  19.6 0.0 collective-permute-done.16.refs_5_
  19.6 0.0 collective-permute-done.14.refs_3_
  19.6 2.5 %shard_map.103 = (s32[16,128]{1,0:T(8,128)S(1)}, bf16[192,256]{1,0:T(8,128)(2,1)S(1)}, bf16[256,128]{1,0:T(8,128)(2,1)S(1)}, f32[8,128]{1,0:T(8,128)S(1)}, f32[5...) custom-call(bf16[336,128]{1,0:T(8,128)(2,1)S(1)} %get-tuple-element., ...), custom_call_target="tpu_custom_call" | custom-call | tf_op jit(solution)/shard_map/pallas_call | solution.py:550
  22.2 0.1 collective-permute-start.25
  22.2 0.6 %shard_map.105 = s32[1]{0:T(128)} custom-call(f32[8,128]{1,0:T(8,128)S(1)} %get-tuple-element.82.excess_ref), custom_call_target="tpu_custom_call" | custom-call | tf_op jit(solution)/shard_map/pallas_call | solution.py:550
  23.5 0.8 %collective-permute-start.19 = (bf16[160,128]{1,0:T(8,128)(2,1)S(1)}, bf16[160,128]{1,0:T(8,128)(2,1)S(1)}, u32[]{:S(2)}, u32[]{:S(2)}) collective-permute-start(bf16[160,128]{1,0:T(8,128)(2,1)S(1)} %get-tuple-element.75), channel_id=1, source_target_pairs={{0,2},{2,0},{4,6},{6,4},{1,3},{3,1},{5,7},{7,5},{8,10},{10,8},{12,... | collective-permute-start | bytes 122888 | tf_op jit(solution)/shard_map/ppermute | solution.py:575
  24.4 2.3 %collective-permute-start.21 = (bf16[160,128]{1,0:T(8,128)(2,1)S(1)}, bf16[160,128]{1,0:T(8,128)(2,1)S(1)}, u32[]{:S(2)}, u32[]{:S(2)}) collective-permute-start(bf16[160,128]{1,0:T(8,128)(2,1)S(1)} %get-tuple-element.76), channel_id=1, source_target_pairs={{0,4},{2,6},{4,0},{6,2},{1,5},{3,7},{5,1},{7,3},{8,12},{10,14},{12... | collective-permute-start | bytes 122888 | tf_op jit(solution)/shard_map/ppermute | solution.py:575
  26.7 1.3 %collective-permute-start.23 = (bf16[160,128]{1,0:T(8,128)(2,1)S(1)}, bf16[160,128]{1,0:T(8,128)(2,1)S(1)}, u32[]{:S(2)}, u32[]{:S(2)}) collective-permute-start(bf16[160,128]{1,0:T(8,128)(2,1)S(1)} %get-tuple-element.77), channel_id=1, source_target_pairs={{0,6},{2,4},{4,2},{6,0},{1,7},{3,5},{5,3},{7,1},{8,14},{10,12},{12... | collective-permute-start | bytes 122888 | tf_op jit(solution)/shard_map/ppermute | solution.py:575
  28.1 0.0 collective-permute-done.19.refs_0_
  28.1 0.0 collective-permute-start.20
  28.1 2.5 %collective-permute-done.21.refs_1_ = bf16[160,128]{1,0:T(8,128)(2,1)S(1)} collective-permute-done((bf16[160,128]{1,0:T(8,128)(2,1)S(1)}, bf16[160,128]{1,0:T(8,128)(2,1)S(1)}, u32[]{:S(2)}, u32[]{:S(2)}) %collective-permute-start.21) | collective-permute-done | bytes 40992 | tf_op jit(solution)/shard_map/ppermute | solution.py:575
  30.6 0.0 collective-permute-start.22
  30.6 1.9 %collective-permute-done.23.refs_2_ = bf16[160,128]{1,0:T(8,128)(2,1)S(1)} collective-permute-done((bf16[160,128]{1,0:T(8,128)(2,1)S(1)}, bf16[160,128]{1,0:T(8,128)(2,1)S(1)}, u32[]{:S(2)}, u32[]{:S(2)}) %collective-permute-start.23) | collective-permute-done | bytes 40992 | tf_op jit(solution)/shard_map/ppermute | solution.py:575
  32.5 0.0 collective-permute-start.24
  32.5 0.0 collective-permute-done.25.near_ref
  32.5 0.5 shard_map.106
  33.0 1.8 %shard_map.104.refs_4_ = f32[5,32,512]{2,1,0:T(8,128)S(1)} custom-call(bf16[3,5,32,512]{3,2,1,0:T(8,128)(2,1)} %bitcast.15, bf16[3,512,512]{2,1,0:T(8,128)(2,1)} %stiff_hbm.7, f32[5,32,512]{2,1,0:T(8,128)S(1)} %get-tuple-element.79.lam_ref, bf16[2,512,512]{2,1,0:T(8,128)(2,1)S(1)} %get-tuple-element.71.held_ref, f32[1,32]{1,0:T(1,128)S(1)} %bitcast.9, ...), custom_call_target="tpu_custom_call" | custom-call | tf_op jit(solution)/shard_map/pallas_call | solution.py:550
  34.8 0.0 collective-permute-done.20.refs_0_
  34.8 0.0 collective-permute-done.22.refs_1_
  34.8 0.0 collective-permute-done.24.refs_2_
  34.8 1.8 %shard_map.107 = (f32[5,32,512]{2,1,0:T(8,128)S(1)}, bf16[320,128]{1,0:T(8,128)(2,1)S(1)}, bf16[320,256]{1,0:T(8,128)(2,1)S(1)}, bf16[160,128]{1,0:T(8,128)(2,1)...) custom-call(bf16[160,128]{1,0:T(8,128)(2,1)S(1)} %collective-permute-done.20.refs_0_, ...), custom_call_target="tpu_custom_call" | custom-call | tf_op jit(solution)/shard_map/pallas_call | solution.py:550
  36.7 0.6 %collective-permute-start.32 = (bf16[320,256]{1,0:T(8,128)(2,1)S(1)}, bf16[320,256]{1,0:T(8,128)(2,1)S(1)}, u32[]{:S(2)}, u32[]{:S(2)}) collective-permute-start(bf16[320,256]{1,0:T(8,128)(2,1)S(1)} %get-tuple-element.93.own_ref), channel_id=1, source_target_pairs={{0,1},{1,0},{2,3},{3,2},{4,5},{5,4},{6,7},{7,6},{8,9},{9,8},{10,11... | collective-permute-start | bytes 491528 | tf_op jit(solution)/shard_map/ppermute | solution.py:570
  37.3 0.0 collective-permute-start.26
  37.3 0.2 conditional.3
  37.5 2.0 %collective-permute-start.28 = (bf16[160,128]{1,0:T(8,128)(2,1)S(1)}, bf16[160,128]{1,0:T(8,128)(2,1)S(1)}, u32[]{:S(2)}, u32[]{:S(2)}) collective-permute-start(bf16[160,128]{1,0:T(8,128)(2,1)S(1)} %get-tuple-element.89), channel_id=1, source_target_pairs={{0,4},{2,6},{4,0},{6,2},{1,5},{3,7},{5,1},{7,3},{8,12},{10,14},{12... | collective-permute-start | bytes 122888 | tf_op jit(solution)/shard_map/ppermute | solution.py:575
  39.4 2.5 %collective-permute-start.30 = (bf16[160,128]{1,0:T(8,128)(2,1)S(1)}, bf16[160,128]{1,0:T(8,128)(2,1)S(1)}, u32[]{:S(2)}, u32[]{:S(2)}) collective-permute-start(bf16[160,128]{1,0:T(8,128)(2,1)S(1)} %get-tuple-element.90), channel_id=1, source_target_pairs={{0,6},{2,4},{4,2},{6,0},{1,7},{3,5},{5,3},{7,1},{8,14},{10,12},{12... | collective-permute-start | bytes 122888 | tf_op jit(solution)/shard_map/ppermute | solution.py:575
  41.9 0.0 collective-permute-done.26.refs_0_
  41.9 0.0 collective-permute-start.27
  41.9 1.0 %collective-permute-done.28.refs_1_ = bf16[160,128]{1,0:T(8,128)(2,1)S(1)} collective-permute-done((bf16[160,128]{1,0:T(8,128)(2,1)S(1)}, bf16[160,128]{1,0:T(8,128)(2,1)S(1)}, u32[]{:S(2)}, u32[]{:S(2)}) %collective-permute-start.28) | collective-permute-done | bytes 40992 | tf_op jit(solution)/shard_map/ppermute | solution.py:575
  42.9 0.0 collective-permute-start.29
  42.9 2.4 %collective-permute-done.30.refs_2_ = bf16[160,128]{1,0:T(8,128)(2,1)S(1)} collective-permute-done((bf16[160,128]{1,0:T(8,128)(2,1)S(1)}, bf16[160,128]{1,0:T(8,128)(2,1)S(1)}, u32[]{:S(2)}, u32[]{:S(2)}) %collective-permute-start.30) | collective-permute-done | bytes 40992 | tf_op jit(solution)/shard_map/ppermute | solution.py:575
  45.2 0.0 collective-permute-start.31
  45.3 0.0 collective-permute-done.32.near_ref
  45.3 0.5 shard_map.109
  45.7 1.8 %shard_map.108.refs_4_ = f32[5,32,512]{2,1,0:T(8,128)S(1)} custom-call(bf16[3,5,32,512]{3,2,1,0:T(8,128)(2,1)} %bitcast.16, bf16[3,512,512]{2,1,0:T(8,128)(2,1)} %stiff_hbm.7, f32[5,32,512]{2,1,0:T(8,128)S(1)} %get-tuple-element.92.lam_ref, bf16[2,512,512]{2,1,0:T(8,128)(2,1)S(1)} %get-tuple-element.71.held_ref, f32[1,32]{1,0:T(1,128)S(1)} %bitcast.11, ...), custom_call_target="tpu_custom_call" | custom-call | tf_op jit(solution)/shard_map/pallas_call | solution.py:550
  47.5 0.0 collective-permute-done.27.refs_0_
  47.6 0.0 collective-permute-done.29.refs_1_
  47.6 0.0 collective-permute-done.31.refs_2_
  47.6 2.0 %shard_map.110 = f32[5,32,512]{2,1,0:T(8,128)} custom-call(bf16[160,128]{1,0:T(8,128)(2,1)S(1)} %collective-permute-done.27.refs_0_, bf16[160,128]{1,0:T(8,128)(2,1)S(1)} %collective-permute-done.29.refs_1_, bf16[160,128]{1,0:T(8,128)(2,1)S(1)} %collective-permute-done.31.refs_2_, bf16[320,128]{1,0:T(8,128)(2,1)S(1)} %get-tuple-element.91.own_ref.refs_3_, ...), custom_call_target="tpu_custom_call" | custom-call | tf_op jit(solution)/shard_map/pallas_call | solution.py:550
  (3 shorter events, 0.0 us)
Async XLA Ops:
  0.0 17.8 %copy-start = (f32[32]{0:T(128)S(1)}, f32[32]{0:T(128)}, u32[]{:S(2)}) copy-start(f32[32]{0:T(128)} %param.16) | copy-start | bytes 388
  1.8 16.0 %collective-permute-start.12 = (bf16[336,256]{1,0:T(8,128)(2,1)S(1)}, bf16[336,256]{1,0:T(8,128)(2,1)S(1)}, u32[]{:S(2)}, u32[]{:S(2)}) collective-permute-start(bf16[336,256]{1,0:T(8,128)(2,1)S(1)} %get-tuple-element.67.own_ref), channel_id=1, source_target_pairs={{0,1},{1,0},{2,3},{3,2},{4,5},{5,4},{6,7},{7,6},{8,9},{9,8},{10,11... | collective-permute-start | bytes 516104 | tf_op jit(solution)/shard_map/ppermute | solution.py:570
  2.3 8.1 %collective-permute-start.17 = (bf16[336,128]{1,0:T(8,128)(2,1)S(1)}, bf16[336,128]{1,0:T(8,128)(2,1)S(1)}, u32[]{:S(2)}, u32[]{:S(2)}) collective-permute-start(bf16[336,128]{1,0:T(8,128)(2,1)S(1)} %get-tuple-element.66.refs_0_.refs_8_), channel_id=1, source_target_pairs={{0,6},{2,4},{4,2},{6,0},{1,7},{3,5},{5,3},{7,1},{8,14},{10,12},{12... | collective-permute-start | bytes 258056 | tf_op jit(solution)/shard_map/ppermute | solution.py:575
  7.0 7.8 %collective-permute-start.15 = (bf16[336,128]{1,0:T(8,128)(2,1)S(1)}, bf16[336,128]{1,0:T(8,128)(2,1)S(1)}, u32[]{:S(2)}, u32[]{:S(2)}) collective-permute-start(bf16[336,128]{1,0:T(8,128)(2,1)S(1)} %get-tuple-element.66.refs_0_.refs_8_), channel_id=1, source_target_pairs={{0,4},{2,6},{4,0},{6,2},{1,5},{3,7},{5,1},{7,3},{8,12},{10,14},{12... | collective-permute-start | bytes 258056 | tf_op jit(solution)/shard_map/ppermute | solution.py:575
  7.0 7.8 %collective-permute-start.13 = (bf16[336,128]{1,0:T(8,128)(2,1)S(1)}, bf16[336,128]{1,0:T(8,128)(2,1)S(1)}, u32[]{:S(2)}, u32[]{:S(2)}) collective-permute-start(bf16[336,128]{1,0:T(8,128)(2,1)S(1)} %get-tuple-element.66.refs_0_.refs_8_), channel_id=1, source_target_pairs={{0,2},{2,0},{4,6},{6,4},{1,3},{3,1},{5,7},{7,5},{8,10},{10,8},{12,... | collective-permute-start | bytes 258056 | tf_op jit(solution)/shard_map/ppermute | solution.py:575
  10.5 9.1 %collective-permute-start.18 = (bf16[336,128]{1,0:T(8,128)(2,1)S(1)}, bf16[336,128]{1,0:T(8,128)(2,1)S(1)}, u32[]{:S(2)}, u32[]{:S(2)}) collective-permute-start(bf16[336,128]{1,0:T(8,128)(2,1)S(1)} %collective-permute-done.17.refs_6_), channel_id=1, source_target_pairs={{0,1},{1,0},{2,3},{3,2},{4,5},{5,4},{6,7},{7,6},{8,9},{9,8},{10,11... | collective-permute-start | bytes 258056 | tf_op jit(solution)/shard_map/ppermute | solution.py:570
  14.8 4.8 %collective-permute-start.16 = (bf16[336,128]{1,0:T(8,128)(2,1)S(1)}, bf16[336,128]{1,0:T(8,128)(2,1)S(1)}, u32[]{:S(2)}, u32[]{:S(2)}) collective-permute-start(bf16[336,128]{1,0:T(8,128)(2,1)S(1)} %collective-permute-done.15.refs_4_), channel_id=1, source_target_pairs={{0,1},{1,0},{2,3},{3,2},{4,5},{5,4},{6,7},{7,6},{8,9},{9,8},{10,11... | collective-permute-start | bytes 258056 | tf_op jit(solution)/shard_map/ppermute | solution.py:570
  14.8 4.8 %collective-permute-start.14 = (bf16[336,128]{1,0:T(8,128)(2,1)S(1)}, bf16[336,128]{1,0:T(8,128)(2,1)S(1)}, u32[]{:S(2)}, u32[]{:S(2)}) collective-permute-start(bf16[336,128]{1,0:T(8,128)(2,1)S(1)} %collective-permute-done.13.refs_2_), channel_id=1, source_target_pairs={{0,1},{1,0},{2,3},{3,2},{4,5},{5,4},{6,7},{7,6},{8,9},{9,8},{10,11... | collective-permute-start | bytes 258056 | tf_op jit(solution)/shard_map/ppermute | solution.py:570
  22.2 10.4 %collective-permute-start.25 = (bf16[320,256]{1,0:T(8,128)(2,1)S(1)}, bf16[320,256]{1,0:T(8,128)(2,1)S(1)}, u32[]{:S(2)}, u32[]{:S(2)}) collective-permute-start(bf16[320,256]{1,0:T(8,128)(2,1)S(1)} %get-tuple-element.80.own_ref), channel_id=1, source_target_pairs={{0,1},{1,0},{2,3},{3,2},{4,5},{5,4},{6,7},{7,6},{8,9},{9,8},{10,11... | collective-permute-start | bytes 491528 | tf_op jit(solution)/shard_map/ppermute | solution.py:570
  23.5 4.5 %collective-permute-start.19 = (bf16[160,128]{1,0:T(8,128)(2,1)S(1)}, bf16[160,128]{1,0:T(8,128)(2,1)S(1)}, u32[]{:S(2)}, u32[]{:S(2)}) collective-permute-start(bf16[160,128]{1,0:T(8,128)(2,1)S(1)} %get-tuple-element.75), channel_id=1, source_target_pairs={{0,2},{2,0},{4,6},{6,4},{1,3},{3,1},{5,7},{7,5},{8,10},{10,8},{12,... | collective-permute-start | bytes 122888 | tf_op jit(solution)/shard_map/ppermute | solution.py:575
  24.4 6.2 %collective-permute-start.21 = (bf16[160,128]{1,0:T(8,128)(2,1)S(1)}, bf16[160,128]{1,0:T(8,128)(2,1)S(1)}, u32[]{:S(2)}, u32[]{:S(2)}) collective-permute-start(bf16[160,128]{1,0:T(8,128)(2,1)S(1)} %get-tuple-element.76), channel_id=1, source_target_pairs={{0,4},{2,6},{4,0},{6,2},{1,5},{3,7},{5,1},{7,3},{8,12},{10,14},{12... | collective-permute-start | bytes 122888 | tf_op jit(solution)/shard_map/ppermute | solution.py:575
  26.7 5.8 %collective-permute-start.23 = (bf16[160,128]{1,0:T(8,128)(2,1)S(1)}, bf16[160,128]{1,0:T(8,128)(2,1)S(1)}, u32[]{:S(2)}, u32[]{:S(2)}) collective-permute-start(bf16[160,128]{1,0:T(8,128)(2,1)S(1)} %get-tuple-element.77), channel_id=1, source_target_pairs={{0,6},{2,4},{4,2},{6,0},{1,7},{3,5},{5,3},{7,1},{8,14},{10,12},{12... | collective-permute-start | bytes 122888 | tf_op jit(solution)/shard_map/ppermute | solution.py:575
  28.1 6.7 %collective-permute-start.20 = (bf16[160,128]{1,0:T(8,128)(2,1)S(1)}, bf16[160,128]{1,0:T(8,128)(2,1)S(1)}, u32[]{:S(2)}, u32[]{:S(2)}) collective-permute-start(bf16[160,128]{1,0:T(8,128)(2,1)S(1)} %collective-permute-done.19.refs_0_), channel_id=1, source_target_pairs={{0,1},{1,0},{2,3},{3,2},{4,5},{5,4},{6,7},{7,6},{8,9},{9,8},{10,11... | collective-permute-start | bytes 122888 | tf_op jit(solution)/shard_map/ppermute | solution.py:570
  30.6 4.2 %collective-permute-start.22 = (bf16[160,128]{1,0:T(8,128)(2,1)S(1)}, bf16[160,128]{1,0:T(8,128)(2,1)S(1)}, u32[]{:S(2)}, u32[]{:S(2)}) collective-permute-start(bf16[160,128]{1,0:T(8,128)(2,1)S(1)} %collective-permute-done.21.refs_1_), channel_id=1, source_target_pairs={{0,1},{1,0},{2,3},{3,2},{4,5},{5,4},{6,7},{7,6},{8,9},{9,8},{10,11... | collective-permute-start | bytes 122888 | tf_op jit(solution)/shard_map/ppermute | solution.py:570
  32.5 2.3 %collective-permute-start.24 = (bf16[160,128]{1,0:T(8,128)(2,1)S(1)}, bf16[160,128]{1,0:T(8,128)(2,1)S(1)}, u32[]{:S(2)}, u32[]{:S(2)}) collective-permute-start(bf16[160,128]{1,0:T(8,128)(2,1)S(1)} %collective-permute-done.23.refs_2_), channel_id=1, source_target_pairs={{0,1},{1,0},{2,3},{3,2},{4,5},{5,4},{6,7},{7,6},{8,9},{9,8},{10,11... | collective-permute-start | bytes 122888 | tf_op jit(solution)/shard_map/ppermute | solution.py:570
  36.7 8.6 %collective-permute-start.32 = (bf16[320,256]{1,0:T(8,128)(2,1)S(1)}, bf16[320,256]{1,0:T(8,128)(2,1)S(1)}, u32[]{:S(2)}, u32[]{:S(2)}) collective-permute-start(bf16[320,256]{1,0:T(8,128)(2,1)S(1)} %get-tuple-element.93.own_ref), channel_id=1, source_target_pairs={{0,1},{1,0},{2,3},{3,2},{4,5},{5,4},{6,7},{7,6},{8,9},{9,8},{10,11... | collective-permute-start | bytes 491528 | tf_op jit(solution)/shard_map/ppermute | solution.py:570
  37.3 4.7 %collective-permute-start.26 = (bf16[160,128]{1,0:T(8,128)(2,1)S(1)}, bf16[160,128]{1,0:T(8,128)(2,1)S(1)}, u32[]{:S(2)}, u32[]{:S(2)}) collective-permute-start(bf16[160,128]{1,0:T(8,128)(2,1)S(1)} %get-tuple-element.88), channel_id=1, source_target_pairs={{0,2},{2,0},{4,6},{6,4},{1,3},{3,1},{5,7},{7,5},{8,10},{10,8},{12,... | collective-permute-start | bytes 122888 | tf_op jit(solution)/shard_map/ppermute | solution.py:575
  37.5 5.4 %collective-permute-start.28 = (bf16[160,128]{1,0:T(8,128)(2,1)S(1)}, bf16[160,128]{1,0:T(8,128)(2,1)S(1)}, u32[]{:S(2)}, u32[]{:S(2)}) collective-permute-start(bf16[160,128]{1,0:T(8,128)(2,1)S(1)} %get-tuple-element.89), channel_id=1, source_target_pairs={{0,4},{2,6},{4,0},{6,2},{1,5},{3,7},{5,1},{7,3},{8,12},{10,14},{12... | collective-permute-start | bytes 122888 | tf_op jit(solution)/shard_map/ppermute | solution.py:575
  39.4 5.8 %collective-permute-start.30 = (bf16[160,128]{1,0:T(8,128)(2,1)S(1)}, bf16[160,128]{1,0:T(8,128)(2,1)S(1)}, u32[]{:S(2)}, u32[]{:S(2)}) collective-permute-start(bf16[160,128]{1,0:T(8,128)(2,1)S(1)} %get-tuple-element.90), channel_id=1, source_target_pairs={{0,6},{2,4},{4,2},{6,0},{1,7},{3,5},{5,3},{7,1},{8,14},{10,12},{12... | collective-permute-start | bytes 122888 | tf_op jit(solution)/shard_map/ppermute | solution.py:575
  41.9 5.6 %collective-permute-start.27 = (bf16[160,128]{1,0:T(8,128)(2,1)S(1)}, bf16[160,128]{1,0:T(8,128)(2,1)S(1)}, u32[]{:S(2)}, u32[]{:S(2)}) collective-permute-start(bf16[160,128]{1,0:T(8,128)(2,1)S(1)} %collective-permute-done.26.refs_0_), channel_id=1, source_target_pairs={{0,1},{1,0},{2,3},{3,2},{4,5},{5,4},{6,7},{7,6},{8,9},{9,8},{10,11... | collective-permute-start | bytes 122888 | tf_op jit(solution)/shard_map/ppermute | solution.py:570
  42.9 4.7 %collective-permute-start.29 = (bf16[160,128]{1,0:T(8,128)(2,1)S(1)}, bf16[160,128]{1,0:T(8,128)(2,1)S(1)}, u32[]{:S(2)}, u32[]{:S(2)}) collective-permute-start(bf16[160,128]{1,0:T(8,128)(2,1)S(1)} %collective-permute-done.28.refs_1_), channel_id=1, source_target_pairs={{0,1},{1,0},{2,3},{3,2},{4,5},{5,4},{6,7},{7,6},{8,9},{9,8},{10,11... | collective-permute-start | bytes 122888 | tf_op jit(solution)/shard_map/ppermute | solution.py:570
  45.2 2.3 %collective-permute-start.31 = (bf16[160,128]{1,0:T(8,128)(2,1)S(1)}, bf16[160,128]{1,0:T(8,128)(2,1)S(1)}, u32[]{:S(2)}, u32[]{:S(2)}) collective-permute-start(bf16[160,128]{1,0:T(8,128)(2,1)S(1)} %collective-permute-done.30.refs_2_), channel_id=1, source_target_pairs={{0,1},{1,0},{2,3},{3,2},{4,5},{5,4},{6,7},{7,6},{8,9},{9,8},{10,11... | collective-permute-start | bytes 122888 | tf_op jit(solution)/shard_map/ppermute | solution.py:570
